TPU v7x, 32 devices: a whole 2x2x4 slice. The times are simulated.
32 devices in a mesh: fsdp: 2 (over x), ctx: 4 (over z), tp: 4 (over y, core).
Axes of the slice: x: 2, y: 2, z: 4, core: 2. Of those that a mesh axis runs over, the one named last changes fastest.
Arguments:
- hidden: bfloat16 [2, 4096, 768], P('fsdp', 'ctx'), may hold values from -6 to 6
- prefix: int32 [2], P('fsdp'), may hold values from 0 to 1024, as said below
- w_qkv: bfloat16 [768, 3, 768], P('fsdp', None, 'tp'), may hold values from -0.21875 to 0.21875
- b_qkv: bfloat16 [3, 12, 64], P(None, 'tp', 'fsdp'), may hold values from -3 to 3
- w_out: bfloat16 [768, 768], P('tp', 'fsdp'), may hold values from -1.75 to 1.75
- b_out: bfloat16 [768], P('fsdp'), may hold values from -2 to 2
- w_up: bfloat16 [768, 3072], P('fsdp', 'tp'), may hold values from -0.21875 to 0.21875
- b_up: bfloat16 [48, 64], P('tp', 'fsdp'), may hold values from -3 to 3
- w_down: bfloat16 [3072, 768], P('tp', 'fsdp'), may hold values from -0.109375 to 0.109375
- b_down: bfloat16 [768], P('fsdp'), may hold values from -2 to 2
- ln1_gain: bfloat16 [768], P('fsdp'), may hold values from 0.5 to 1.5
- ln1_shift: bfloat16 [768], P('fsdp'), may hold values from -2 to 2
- ln2_gain: bfloat16 [768], P('fsdp'), may hold values from 0.5 to 1.5
- ln2_shift: bfloat16 [768], P('fsdp'), may hold values from -2 to 2
- cotangent: bfloat16 [2, 4096, 768], P('fsdp', 'ctx'), may hold values from -6 to 6
Outputs:
- result: bfloat16 [2, 4096, 768], P('fsdp', 'ctx')
- grad_hidden: float32 [2, 4096, 768], P('fsdp', 'ctx')
- grad_w_qkv: float32 [768, 3, 768], P('fsdp', None, 'tp')
- grad_b_qkv: float32 [3, 12, 64], P(None, 'tp', 'fsdp')
- grad_w_out: float32 [768, 768], P('tp', 'fsdp')
- grad_b_out: float32 [768], P('fsdp')
- grad_w_up: float32 [768, 3072], P('fsdp', 'tp')
- grad_b_up: float32 [48, 64], P('tp', 'fsdp')
- grad_w_down: float32 [3072, 768], P('tp', 'fsdp')
- grad_b_down: float32 [768], P('fsdp')
- grad_ln1_gain: float32 [768], P('fsdp')
- grad_ln1_shift: float32 [768], P('fsdp')
- grad_ln2_gain: float32 [768], P('fsdp')
- grad_ln2_shift: float32 [768], P('fsdp')
Inputs may be any that keep to these rules, and one draw needn't show every extreme that they name: One sequence has a prefix of exactly 1024 positions.
All inputs are finite; a program needn't handle non-finite values.
Results may differ from a plain program's by a relative error of at most 0.012.
The roundings to bfloat16 on the way count: a program that leaves them out, or rounds other values in their place, can miss the bound.
Values may be sent and summed in bfloat16 or wider, within the bound.
No kernel may reach another device: no remote copies, remote signals or barrier semaphores. Data moves between devices by JAX's collectives and lax.ppermute only.
A program may use at most 192 MiB of HBM per device.

v0:
```python
import jax
import jax.numpy as jnp
from jax import lax
from jax.sharding import PartitionSpec as P

HD = 64
BLOCK = 16
SEQ_LEN = 2048


epsilon = 1e-05


def norm_rows(values, gain_value, shift_value):
    row_mean = jnp.mean(values, axis=-1, keepdims=True)
    centered = values - row_mean
    variance = jnp.mean(centered * centered, axis=-1, keepdims=True)
    return centered * lax.rsqrt(variance + epsilon) * gain_value + shift_value


def exact_gelu(values):
    return jax.nn.gelu(values, approximate=False)


def rotate(values, cosine, sine_value):
    half_width = values.shape[-1] // 2
    first_half = values[..., :half_width]
    second = values[..., half_width:]
    return jnp.concatenate(
        [first_half * cosine - second * sine_value, second * cosine + first_half * sine_value],
        axis=-1,
    )


def rotate_back(grads, cosine, sine_value):
    half_width = grads.shape[-1] // 2
    first_half = grads[..., :half_width]
    second = grads[..., half_width:]
    return jnp.concatenate(
        [first_half * cosine + second * sine_value, second * cosine - first_half * sine_value],
        axis=-1,
    )


def angles(positions):
    half_width = HD // 2
    frequency = jnp.power(
        jnp.float32(10000.0), -2.0 * jnp.arange(half_width, dtype=jnp.float32) / HD
    )
    angle_rows = positions.astype(jnp.float32)[:, None] * frequency[None, :]
    return (jnp.cos(angle_rows)[:, None, :], jnp.sin(angle_rows)[:, None, :])


def visible(query_rows, key_rows, prefix_len):
    q_noisy = query_rows < SEQ_LEN
    k_noisy = key_rows < SEQ_LEN
    q_place = jnp.where(q_noisy, query_rows, query_rows - SEQ_LEN)
    k_place = jnp.where(k_noisy, key_rows, key_rows - SEQ_LEN)
    q_block = (q_place // BLOCK)[:, None]
    k_block = (k_place // BLOCK)[None, :]
    q_flag = q_noisy[:, None]
    k_flag = k_noisy[None, :]
    same_block = q_flag & k_flag & (q_block == k_block)
    earlier = q_flag & ~k_flag & (k_block < q_block)
    causal = ~q_flag & ~k_flag & (k_block <= q_block)
    opened = ~k_flag & (k_place[None, :] < prefix_len)
    return same_block | earlier | causal | opened


def body(
    hidden,
    prefix,
    w_qkv,
    b_qkv,
    w_out,
    b_out,
    w_up,
    b_up,
    w_down,
    b_down,
    ln1_gain,
    ln1_shift,
    ln2_gain,
    ln2_shift,
    cotangent,
):
    gathered = (
        lax.all_gather(w_qkv, "fsdp", axis=0, tiled=True),
        lax.all_gather(b_qkv, "fsdp", axis=2, tiled=True),
        lax.all_gather(w_out, "fsdp", axis=1, tiled=True),
        lax.all_gather(b_out, "fsdp", axis=0, tiled=True),
        lax.all_gather(w_up, "fsdp", axis=0, tiled=True),
        lax.all_gather(b_up, "fsdp", axis=1, tiled=True),
        lax.all_gather(w_down, "fsdp", axis=1, tiled=True),
        lax.all_gather(b_down, "fsdp", axis=0, tiled=True),
        lax.all_gather(ln1_gain, "fsdp", axis=0, tiled=True),
        lax.all_gather(ln1_shift, "fsdp", axis=0, tiled=True),
        lax.all_gather(ln2_gain, "fsdp", axis=0, tiled=True),
        lax.all_gather(ln2_shift, "fsdp", axis=0, tiled=True),
    )
    (
        full_qkv,
        full_bqkv,
        full_out,
        full_bout,
        full_up,
        full_bup,
        full_down,
        full_bdown,
        gain_one,
        shift_one,
        gain_two,
        shift_two,
    ) = gathered
    bias_qkv = full_bqkv.astype(jnp.float32)
    bias_out = full_bout.astype(jnp.float32)
    bias_up = full_bup.astype(jnp.float32)
    bias_down = full_bdown.astype(jnp.float32)
    gain_one = gain_one.astype(jnp.float32)
    shift_one = shift_one.astype(jnp.float32)
    gain_two = gain_two.astype(jnp.float32)
    shift_two = shift_two.astype(jnp.float32)
    row_count = hidden.shape[1]
    local_width = full_qkv.shape[2]
    local_heads = local_width // HD
    total_rows = 2 * SEQ_LEN
    row_ids = lax.axis_index("ctx") * row_count + jnp.arange(row_count, dtype=jnp.int32)
    positions = jnp.where(row_ids < SEQ_LEN, row_ids, row_ids - SEQ_LEN)
    cosine, sine_value = angles(positions)
    key_ids = jnp.arange(total_rows, dtype=jnp.int32)
    prefix_len = prefix[0]
    score_scale = HD ** (-0.5)
    values = hidden[0].astype(jnp.float32)
    upstream = cotangent[0].astype(jnp.float32)
    normed, norm_one_pull = jax.vjp(norm_rows, values, gain_one, shift_one)
    normed_low = normed.astype(jnp.bfloat16)
    projected = jnp.einsum(
        "nd,dcj->ncj", normed_low, full_qkv, preferred_element_type=jnp.float32
    ) + bias_qkv.reshape(3, local_width)
    queries = rotate(
        projected[:, 0].reshape(row_count, local_heads, HD), cosine, sine_value
    ).astype(jnp.bfloat16)
    keys_local = (
        rotate(projected[:, 1].reshape(row_count, local_heads, HD), cosine, sine_value)
        .astype(jnp.bfloat16)
        .reshape(row_count, local_width)
    )
    values_local = projected[:, 2].astype(jnp.bfloat16)
    keys_all, values_all = (
        lax.all_gather(keys_local, "ctx", axis=0, tiled=True),
        lax.all_gather(values_local, "ctx", axis=0, tiled=True),
    )
    key_heads = keys_all.reshape(total_rows, local_heads, HD)
    value_heads = values_all.reshape(total_rows, local_heads, HD)
    block_span = min(512, row_count)
    block_count = row_count // block_span

    def scores_of(row_start):
        query_block = queries[row_start : row_start + block_span]
        scores = (
            jnp.einsum("qhe,khe->hqk", query_block, key_heads, preferred_element_type=jnp.float32)
            * score_scale
        )
        allowed = visible(row_ids[row_start : row_start + block_span], key_ids, prefix_len)
        return jnp.where(allowed[None], scores, -1e30)

    outputs = []
    log_sums = []
    for block_index in range(block_count):
        scores = scores_of(block_index * block_span)
        row_top = jnp.max(scores, axis=-1, keepdims=True)
        weights = jnp.exp(scores - row_top)
        total_sum = jnp.sum(weights, axis=-1, keepdims=True)
        probs = weights / total_sum
        log_sums.append(row_top + jnp.log(total_sum))
        outputs.append(
            jnp.einsum(
                "hqk,khe->qhe",
                probs.astype(jnp.bfloat16),
                value_heads,
                preferred_element_type=jnp.float32,
            )
        )
    attended = jnp.concatenate(outputs, axis=0).reshape(row_count, local_width).astype(jnp.bfloat16)
    branch_part = jnp.dot(attended, full_out, preferred_element_type=jnp.float32)
    middle = values + lax.psum(branch_part, "tp") + bias_out
    normed_two, norm_two_pull = jax.vjp(norm_rows, middle, gain_two, shift_two)
    normed_two_low = normed_two.astype(jnp.bfloat16)
    pre_act = jnp.dot(
        normed_two_low, full_up, preferred_element_type=jnp.float32
    ) + bias_up.reshape(-1)
    activated, gelu_pull = jax.vjp(exact_gelu, pre_act)
    activated_low = activated.astype(jnp.bfloat16)
    mlp_part = jnp.dot(activated_low, full_down, preferred_element_type=jnp.float32)
    result_low = (
        middle + lax.psum(mlp_part.astype(jnp.bfloat16), "tp").astype(jnp.float32) + bias_down
    ).astype(jnp.bfloat16)
    grad_out_low = upstream.astype(jnp.bfloat16)
    g_bdown = jnp.sum(grad_out_low.astype(jnp.float32), axis=0)
    g_down = jnp.dot(activated_low.T, grad_out_low, preferred_element_type=jnp.float32)
    grad_act = jnp.dot(grad_out_low, full_down.T, preferred_element_type=jnp.float32)
    grad_pre = gelu_pull(grad_act)[0].astype(jnp.bfloat16)
    g_bup = jnp.sum(grad_pre.astype(jnp.float32), axis=0).reshape(full_bup.shape)
    g_up = jnp.dot(normed_two_low.T, grad_pre, preferred_element_type=jnp.float32)
    grad_two_part = jnp.dot(grad_pre, full_up.T, preferred_element_type=jnp.float32)
    grad_normed_two = lax.psum(grad_two_part, "tp")
    grad_middle, g_gain_two, g_shift_two = norm_two_pull(grad_normed_two)
    grad_middle = upstream + grad_middle
    grad_branch = grad_middle.astype(jnp.bfloat16)
    g_bout = jnp.sum(grad_branch.astype(jnp.float32), axis=0)
    g_out = jnp.dot(attended.T, grad_branch, preferred_element_type=jnp.float32)
    grad_att = (
        jnp.dot(grad_branch, full_out.T, preferred_element_type=jnp.float32)
        .astype(jnp.bfloat16)
        .reshape(row_count, local_heads, HD)
    )
    grad_query_parts = []
    grad_keys = jnp.zeros((total_rows, local_heads, HD), jnp.float32)
    grad_values = jnp.zeros((total_rows, local_heads, HD), jnp.float32)
    for block_index in range(block_count):
        row_start = block_index * block_span
        scores = scores_of(row_start)
        probs = jnp.exp(scores - log_sums[block_index])
        grad_block = grad_att[row_start : row_start + block_span]
        grad_probs = jnp.einsum(
            "qhe,khe->hqk", grad_block, value_heads, preferred_element_type=jnp.float32
        )
        inner_sum = jnp.sum(probs * grad_probs, axis=-1, keepdims=True)
        grad_scores = (probs * (grad_probs - inner_sum)).astype(jnp.bfloat16)
        grad_query_parts.append(
            jnp.einsum("hqk,khe->qhe", grad_scores, key_heads, preferred_element_type=jnp.float32)
            * score_scale
        )
        grad_keys = (
            grad_keys
            + jnp.einsum(
                "hqk,qhe->khe",
                grad_scores,
                queries[row_start : row_start + block_span],
                preferred_element_type=jnp.float32,
            )
            * score_scale
        )
        grad_values = grad_values + jnp.einsum(
            "hqk,qhe->khe",
            probs.astype(jnp.bfloat16),
            grad_block,
            preferred_element_type=jnp.float32,
        )
    key_grad, value_grad = (
        lax.psum_scatter(
            grad_keys.reshape(total_rows, local_width), "ctx", scatter_dimension=0, tiled=True
        ),
        lax.psum_scatter(
            grad_values.reshape(total_rows, local_width), "ctx", scatter_dimension=0, tiled=True
        ),
    )
    grad_query = rotate_back(jnp.concatenate(grad_query_parts, axis=0), cosine, sine_value).reshape(
        row_count, local_width
    )
    grad_key = rotate_back(
        key_grad.reshape(row_count, local_heads, HD), cosine, sine_value
    ).reshape(row_count, local_width)
    grad_proj = jnp.stack([grad_query, grad_key, value_grad], axis=1).astype(jnp.bfloat16)
    g_bqkv = jnp.sum(grad_proj.astype(jnp.float32), axis=0).reshape(full_bqkv.shape)
    g_qkv = jnp.einsum("nd,ncj->dcj", normed_low, grad_proj, preferred_element_type=jnp.float32)
    grad_one_part = jnp.einsum(
        "ncj,dcj->nd", grad_proj, full_qkv, preferred_element_type=jnp.float32
    )
    grad_normed = lax.psum(grad_one_part, "tp")
    grad_input, g_gain_one, g_shift_one = norm_one_pull(grad_normed)
    grad_input = grad_middle + grad_input
    summed = lax.psum(
        (
            g_qkv,
            g_bqkv,
            g_out,
            g_bout,
            g_up,
            g_bup,
            g_down,
            g_bdown,
            g_gain_one,
            g_shift_one,
            g_gain_two,
            g_shift_two,
        ),
        "ctx",
    )
    owned = (
        lax.psum_scatter(summed[0], "fsdp", scatter_dimension=0, tiled=True),
        lax.psum_scatter(summed[1], "fsdp", scatter_dimension=2, tiled=True),
        lax.psum_scatter(summed[2], "fsdp", scatter_dimension=1, tiled=True),
        lax.psum_scatter(summed[3], "fsdp", scatter_dimension=0, tiled=True),
        lax.psum_scatter(summed[4], "fsdp", scatter_dimension=0, tiled=True),
        lax.psum_scatter(summed[5], "fsdp", scatter_dimension=1, tiled=True),
        lax.psum_scatter(summed[6], "fsdp", scatter_dimension=1, tiled=True),
        lax.psum_scatter(summed[7], "fsdp", scatter_dimension=0, tiled=True),
        lax.psum_scatter(summed[8], "fsdp", scatter_dimension=0, tiled=True),
        lax.psum_scatter(summed[9], "fsdp", scatter_dimension=0, tiled=True),
        lax.psum_scatter(summed[10], "fsdp", scatter_dimension=0, tiled=True),
        lax.psum_scatter(summed[11], "fsdp", scatter_dimension=0, tiled=True),
    )
    return (
        result_low[None],
        grad_input[None],
        owned[0],
        owned[1],
        owned[2],
        owned[3],
        owned[4],
        owned[5],
        owned[6],
        owned[7],
        owned[8],
        owned[9],
        owned[10],
        owned[11],
    )


def solution(mesh):
    in_specs = (
        P("fsdp", "ctx", None),
        P("fsdp"),
        P("fsdp", None, "tp"),
        P(None, "tp", "fsdp"),
        P("tp", "fsdp"),
        P("fsdp"),
        P("fsdp", "tp"),
        P("tp", "fsdp"),
        P("tp", "fsdp"),
        P("fsdp"),
        P("fsdp"),
        P("fsdp"),
        P("fsdp"),
        P("fsdp"),
        P("fsdp", "ctx", None),
    )
    out_specs = (
        P("fsdp", "ctx", None),
        P("fsdp", "ctx", None),
        P("fsdp", None, "tp"),
        P(None, "tp", "fsdp"),
        P("tp", "fsdp"),
        P("fsdp"),
        P("fsdp", "tp"),
        P("tp", "fsdp"),
        P("tp", "fsdp"),
        P("fsdp"),
        P("fsdp"),
        P("fsdp"),
        P("fsdp"),
        P("fsdp"),
    )
    return jax.shard_map(body, mesh=mesh, in_specs=in_specs, out_specs=out_specs, check_vma=False)
```

profile of v0, /device:TPU:25, one launch (start us, length us, event | category | flops | bytes accessed | tf_op | source)
XLA Modules:
  0.0 941.3 jit_solution(2657644902904457582)
XLA Ops:
  8.9 3.2 all-gather.1
  12.8 3.2 all-gather.2
  17.8 2.0 fusion.27
  20.5 3.4 all_gather.45
  24.1 8.4 all_gather.44
  36.6 1.9 slice.139
  39.3 4.9 all_gather.48
  44.2 11.1 %or_or_fusion.1 = (pred[512,4096]{1,0:T(8,128)(4,1)}, pred[512,4096]{1,0:T(8,128)(4,1)}) fusion(s32[4096]{0:T(1024)S(1)} %add_select_fusion, s32[512]{0:T(512)S(1)} %get-tuple-element.76, pred[4096]{0:T(1024)(128)(4,1)S(1)} %fusion.57, pred[4096]{0:T(1024)(128)(4,1)S(1)} %get-tuple-element.94, pred[4096]{0:T(1024)(128)(4,1)S(1)} %get-tuple-element.93, ...), kind=kLoop, calls=%fused_computation.23 | loop fusion | flops 50331648 | bytes 4229120 | tf_op jit(solution)/shard_map/or | solution.py:67
  55.3 21.5 %all-gather.13.cloned.1.call-done = bf16[4096,192]{0,1:T(8,128)(2,1)} async-done(((bf16[1024,192]{0,1:T(8,128)(2,1)}), bf16[4096,192]{0,1:T(8,128)(2,1)}) %all-gather.13.cloned.1.call-update) | async-done | bytes 1572880 | tf_op jit(solution)/shard_map/all_gather | solution.py:150
  76.8 13.2 %fusion.86 = (f32[3,512]{1,0:T(4,128)S(1)}, f32[3,512,4096]{2,1,0:T(8,128)}) fusion(bf16[4096,3,64]{0,2,1:T(8,128)(2,1)} %bitcast.138, bf16[1024,3,32]{0,2,1:T(8,128)(2,1)S(1)} %get-tuple-element.62, bf16[1024,3,32]{0,2,1:T(8,128)(2,1)S(1)} %get-tuple-element.63, pred[512,4096]{1,0:T(8,128)(4,1)} %get-tuple-element.72), kind=kOutput, calls=%fused_computation.183 | convolution fusion | flops 824572416 | bytes 29235200 | tf_op jit(solution)/shard_map/qhe,khe->hqk/dot_general | solution.py:161
  90.1 11.1 %fusion.85 = (f32[3,512]{1,0:T(4,128)S(1)}, f32[3,512,4096]{2,1,0:T(8,128)}) fusion(bf16[4096,3,64]{0,2,1:T(8,128)(2,1)S(1)} %bitcast.139, bf16[1024,3,32]{0,2,1:T(8,128)(2,1)S(1)} %get-tuple-element.63, bf16[1024,3,32]{0,2,1:T(8,128)(2,1)S(1)} %get-tuple-element.62, pred[512,4096]{1,0:T(8,128)(4,1)S(1)} %copy-done.22), kind=kOutput, calls=%fused_computation.182 | convolution fusion | flops 824572416 | bytes 29235200 | tf_op jit(solution)/shard_map/qhe,khe->hqk/dot_general | solution.py:161
  101.2 10.5 %fusion = f32[3,512]{1,0:T(4,128)S(1)} fusion(f32[3,512,4096]{2,1,0:T(8,128)} %get-tuple-element.83, f32[3,512]{1,0:T(4,128)S(1)} %get-tuple-element.82), kind=kLoop, calls=%fused_computation.12 | loop fusion | flops 12581376 | bytes 25178112 | tf_op jit(solution)/shard_map/reduce_sum | solution.py:173
  111.7 3.2 all-gather.19.cloned.1.call-done
  114.9 11.0 %fusion.48 = bf16[512,3,64]{0,2,1:T(8,128)(2,1)S(1)} fusion(bf16[4096,3,64]{0,2,1:T(8,128)(2,1)} %bitcast.142, f32[3,512,4096]{2,1,0:T(8,128)} %get-tuple-element.83, f32[3,512]{1,0:T(4,128)S(1)} %fusion, f32[3,512]{1,0:T(4,128)S(1)} %get-tuple-element.82), kind=kOutput, calls=%fused_computation.90 | convolution fusion | flops 824279040 | bytes 26947584 | tf_op jit(solution)/shard_map/hqk,khe->qhe/dot_general | solution.py:177
  125.9 10.6 %fusion.1 = f32[3,512]{1,0:T(4,128)S(1)} fusion(f32[3,512,4096]{2,1,0:T(8,128)} %get-tuple-element.81, f32[3,512]{1,0:T(4,128)S(1)} %get-tuple-element.80), kind=kLoop, calls=%fused_computation.13 | loop fusion | flops 12581376 | bytes 25178112 | tf_op jit(solution)/shard_map/reduce_sum | solution.py:173
  136.5 11.0 %fusion.49 = bf16[512,3,64]{0,2,1:T(8,128)(2,1)S(1)} fusion(bf16[4096,3,64]{0,2,1:T(8,128)(2,1)S(1)} %bitcast.144, f32[3,512,4096]{2,1,0:T(8,128)} %get-tuple-element.81, f32[3,512]{1,0:T(4,128)S(1)} %fusion.1, f32[3,512]{1,0:T(4,128)S(1)} %get-tuple-element.80), kind=kOutput, calls=%fused_computation.91 | convolution fusion | flops 824279040 | bytes 26947584 | tf_op jit(solution)/shard_map/hqk,khe->qhe/dot_general | solution.py:177
  148.3 2.3 fusion.88
  151.8 3.2 all-gather.3
  155.1 3.2 all-gather.4
  158.3 3.5 all-gather.5
  161.9 3.6 all-gather.6
  165.7 54.2 %all-reduce.15.cloned.1.call-done = f32[1024,768]{1,0:T(8,128)} async-done(((f32[1024,768]{1,0:T(8,128)}), f32[1024,768]{1,0:T(8,128)}) %all-reduce.15.cloned.1.call-update) | async-done | bytes 3145744 | tf_op jit(solution)/shard_map/psum | solution.py:186
  219.9 2.4 fusion.79
  224.5 11.9 %multiply_convert_fusion.2 = (bf16[1024,768]{1,0:T(8,128)(2,1)}, f32[1024,768]{1,0:T(8,128)}, f32[1024,768]{1,0:T(8,128)}) fusion(f32[768]{0:T(1024)S(1)} %reshape.596, bf16[768,768]{1,0:T(8,128)(2,1)} %all-gather.15.cloned.1.call-done, f32[1024,768]{1,0:T(8,128)} %copy-done.4, f32[768]{0:T(1024)S(1)} %reshape.617, f32[768]{0:T(1024)S(1)} %reshape.616, ...), kind=kOutput, calls=%fused_computation.56 | convolution fusion | flops 1263796224 | bytes 12207104 | tf_op jit(solution)/shard_map/dot_general | solution.py:189
  236.4 6.1 convert_reduce_fusion.2
  243.6 3.1 fusion.89
  247.4 3.4 all-gather.7
  250.8 4.4 convolution_convert_fusion
  255.3 60.1 %all-reduce.19.cloned.1.call-done = f32[1024,768]{1,0:T(8,128)} async-done(((f32[1024,768]{1,0:T(8,128)}), f32[1024,768]{1,0:T(8,128)}) %all-reduce.19.cloned.1.call-update) | async-done | bytes 3145744 | tf_op jit(solution)/shard_map/psum | solution.py:206
  315.4 3.4 multiply_reduce_fusion.2
  318.8 42.5 %all-reduce.17.cloned.1.call-done = bf16[1024,768]{1,0:T(8,128)(2,1)} async-done(((bf16[1024,768]{1,0:T(8,128)(2,1)}), bf16[1024,768]{1,0:T(8,128)(2,1)}) %all-reduce.17.cloned.1.call-update) | async-done | bytes 1572880 | tf_op jit(solution)/shard_map/psum | solution.py:196
  361.4 4.2 fusion.77
  369.1 19.3 %multiply_reduce_fusion.1 = (f32[3,512]{1,0:T(4,128)S(1)}, f32[3,512,4096]{2,1,0:T(8,128)}) fusion(f32[3,512,4096]{2,1,0:T(8,128)} %get-tuple-element.83, f32[3,512]{1,0:T(4,128)S(1)} %log_add_fusion.1, bf16[512,3,64]{0,2,1:T(8,128)(2,1)S(1)} %bitcast.151, bf16[4096,3,64]{0,2,1:T(8,128)(2,1)S(1)} %bitcast.145), kind=kOutput, calls=%fused_computation.4 | convolution fusion | flops 824179200 | bytes 52113408 | tf_op jit(solution)/shard_map/qhe,khe->hqk/dot_general | solution.py:225
  388.3 17.0 %multiply_convert_fusion.1 = bf16[3,512,4096]{2,1,0:T(8,128)(2,1)S(1)} fusion(f32[3,512,4096]{2,1,0:T(8,128)} %get-tuple-element.88, f32[3,512,4096]{2,1,0:T(8,128)} %get-tuple-element.83, f32[3,512]{1,0:T(4,128)S(1)} %get-tuple-element.87, f32[3,512]{1,0:T(4,128)S(1)} %log_add_fusion.1), kind=kLoop, calls=%fused_computation.3 | loop fusion | flops 25165824 | bytes 62926848 | tf_op jit(solution)/shard_map/convert_element_type | solution.py:229
  405.4 2.3 fusion.67
  407.7 2.2 copy-done
  409.9 16.8 %multiply_reduce_fusion = (f32[3,512]{1,0:T(4,128)}, f32[3,512,4096]{2,1,0:T(8,128)}) fusion(f32[3,512,4096]{2,1,0:T(8,128)} %get-tuple-element.81, f32[3,512]{1,0:T(4,128)S(1)} %log_add_fusion, bf16[512,3,64]{0,2,1:T(8,128)(2,1)S(1)} %bitcast.153, bf16[4096,3,64]{0,2,1:T(8,128)(2,1)} %bitcast.143), kind=kOutput, calls=%fused_computation.1 | convolution fusion | flops 824179200 | bytes 52113408 | tf_op jit(solution)/shard_map/qhe,khe->hqk/dot_general | solution.py:225
  426.7 17.3 %multiply_convert_fusion = bf16[3,512,4096]{2,1,0:T(8,128)(2,1)S(1)} fusion(f32[3,512,4096]{2,1,0:T(8,128)} %get-tuple-element.86, f32[3,512,4096]{2,1,0:T(8,128)} %get-tuple-element.81, f32[3,512]{1,0:T(4,128)} %get-tuple-element.85, f32[3,512]{1,0:T(4,128)S(1)} %log_add_fusion), kind=kLoop, calls=%fused_computation | loop fusion | flops 25165824 | bytes 62926848 | tf_op jit(solution)/shard_map/convert_element_type | solution.py:229
  444.1 4.6 fusion.12
  449.6 10.9 %fusion.4 = f32[3,64,4096]{2,1,0:T(8,128)S(1)} fusion(bf16[512,3,64]{0,2,1:T(8,128)(2,1)S(1)} %bitcast.154, f32[3,512,4096]{2,1,0:T(8,128)} %get-tuple-element.81, f32[3,512]{1,0:T(4,128)S(1)} %log_add_fusion), kind=kOutput, calls=%fused_computation.16 | convolution fusion | flops 817889280 | bytes 28514304 | tf_op jit(solution)/shard_map/hqk,qhe->khe/dot_general | solution.py:244
  460.5 12.5 %fusion.13 = f32[3,64,4096]{2,1,0:T(8,128)} fusion(f32[3,64,4096]{2,1,0:T(8,128)S(1)} %fusion.4, bf16[512,3,64]{0,2,1:T(8,128)(2,1)S(1)} %bitcast.152, f32[3,512,4096]{2,1,0:T(8,128)} %get-tuple-element.83, f32[3,512]{1,0:T(4,128)S(1)} %log_add_fusion.1), kind=kOutput, calls=%fused_computation.26 | convolution fusion | flops 818675712 | bytes 31660032 | tf_op jit(solution)/shard_map/hqk,qhe->khe/dot_general | solution.py:244
  475.9 4.9 fusion.38
  480.9 4.6 fusion.87
  487.0 8.6 fusion.45
  495.5 8.6 fusion.44
  504.1 4.9 reduce-scatter.13.cloned.1.call-done
  510.5 61.2 %reduce-scatter.15.cloned.1.call-done = f32[1024,192]{0,1:T(8,128)} async-done(((f32[4096,192]{0,1:T(8,128)}), f32[1024,192]{0,1:T(8,128)}) %reduce-scatter.15.cloned.1.call-update) | async-done | bytes 786448 | tf_op jit(solution)/shard_map/reduce_scatter | solution.py:254
  573.2 3.3 fusion.70
  578.5 4.3 convolution_bitcast_fusion
  583.1 7.8 reduce-scatter.19.cloned.1.call-done
  590.9 37.1 %reduce-scatter.23.cloned.1.call-done = f32[768,384]{1,0:T(8,128)} async-done(((f32[768,768]{1,0:T(8,128)}), f32[768,384]{1,0:T(8,128)}) %reduce-scatter.23.cloned.1.call-update) | async-done | bytes 1179664 | tf_op jit(solution)/shard_map/reduce_scatter | solution.py:297
  628.0 36.9 %reduce-scatter.21.cloned.1.call-done = f32[384,768]{1,0:T(8,128)} async-done(((f32[768,768]{1,0:T(8,128)}), f32[384,768]{1,0:T(8,128)}) %reduce-scatter.21.cloned.1.call-update) | async-done | bytes 1179664 | tf_op jit(solution)/shard_map/reduce_scatter | solution.py:295
  664.9 30.6 %reduce-scatter.17.cloned.1.call-done = f32[384,3,192]{0,2,1:T(8,128)} async-done(((f32[768,3,192]{0,2,1:T(8,128)}), f32[384,3,192]{0,2,1:T(8,128)}) %reduce-scatter.17.cloned.1.call-update) | async-done | bytes 884752 | tf_op jit(solution)/shard_map/reduce_scatter | solution.py:291
  696.8 11.0 %reduce-scatter.27.cloned.1.call-done = f32[32,12]{1,0:T(8,128)} async-done(((f32[64,12]{1,0:T(8,128)}), f32[32,12]{1,0:T(8,128)}) %reduce-scatter.27.cloned.1.call-update) | async-done | bytes 1552
  708.5 12.0 %reduce-scatter.25.cloned.1.call-done = f32[32,9]{1,0:T(8,128)} async-done(((f32[64,9]{1,0:T(8,128)}), f32[32,9]{1,0:T(8,128)}) %reduce-scatter.25.cloned.1.call-update) | async-done | bytes 1168
  721.4 70.6 %all-reduce.21.cloned.1.call-done = f32[1024,768]{1,0:T(8,128)} async-done(((f32[1024,768]{1,0:T(8,128)}), f32[1024,768]{1,0:T(8,128)}) %all-reduce.21.cloned.1.call-update) | async-done | bytes 3145744 | tf_op jit(solution)/shard_map/psum | solution.py:270
  792.0 2.9 fusion.75
  795.0 1.7 fusion.26
  797.3 2.8 convert_reduce_fusion
  800.1 7.0 all-reduce.8
  807.6 15.4 %all-reduce.6 = (f32[3,3,32]{2,1,0:T(4,128)}, f32[384]{0:T(512)}, f32[12,32]{1,0:T(8,128)}, f32[384]{0:T(512)}, f32[384]{0:T(512)}, /*index=5*/f32[384]{0:T(512)}, f32[384]{0:T(512)}, f32[384]{0:T(512)}) all-reduce(f32[3,3,32]{2,1,0:T(4,128)S(1)} %copy.39, ...), channel_id=1, replica_groups=mesh['fsdp'=2,'ctx'=4,'tp'=4] {'ctx'}, use_global_device_ids=true, to_apply=%region_23.24 | all-reduce | flops 2976 | bytes 23808 | tf_op jit(solution)/shard_map/psum | solution.py:273
  823.1 104.6 %all-reduce.23.cloned.1.call-done = (f32[384,3,192]{0,2,1:T(8,128)}, f32[192,384]{1,0:T(8,128)}, f32[384,768]{1,0:T(8,128)}, f32[768,384]{1,0:T(8,128)}) async-done(((f32[384,3,192]{0,2,1:T(8,128)}, f32[192,384]{1,0:T(8,128)}, f32[384,768]{1,0:T(8,128)}, f32[768,384]{1,0:T(8,128)}), (f32[384,3,192]{0,2,1:T(8,128)}, f32[192,384]{1,0:T(8,128)}, f32[384,768]{1,0:T(8,128)}, ...) | async-done | bytes 3538960 | tf_op jit(solution)/shard_map/psum | solution.py:273
  927.7 2.3 copy.51
  930.0 1.7 copy.52
  (251 shorter events, 33.7 us)
Async XLA Ops:
  8.0 24.6 %copy-start.2 = (bf16[1,1024,768]{2,1,0:T(8,128)(2,1)S(1)}, bf16[1,1024,768]{2,1,0:T(8,128)(2,1)}, u32[]{:S(2)}) copy-start(bf16[1,1024,768]{2,1,0:T(8,128)(2,1)} %param.15) | copy-start | bytes 4718596
  8.0 12.4 %copy-start.62 = (bf16[3,3,32]{2,1,0:T(4,128)(2,1)S(1)}, bf16[3,3,32]{2,1,0:T(4,128)(2,1)}, u32[]{:S(2)}) copy-start(bf16[3,3,32]{2,1,0:T(4,128)(2,1)} %param.18) | copy-start | bytes 1732
  8.0 16.1 %copy-start.36 = (bf16[384,3,192]{0,2,1:T(8,128)(2,1)S(1)}, bf16[384,3,192]{0,2,1:T(8,128)(2,1)}, u32[]{:S(2)}) copy-start(bf16[384,3,192]{0,2,1:T(8,128)(2,1)} %param.17) | copy-start | bytes 1327108
  8.0 68.8 %all-gather.13.cloned.1.call-start = ((), (), s32[]{:S(2)}) async-start(), calls=%async_computation.8 | async-start | bytes 1966080 | tf_op jit(solution)/shard_map/all_gather | solution.py:150
  12.1 21.8 %copy-start.40 = (f32[768]{0:T(1024)}, f32[768]{0:T(1024)S(1)}, u32[]{:S(2)}) copy-start(f32[768]{0:T(1024)S(1)} %reshape.613) | copy-start | bytes 9220
  16.1 17.9 %copy-start.59 = (f32[768]{0:T(1024)}, f32[768]{0:T(1024)S(1)}, u32[]{:S(2)}) copy-start(f32[768]{0:T(1024)S(1)} %reshape.614) | copy-start | bytes 9220
  17.8 16.2 %copy-start.38 = (f32[1024]{0:T(1024)}, f32[1024]{0:T(1024)S(1)}, u32[]{:S(2)}) copy-start(f32[1024]{0:T(1024)S(1)} %broadcast_multiply_fusion.1) | copy-start | bytes 12292
  19.8 14.1 %copy-start.44 = (f32[1024]{0:T(1024)}, f32[1024]{0:T(1024)S(1)}, u32[]{:S(2)}) copy-start(f32[1024]{0:T(1024)S(1)} %fusion.59) | copy-start | bytes 12292
  34.3 5.0 copy-start.37
  35.6 54.5 %copy-start.23 = (bf16[1024,3,32]{0,2,1:T(8,128)(2,1)}, bf16[1024,3,32]{0,2,1:T(8,128)(2,1)S(1)}, u32[]{:S(2)}) copy-start(bf16[1024,3,32]{0,2,1:T(8,128)(2,1)S(1)} %get-tuple-element.62) | copy-start | bytes 589828
  35.6 54.5 %copy-start.26 = (bf16[1024,3,32]{0,2,1:T(8,128)(2,1)}, bf16[1024,3,32]{0,2,1:T(8,128)(2,1)S(1)}, u32[]{:S(2)}) copy-start(bf16[1024,3,32]{0,2,1:T(8,128)(2,1)S(1)} %get-tuple-element.63) | copy-start | bytes 589828
  36.5 78.4 %all-gather.19.cloned.1.call-start = ((), (), s32[]{:S(2)}) async-start(), calls=%async_computation.17 | async-start | bytes 1966080 | tf_op jit(solution)/shard_map/all_gather | solution.py:151
  38.5 181.4 %all-reduce.15.cloned.1.call-start = ((), (), s32[]{:S(2)}) async-start(), calls=%async_computation.9 | async-start | bytes 6291456 | tf_op jit(solution)/shard_map/psum | solution.py:186
  76.8 13.2 %copy-start.10 = (bf16[4096,192]{0,1:T(8,128)(2,1)S(1)}, bf16[4096,192]{0,1:T(8,128)(2,1)}, u32[]{:S(2)}) copy-start(bf16[4096,192]{0,1:T(8,128)(2,1)} %all-gather.13.cloned.1.call-done) | copy-start | bytes 4718596
  76.8 13.3 %copy-start.22 = (pred[512,4096]{1,0:T(8,128)(4,1)S(1)}, pred[512,4096]{1,0:T(8,128)(4,1)}, u32[]{:S(2)}) copy-start(pred[512,4096]{1,0:T(8,128)(4,1)} %get-tuple-element.73) | copy-start | bytes 6291460
  125.9 10.6 %copy-start.13 = (bf16[4096,1,192]{0,2,1:T(8,128)(2,1)S(1)}, bf16[4096,1,192]{0,2,1:T(8,128)(2,1)}, u32[]{:S(2)}) copy-start(bf16[4096,1,192]{0,2,1:T(8,128)(2,1)} %all-gather.19.cloned.1.call-done) | copy-start | bytes 4718596
  148.3 3.5 copy-start.63
  148.3 6.8 copy-start.64
  148.3 10.1 %copy-start.65 = (bf16[384]{0:T(512)(128)(2,1)S(1)}, bf16[384]{0:T(512)(128)(2,1)}, u32[]{:S(2)}) copy-start(bf16[384]{0:T(512)(128)(2,1)} %param.28) | copy-start | bytes 2308
  150.6 11.4 %copy-start.57 = (bf16[12,32]{1,0:T(8,128)(2,1)S(1)}, bf16[12,32]{1,0:T(8,128)(2,1)}, u32[]{:S(2)}) copy-start(bf16[12,32]{1,0:T(8,128)(2,1)} %param.22) | copy-start | bytes 2308
  150.6 73.9 %all-gather.15.cloned.1.call-start = ((), (), s32[]{:S(2)}) async-start(), calls=%async_computation.10 | async-start | bytes 1769472 | tf_op jit(solution)/shard_map/all_gather | solution.py:92
  151.2 85.2 %all-gather.17.cloned.1.call-start = ((), (), s32[]{:S(2)}) async-start(), calls=%async_computation.11 | async-start | bytes 1769472 | tf_op jit(solution)/shard_map/all_gather | solution.py:94
  151.8 163.7 %all-reduce.19.cloned.1.call-start = ((), (), s32[]{:S(2)}) async-start(), calls=%async_computation.13 | async-start | bytes 6291456 | tf_op jit(solution)/shard_map/psum | solution.py:206
  158.3 203.0 %copy-start.48 = (f32[768]{0:T(1024)}, f32[768]{0:T(1024)S(1)}, u32[]{:S(2)}) copy-start(f32[768]{0:T(1024)S(1)} %reshape.616) | copy-start | bytes 9220
  161.9 62.6 %copy-start.60 = (f32[768]{0:T(1024)}, f32[768]{0:T(1024)S(1)}, u32[]{:S(2)}) copy-start(f32[768]{0:T(1024)S(1)} %reshape.617) | copy-start | bytes 9220
  222.3 139.0 %copy-start.42 = (f32[1024]{0:T(1024)}, f32[1024]{0:T(1024)S(1)}, u32[]{:S(2)}) copy-start(f32[1024]{0:T(1024)S(1)} %broadcast_multiply_fusion) | copy-start | bytes 12292
  224.5 136.9 %copy-start.50 = (f32[1024]{0:T(1024)}, f32[1024]{0:T(1024)S(1)}, u32[]{:S(2)}) copy-start(f32[1024]{0:T(1024)S(1)} %fusion.60) | copy-start | bytes 12292
  224.5 11.9 %copy-start.15 = (bf16[1,1024,768]{2,1,0:T(8,128)(2,1)S(1)}, bf16[1,1024,768]{2,1,0:T(8,128)(2,1)}, u32[]{:S(2)}) copy-start(bf16[1,1024,768]{2,1,0:T(8,128)(2,1)} %param.29) | copy-start | bytes 4718596
  236.4 7.2 copy-start.67
  246.7 114.7 %all-reduce.17.cloned.1.call-start = ((), (), s32[]{:S(2)}) async-start(), calls=%async_computation.12 | async-start | bytes 3145728 | tf_op jit(solution)/shard_map/psum | solution.py:196
  250.8 64.6 %copy-start.5 = (f32[1024,768]{1,0:T(8,128)S(1)}, f32[1024,768]{1,0:T(8,128)}, u32[]{:S(2)}) copy-start(f32[1024,768]{1,0:T(8,128)} %copy-done.4) | copy-start | bytes 9437188
  255.2 253.8 %reduce-scatter.13.cloned.1.call-start = ((), (), s32[]{:S(2)}) async-start(), calls=%async_computation.14 | async-start | bytes 3932160 | tf_op jit(solution)/shard_map/reduce_scatter | solution.py:251
  361.4 4.2 copy-start.16
  365.6 3.5 copy-start.14
  388.3 17.0 %copy-start.24 = (bf16[1024,3,32]{0,2,1:T(8,128)(2,1)S(1)}, bf16[1024,3,32]{0,2,1:T(8,128)(2,1)}, u32[]{:S(2)}) copy-start(bf16[1024,3,32]{0,2,1:T(8,128)(2,1)} %copy-done.23) | copy-start | bytes 589828
  388.3 17.1 %copy-start.27 = (bf16[1024,3,32]{0,2,1:T(8,128)(2,1)S(1)}, bf16[1024,3,32]{0,2,1:T(8,128)(2,1)}, u32[]{:S(2)}) copy-start(bf16[1024,3,32]{0,2,1:T(8,128)(2,1)} %copy-done.26) | copy-start | bytes 589828
  405.4 4.5 copy-start
  426.7 17.3 %copy-start.25 = (bf16[1024,3,32]{0,2,1:T(8,128)(2,1)S(1)}, bf16[1024,3,32]{0,2,1:T(8,128)(2,1)}, u32[]{:S(2)}) copy-start(bf16[1024,3,32]{0,2,1:T(8,128)(2,1)} %copy-done.23) | copy-start | bytes 589828
  426.7 17.3 %copy-start.28 = (bf16[1024,3,32]{0,2,1:T(8,128)(2,1)S(1)}, bf16[1024,3,32]{0,2,1:T(8,128)(2,1)}, u32[]{:S(2)}) copy-start(bf16[1024,3,32]{0,2,1:T(8,128)(2,1)} %copy-done.26) | copy-start | bytes 589828
  444.1 5.4 copy-start.1
  449.5 122.2 %reduce-scatter.15.cloned.1.call-start = ((), (), s32[]{:S(2)}) async-start(), calls=%async_computation.15 | async-start | bytes 3932160 | tf_op jit(solution)/shard_map/reduce_scatter | solution.py:254
  473.0 117.9 %reduce-scatter.19.cloned.1.call-start = ((), (), s32[]{:S(2)}) async-start(), calls=%async_computation.19 | async-start | bytes 884736 | tf_op jit(solution)/shard_map/reduce_scatter | solution.py:293
  475.8 5.1 copy-start.6
  475.8 5.1 copy-start.43
  475.8 5.1 copy-start.49
  475.8 5.1 copy-start.51
  475.8 5.1 copy-start.61
  475.8 152.1 %reduce-scatter.23.cloned.1.call-start = ((), (), s32[]{:S(2)}) async-start(), calls=%async_computation.21 | async-start | bytes 3538944 | tf_op jit(solution)/shard_map/reduce_scatter | solution.py:297
  480.8 184.1 %reduce-scatter.21.cloned.1.call-start = ((), (), s32[]{:S(2)}) async-start(), calls=%async_computation.20 | async-start | bytes 3538944 | tf_op jit(solution)/shard_map/reduce_scatter | solution.py:295
  485.5 209.9 %reduce-scatter.17.cloned.1.call-start = ((), (), s32[]{:S(2)}) async-start(), calls=%async_computation.18 | async-start | bytes 2654208 | tf_op jit(solution)/shard_map/reduce_scatter | solution.py:291
  495.5 13.5 %copy-start.30 = (f32[1024,32]{0,1:T(8,128)S(1)}, f32[1024,32]{0,1:T(8,128)}, u32[]{:S(2)}) copy-start(f32[1024,32]{0,1:T(8,128)} %copy-done.29) | copy-start | bytes 393220
  495.5 13.5 %copy-start.32 = (f32[1024,32]{0,1:T(8,128)S(1)}, f32[1024,32]{0,1:T(8,128)}, u32[]{:S(2)}) copy-start(f32[1024,32]{0,1:T(8,128)} %copy-done.31) | copy-start | bytes 393220
  510.4 62.8 %copy-start.3 = (bf16[1,1024,768]{2,1,0:T(8,128)(2,1)S(1)}, bf16[1,1024,768]{2,1,0:T(8,128)(2,1)}, u32[]{:S(2)}) copy-start(bf16[1,1024,768]{2,1,0:T(8,128)(2,1)} %param.15) | copy-start | bytes 4718596
  510.4 62.8 %copy-start.39 = (f32[1024]{0:T(1024)S(1)}, f32[1024]{0:T(1024)}, u32[]{:S(2)}) copy-start(f32[1024]{0:T(1024)} %copy-done.38) | copy-start | bytes 12292
  510.4 62.8 %copy-start.41 = (f32[768]{0:T(1024)S(1)}, f32[768]{0:T(1024)}, u32[]{:S(2)}) copy-start(f32[768]{0:T(1024)} %copy-done.40) | copy-start | bytes 9220
  510.4 62.8 %copy-start.45 = (f32[1024]{0:T(1024)S(1)}, f32[1024]{0:T(1024)}, u32[]{:S(2)}) copy-start(f32[1024]{0:T(1024)} %copy-done.44) | copy-start | bytes 12292
  576.5 131.2 %reduce-scatter.27.cloned.1.call-start = ((), (), s32[]{:S(2)}) async-start(), calls=%async_computation.23 | async-start | bytes 49152
  577.4 143.1 %reduce-scatter.25.cloned.1.call-start = ((), (), s32[]{:S(2)}) async-start(), calls=%async_computation.22 | async-start | bytes 49152
  578.4 213.6 %all-reduce.21.cloned.1.call-start = ((), (), s32[]{:S(2)}) async-start(), calls=%async_computation.16 | async-start | bytes 6291456 | tf_op jit(solution)/shard_map/psum | solution.py:270
  582.7 112.8 %copy-start.68 = (u32[32]{0:T(128)S(1)}, u32[32]{0:T(128)}, u32[]{:S(2)}) copy-start(u32[32]{0:T(128)} %constant.156) | copy-start | bytes 388
  582.8 344.9 %all-reduce.23.cloned.1.call-start = ((), (), s32[]{:S(2)}) async-start(), calls=%async_computation.24 | async-start | bytes 7077888 | tf_op jit(solution)/shard_map/psum | solution.py:273
  695.5 99.5 %copy-start.53 = (f32[1024]{0:T(1024)S(1)}, f32[1024]{0:T(1024)}, u32[]{:S(2)}) copy-start(f32[1024]{0:T(1024)} %copy-done.52) | copy-start | bytes 12292
  927.7 4.0 copy-start.34
  927.7 5.0 copy-start.33
  (23 other events, 40.2 us)
Sparse Core Ops, SparseCore 0:
  36.6 40.1 all-gather.12
  79.0 35.8 all-gather.18
  150.7 69.1 all-reduce.14
  246.8 68.5 all-reduce.18
  318.2 43.1 all-reduce.16
  449.6 59.3 reduce-scatter.12
  511.3 60.3 reduce-scatter.14
  574.6 16.2 reduce-scatter.18
  593.1 34.7 reduce-scatter.22
  630.1 34.7 reduce-scatter.20
  667.1 28.3 reduce-scatter.16
  698.1 9.5 reduce-scatter.26
  710.5 9.9 reduce-scatter.24
  723.3 68.7 all-reduce.20
  794.5 133.1 all-reduce.22
Sparse Core Ops, SparseCore 1:
  152.6 23.5 all-gather.14
  177.6 22.6 all-gather.16
where the time goes:
time: 950 us; the launch traced here: 941 us
  waiting for transfers between devices  560 us (59%)
  matrix products  178 us (19%)
  other arithmetic  94.1 us (10%)
  blocking collectives  62.5 us (7%)
  local copies, waits for them, and re-layouts  27.8 us (3%)
  between operations  18.2 us (2%)
    psum x1, waiting for transfers between devices, body(): lax.psum((g_qkv, g_bqkv, g_out, g_bout, g_up, g_bup, g_down, g_bdown, g_g...  105 us
    psum x1, waiting for transfers between devices, body(): grad_normed = lax.psum(grad_one_part, 'tp')  70.6 us
    reduce_scatter x1, waiting for transfers between devices, body(): lax.psum_scatter(grad_values.reshape(total_rows, local_width), 'ctx', sca...  61.2 us
    psum x1, waiting for transfers between devices, body(): grad_normed_two = lax.psum(grad_two_part, 'tp')  60.1 us
    psum x1, waiting for transfers between devices, body(): middle = values + lax.psum(branch_part, 'tp') + bias_out  54.2 us
    psum x1, waiting for transfers between devices, body(): lax.psum(mlp_part.astype(jnp.bfloat16), 'tp').astype(jnp.float32)  42.5 us
    reduce_scatter x1, waiting for transfers between devices, body(): lax.psum_scatter(summed[6], 'fsdp', scatter_dimension=1, tiled=True)  37.1 us
    reduce_scatter x1, waiting for transfers between devices, body(): lax.psum_scatter(summed[4], 'fsdp', scatter_dimension=0, tiled=True)  36.9 us
  transfers between devices with their start and end apart: 17, of which 15 were waited for; matrix products, arithmetic and copies ran while one was open for 15% of the time, Pallas kernels for 0%

commit v1 on v0

v1 whole, which is shorter than its diff:
```python
import functools
import jax
import jax.numpy as jnp
from jax import lax
from jax.experimental import pallas as pl
from jax.experimental.pallas import tpu as pltpu
from jax.sharding import PartitionSpec as P

HD = 64
BLOCK = 16
TILE = 256
LOG2E = 1.4426950408889634
NEG = -1e30


def stack_heads(rows, heads):
    lane = lax.broadcasted_iota(jnp.int32, rows.shape, 1) // HD
    return jnp.concatenate([jnp.where(lane == h, rows, jnp.zeros_like(rows)) for h in range(heads)], axis=0)


def tile_plan(sc_ref, i, tiles):
    z, s, pfx = sc_ref[0], sc_ref[1], sc_ref[2]
    half = sc_ref[3]
    noisy = z < half
    late = lax.rem(z, half)
    place = late * tiles + (i ^ s)
    below = i ^ s
    full_f = late * tiles
    plain = below + full_f
    opened = jnp.where(late == 0, (pfx + TILE - 1) // TILE, 0)
    top = jnp.maximum(below + 1, opened)
    masked = top - below
    total = plain + masked + noisy.astype(jnp.int32)

    def address(slot):
        near = tiles + (slot ^ s)
        far = 2 * tiles + (slot - below)
        edge = tiles + (((slot - plain + below) & (tiles - 1)) ^ s)
        own = i
        at = jnp.where(slot < below, near, jnp.where(slot < plain, far, jnp.where(slot < plain + masked, edge, own)))
        return pl.multiple_of(at * TILE, TILE)

    def mask_terms(slot):
        is_own = slot >= plain + masked
        tile_at = slot - plain + below
        return is_own, tile_at

    return noisy, late, below, plain, masked, total, address, mask_terms, pfx


def allowed(q_pos, k_pos, q_tile, k_tile, is_own, noisy, prefix):
    qb = q_tile * (TILE // BLOCK) + q_pos // BLOCK
    kb = k_tile * (TILE // BLOCK) + k_pos // BLOCK
    step = jnp.where(noisy, 0, 1)
    seen = (kb < qb + step) | (k_tile * TILE + k_pos < prefix)
    return seen


def fwd_kernel(tiles, heads, sc_ref, q_ref, k_ref, v_ref, o_ref, lse_ref, sbuf, mbuf, lbuf, acc):
    i = pl.program_id(0)
    noisy, late, below, plain, masked, total, address, mask_terms, pfx = tile_plan(sc_ref, i, tiles)
    width = heads * HD
    qs = stack_heads(q_ref[...], heads)
    mbuf[...] = jnp.full_like(mbuf, NEG)
    lbuf[...] = jnp.zeros_like(lbuf)
    acc[...] = jnp.zeros_like(acc)

    def score(slot):
        k = k_ref[pl.ds(address(slot), TILE), :]
        return lax.dot_general(qs, k, (((1,), (1,)), ((), ())), preferred_element_type=jnp.float32)

    def keep(slot, s):
        sbuf[slot] = s
        mbuf[...] = jnp.maximum(mbuf[...], jnp.maximum(s[:, :128], s[:, 128:]))

    def plain_step(slot, carry):
        keep(slot, score(slot))
        return carry

    lax.fori_loop(0, plain, plain_step, 0)
    q_pos = lax.broadcasted_iota(jnp.int32, (heads * TILE, TILE), 0) & (TILE - 1)
    k_pos = lax.broadcasted_iota(jnp.int32, (heads * TILE, TILE), 1)
    prefix = jnp.where(late == 0, pfx, 0)

    def edge_step(slot, carry):
        s = score(slot)
        seen = allowed(q_pos, k_pos, below, slot - plain + below, None, noisy, prefix)
        keep(slot, jnp.where(seen, s, NEG))
        return carry

    lax.fori_loop(plain, plain + masked, edge_step, 0)

    @pl.when(noisy)
    def _():
        slot = plain + masked
        s = score(slot)
        keep(slot, jnp.where(q_pos // BLOCK == k_pos // BLOCK, s, NEG))

    top = jnp.max(mbuf[...], axis=1, keepdims=True) * LOG2E
    mbuf[...] = jnp.broadcast_to(top, mbuf.shape)

    def sum_step(slot, carry):
        v = v_ref[pl.ds(address(slot), TILE), :]
        m = mbuf[...]
        s = sbuf[slot]
        p0 = jnp.exp2(s[:, :128] * LOG2E - m)
        p1 = jnp.exp2(s[:, 128:] * LOG2E - m)
        lbuf[...] += p0 + p1
        p = jnp.concatenate([p0, p1], axis=1).astype(jnp.bfloat16)
        acc[...] += jnp.dot(p, v, preferred_element_type=jnp.float32)
        return carry

    lax.fori_loop(0, total, sum_step, 0)
    norm = jnp.sum(lbuf[...], axis=1, keepdims=True)
    out = acc[...] * (1.0 / norm)
    lane = lax.broadcasted_iota(jnp.int32, (TILE, width), 1) // HD
    picked = out[:TILE]
    for h in range(1, heads):
        picked = jnp.where(lane == h, out[h * TILE : (h + 1) * TILE], picked)
    o_ref[...] = picked.astype(o_ref.dtype)
    lse = jnp.broadcast_to(top + jnp.log2(norm), (heads * TILE, 128))
    lse_ref[0] = jnp.concatenate([lse[h * TILE : (h + 1) * TILE].T[:1] for h in range(heads)] + [jnp.zeros((8 - heads, TILE), jnp.float32)], axis=0)


def attention(scalars, q, k, v):
    rows, width = q.shape
    tiles, heads = rows // TILE, width // HD
    whole = lambda i, sc: (0, 0)
    slots = 2 * tiles + 1
    return pl.pallas_call(
        functools.partial(fwd_kernel, tiles, heads),
        name="attn_fwd",
        out_shape=(jax.ShapeDtypeStruct((rows, width), jnp.bfloat16), jax.ShapeDtypeStruct((tiles, 8, TILE), jnp.float32)),
        grid_spec=pltpu.PrefetchScalarGridSpec(
            num_scalar_prefetch=1,
            grid=(tiles,),
            in_specs=[
                pl.BlockSpec((TILE, width), lambda i, sc: (i, 0)),
                pl.BlockSpec(k.shape, whole),
                pl.BlockSpec(v.shape, whole),
            ],
            out_specs=[
                pl.BlockSpec((TILE, width), lambda i, sc: (i, 0)),
                pl.BlockSpec((1, 8, TILE), lambda i, sc: (i, 0, 0)),
            ],
            scratch_shapes=[
                pltpu.VMEM((slots, heads * TILE, TILE), jnp.float32),
                pltpu.VMEM((heads * TILE, 128), jnp.float32),
                pltpu.VMEM((heads * TILE, 128), jnp.float32),
                pltpu.VMEM((heads * TILE, width), jnp.float32),
            ],
        ),
        compiler_params=pltpu.CompilerParams(dimension_semantics=("arbitrary",), vmem_limit_bytes=48 << 20),
        cost_estimate=pl.CostEstimate(flops=12_000_000_000, bytes_accessed=4_000_000, transcendentals=0),
    )(scalars, q, k, v)


def bwd_kernel(tiles, heads, sc_ref, q_ref, o_ref, g_ref, lse_ref, k_ref, v_ref, dq_ref, dk_ref, dv_ref, dqt, st, gt, lse_s, del_s, qs_s, gs_s):
    i = pl.program_id(0)
    noisy, late, below, plain, masked, total, address, mask_terms, pfx = tile_plan(sc_ref, i, tiles)
    width = heads * HD

    @pl.when(i == 0)
    def _():
        dk_ref[...] = jnp.zeros_like(dk_ref)
        dv_ref[...] = jnp.zeros_like(dv_ref)

    q = q_ref[...]
    g = g_ref[...]
    qs_s[...] = stack_heads(q, heads)
    gs_s[...] = stack_heads(g, heads)
    q_t = q.astype(jnp.float32).T
    g_t = g.astype(jnp.float32).T
    prod = (o_ref[...].astype(jnp.float32) * g.astype(jnp.float32)).T
    head_of = lax.broadcasted_iota(jnp.int32, (width, TILE), 0) // HD
    for h in range(heads):
        cols = slice(h * TILE, (h + 1) * TILE)
        st[:, cols] = jnp.where(head_of == h, q_t, 0.0).astype(jnp.bfloat16)
        gt[:, cols] = jnp.where(head_of == h, g_t, 0.0).astype(jnp.bfloat16)
        del_s[:, cols] = jnp.sum(prod[h * HD : (h + 1) * HD], axis=0, keepdims=True)
        lse_s[:, cols] = lse_ref[0, h : h + 1, :]
    dqt[...] = jnp.zeros_like(dqt)

    def step(slot, mask):
        at = address(slot)
        k = k_ref[pl.ds(at, TILE), :]
        v = v_ref[pl.ds(at, TILE), :]
        s = jnp.dot(k, st[...], preferred_element_type=jnp.float32)
        p = jnp.exp2(s * LOG2E - lse_s[...])
        if mask is not None:
            p = jnp.where(mask, p, 0.0)
        dp = jnp.dot(v, gt[...], preferred_element_type=jnp.float32)
        ds = (p * (dp - del_s[...])).astype(jnp.bfloat16)
        p = p.astype(jnp.bfloat16)
        dv_ref[pl.ds(at, TILE), :] += jnp.dot(p, gs_s[...], preferred_element_type=jnp.float32)
        dk_ref[pl.ds(at, TILE), :] += jnp.dot(ds, qs_s[...], preferred_element_type=jnp.float32)
        dqt[...] += lax.dot_general(k, ds, (((0,), (0,)), ((), ())), preferred_element_type=jnp.float32)

    def plain_step(slot, carry):
        step(slot, None)
        return carry

    lax.fori_loop(0, plain, plain_step, 0)
    k_pos = lax.broadcasted_iota(jnp.int32, (TILE, heads * TILE), 0)
    q_pos = lax.broadcasted_iota(jnp.int32, (TILE, heads * TILE), 1) & (TILE - 1)
    prefix = jnp.where(late == 0, pfx, 0)

    def edge_step(slot, carry):
        step(slot, allowed(q_pos, k_pos, below, slot - plain + below, None, noisy, prefix))
        return carry

    lax.fori_loop(plain, plain + masked, edge_step, 0)

    @pl.when(noisy)
    def _():
        step(plain + masked, q_pos // BLOCK == k_pos // BLOCK)

    dq_t = jnp.where(head_of == 0, dqt[:, :TILE], 0.0)
    for h in range(1, heads):
        dq_t = jnp.where(head_of == h, dqt[:, h * TILE : (h + 1) * TILE], dq_t)
    dq_ref[...] = dq_t.T * (HD**-0.5)


def attention_grads(scalars, q, o, g, lse, k, v):
    rows, width = q.shape
    tiles, heads = rows // TILE, width // HD
    whole = lambda i, sc: (0, 0)
    tile = pl.BlockSpec((TILE, width), lambda i, sc: (i, 0))
    return pl.pallas_call(
        functools.partial(bwd_kernel, tiles, heads),
        name="attn_bwd",
        out_shape=(
            jax.ShapeDtypeStruct((rows, width), jnp.float32),
            jax.ShapeDtypeStruct(k.shape, jnp.float32),
            jax.ShapeDtypeStruct(v.shape, jnp.float32),
        ),
        grid_spec=pltpu.PrefetchScalarGridSpec(
            num_scalar_prefetch=1,
            grid=(tiles,),
            in_specs=[
                tile,
                tile,
                tile,
                pl.BlockSpec((1, 8, TILE), lambda i, sc: (i, 0, 0)),
                pl.BlockSpec(k.shape, whole),
                pl.BlockSpec(v.shape, whole),
            ],
            out_specs=[tile, pl.BlockSpec(k.shape, whole), pl.BlockSpec(v.shape, whole)],
            scratch_shapes=[
                pltpu.VMEM((width, heads * TILE), jnp.float32),
                pltpu.VMEM((width, heads * TILE), jnp.bfloat16),
                pltpu.VMEM((width, heads * TILE), jnp.bfloat16),
                pltpu.VMEM((1, heads * TILE), jnp.float32),
                pltpu.VMEM((1, heads * TILE), jnp.float32),
                pltpu.VMEM((heads * TILE, width), jnp.bfloat16),
                pltpu.VMEM((heads * TILE, width), jnp.bfloat16),
            ],
        ),
        compiler_params=pltpu.CompilerParams(dimension_semantics=("arbitrary",), vmem_limit_bytes=48 << 20),
        cost_estimate=pl.CostEstimate(flops=30_000_000_000, bytes_accessed=12_000_000, transcendentals=0),
    )(scalars, q, o, g, lse, k, v)


epsilon = 1e-05
PAIR = [(0, 1), (1, 0)]


def low(values):
    return values.astype(jnp.bfloat16)


def wide(values):
    return values.astype(jnp.float32)


def dot(a, b, ca=1, cb=0):
    return lax.dot_general(a, b, (((ca,), (cb,)), ((), ())), preferred_element_type=jnp.float32)


def row_stats(values):
    mean = jnp.mean(values, axis=-1, keepdims=True)
    centered = values - mean
    variance = jnp.mean(centered * centered, axis=-1, keepdims=True)
    return mean, lax.rsqrt(variance + epsilon)


def normalize(values, gain, shift):
    mean, scale = row_stats(values)
    return (values - mean) * scale * gain + shift


def norm_grad(grad, values, gain):
    mean, scale = row_stats(values)
    unit = (values - mean) * scale
    weighted = grad * gain
    return scale * (weighted - jnp.mean(weighted, axis=-1, keepdims=True) - unit * jnp.mean(weighted * unit, axis=-1, keepdims=True))


def rotate(values, cosine, sine):
    rows, width = values.shape
    split = values.reshape(rows, width // HD, HD)
    first, second = split[..., : HD // 2], split[..., HD // 2 :]
    return jnp.concatenate([first * cosine - second * sine, second * cosine + first * sine], axis=-1).reshape(rows, width)


def angles(positions):
    half_width = HD // 2
    frequency = jnp.power(jnp.float32(10000.0), -2.0 * jnp.arange(half_width, dtype=jnp.float32) / HD)
    angle_rows = wide(positions)[:, None] * frequency[None, :]
    return (jnp.cos(angle_rows)[:, None, :], jnp.sin(angle_rows)[:, None, :])


def swap_core(values):
    return lax.ppermute(values, "tp", [(i, i ^ 1) for i in range(4)])


def swap_y(values):
    return lax.ppermute(values, "tp", [(i, i ^ 2) for i in range(4)])


def hop(values, pairs):
    return lax.ppermute(values, "ctx", pairs)


def pick(parts, index):
    return lax.dynamic_index_in_dim(parts, index, 0, keepdims=False)


def ordered(first, second, flip):
    return jnp.where(flip == 0, jnp.stack([first, second]), jnp.stack([second, first]))


def sum_ctx(values, z):
    near, far = z & 1, z >> 1
    near_pairs, far_pairs = [(i, i ^ 1) for i in range(4)], [(i, i ^ 2) for i in range(4)]
    rows, cols = values.shape
    halves = values.reshape(2, rows // 2, cols)
    half = pick(halves, near) + wide(hop(low(pick(halves, 1 - near)), near_pairs))
    quarters = half.reshape(2, rows // 4, cols)
    quarter = low(pick(quarters, far) + wide(hop(low(pick(quarters, 1 - far)), far_pairs)))
    half = ordered(quarter, hop(quarter, far_pairs), far).reshape(rows // 2, cols)
    return wide(ordered(half, hop(half, near_pairs), near).reshape(rows, cols))


def body(
    hidden,
    prefix,
    w_qkv,
    b_qkv,
    w_out,
    b_out,
    w_up,
    b_up,
    w_down,
    b_down,
    ln1_gain,
    ln1_shift,
    ln2_gain,
    ln2_shift,
    cotangent,
):
    members = lax.axis_size("fsdp")
    paired = members == 2
    z = lax.axis_index("ctx")
    t = lax.axis_index("tp")
    half_ctx = lax.axis_size("ctx") // 2
    core, side = t & 1, t >> 1
    turn = 2 * core + side
    f = lax.axis_index("fsdp") if paired else jnp.int32(0)
    rows, width = hidden.shape[1], hidden.shape[2]
    local = w_qkv.shape[2]
    units = w_up.shape[1]
    tiles = rows // TILE
    half, quarter = rows // 2, rows // 4
    part = width // 2

    def turned(values):
        grid = values.reshape(tiles, TILE, 2, part)
        near = lax.dynamic_index_in_dim(grid, f, 2, keepdims=False)
        far = lax.dynamic_index_in_dim(grid, 1 - f, 2, keepdims=False)
        both = jnp.concatenate([near, far], axis=-1)
        return jnp.concatenate([pick(both, j ^ turn) for j in range(tiles)], axis=0)

    def unturned(values):
        grid = values.reshape(tiles, TILE, width)
        grid = jnp.concatenate([pick(grid, j ^ turn) for j in range(tiles)], axis=0)
        return jnp.where(f == 0, grid, jnp.concatenate([grid[:, part:], grid[:, :part]], axis=1))

    def gathered(values, axis):
        if paired:
            return jnp.concatenate([values, lax.ppermute(values, "fsdp", PAIR)], axis=axis)
        return lax.all_gather(values, "fsdp", axis=axis, tiled=True)

    small = jnp.concatenate(
        [v.reshape(-1) for v in (ln1_gain, ln1_shift, b_qkv, b_out, ln2_gain, ln2_shift, b_up, b_down)]
    )
    if paired:
        own_small, other_small = small, lax.ppermute(small, "fsdp", PAIR)
        pieces = [own_small, other_small]
    else:
        pieces = list(lax.all_gather(small, "fsdp", axis=0, tiled=False))
    sizes = [v.size for v in (ln1_gain, ln1_shift, b_qkv, b_out, ln2_gain, ln2_shift, b_up, b_down)]
    starts = [sum(sizes[:n]) for n in range(len(sizes))]

    def vector(n):
        return wide(jnp.concatenate([p[starts[n] : starts[n] + sizes[n]] for p in pieces]))

    def folded(n, shape):
        parts = [p[starts[n] : starts[n] + sizes[n]].reshape(shape) for p in pieces]
        if paired:
            parts = [jnp.where(f == 0, parts[0], parts[1]), jnp.where(f == 0, parts[1], parts[0])]
        return wide(jnp.concatenate(parts, axis=-1)).reshape(-1)

    gain_one, shift_one = vector(0), vector(1)
    bias_qkv = folded(2, b_qkv.shape)
    bias_out, gain_two, shift_two = vector(3), vector(4), vector(5)
    bias_up = folded(6, b_up.shape)
    bias_down = vector(7)

    full_qkv = gathered(w_qkv.reshape(w_qkv.shape[0], 3 * local), 0)
    values_low = turned(hidden[0])

    own_quarter = values_low[:quarter]
    near_quarter = hop(own_quarter, [(i + half_ctx, i) for i in range(half_ctx)])
    near_quarter = jnp.where(z >= half_ctx, own_quarter, near_quarter)
    far_quarter = hop(own_quarter, [(2, 1)]) + hop(own_quarter, [(2, 3)])

    def spread(values):
        pair = jnp.concatenate([values, swap_y(values)], axis=0)
        return [pair, swap_core(pair)]

    seen_low = jnp.concatenate(spread(near_quarter) + spread(far_quarter), axis=0)

    full_out = gathered(w_out, 1)
    full_up = gathered(w_up, 0)
    full_down = gathered(w_down, 1)

    values = wide(values_low)
    upstream_low = turned(cotangent[0])

    tile_at = jnp.concatenate([jnp.full((TILE,), j, jnp.int32) ^ turn for j in range(tiles)])
    place = tile_at * TILE + (jnp.arange(rows, dtype=jnp.int32) & (TILE - 1))
    cos_own, sin_own = angles(place + (z % half_ctx) * rows)
    cos_far, sin_far = angles(place)
    cos_seen, sin_seen = jnp.concatenate([cos_own, cos_far]), jnp.concatenate([sin_own, sin_far])

    normed = low(normalize(values, gain_one, shift_one))
    projected = dot(normed, full_qkv) + bias_qkv
    score_scale = HD ** (-0.5)
    queries = low(rotate(projected[:, :local], cos_own, sin_own)) * jnp.bfloat16(score_scale)
    keys_own = low(rotate(projected[:, local : 2 * local], cos_own, sin_own))
    values_own = low(projected[:, 2 * local :])
    normed_seen = low(normalize(wide(seen_low), gain_one, shift_one))
    projected_seen = dot(normed_seen, full_qkv[:, local:]) + bias_qkv[local:]
    keys_seen = low(rotate(projected_seen[:, :local], cos_seen, sin_seen))
    values_seen = low(projected_seen[:, local:])
    keys_all = jnp.concatenate([keys_own, keys_seen], axis=0)
    values_all = jnp.concatenate([values_own, values_seen], axis=0)
    scalars = jnp.stack([z, turn, prefix[0], jnp.int32(half_ctx)]).astype(jnp.int32)
    attended, log_sums = attention(scalars, queries, keys_all, values_all)

    def reduced_half(first, second):
        return low(first + wide(swap_core(low(second))))

    def summed_half(first, second):
        mine = reduced_half(first, second)
        theirs = swap_y(mine)
        return wide(mine) + wide(jnp.concatenate([theirs[quarter:], theirs[:quarter]], axis=0))

    branch = summed_half(dot(attended[:half], full_out), dot(attended[half:], full_out))
    middle = values[:half] + branch + bias_out
    two_own = low(normalize(middle, gain_two, shift_two))
    two = (two_own, swap_core(two_own))
    dy = (upstream_low[:half], upstream_low[half:])
    acts, slopes = [], []
    for h in range(2):
        pre = dot(two[h], full_up) + bias_up
        cdf = 0.5 * (1.0 + lax.erf(pre * (2.0**-0.5)))
        acts.append(low(pre * cdf))
        slopes.append(cdf + pre * jnp.exp(-0.5 * pre * pre) * ((2.0 * jnp.pi) ** -0.5))
    grads_pre = [low(dot(dy[h], full_down, 1, 1) * slopes[h]) for h in range(2)]
    da_two = summed_half(dot(grads_pre[0], full_up, 1, 1), dot(grads_pre[1], full_up, 1, 1))
    dmid = wide(dy[0]) + norm_grad(da_two, middle, gain_two)
    dz_own = low(dmid)
    dz = (dz_own, swap_core(dz_own))
    grad_att = jnp.concatenate([low(dot(dz[h], full_out, 1, 1)) for h in range(2)], axis=0)

    down = summed_half(dot(acts[0], full_down), dot(acts[1], full_down))
    result_own = low(middle + down + bias_down)
    result = unturned(jnp.concatenate([result_own, swap_core(result_own)], axis=0))

    g_up = sum(dot(two[h], grads_pre[h], 0, 0) for h in range(2))
    g_down = sum(dot(dy[h], acts[h], 0, 0) for h in range(2))
    g_out = sum(dot(dz[h], attended[h * half : (h + 1) * half], 0, 0) for h in range(2))
    gb_up = sum(jnp.sum(wide(grads_pre[h]), axis=0) for h in range(2))
    gb_down = sum(jnp.sum(wide(dy[h]), axis=0) for h in range(2)) * 0.25
    gb_out = jnp.sum(wide(dz_own), axis=0) * 0.5

    def own_rows(values):
        if paired:
            return values[:part] + wide(lax.ppermute(low(values[part:]), "fsdp", PAIR))
        return lax.psum_scatter(values, "fsdp", scatter_dimension=0, tiled=True)

    def reduce_weights(values):
        return sum_ctx(own_rows(values), z)

    first_group = reduce_weights(jnp.concatenate([g_up, g_down], axis=1))

    dq, dk, dv = attention_grads(scalars, queries, attended, grad_att, log_sums, keys_all, values_all)
    dproj = low(
        jnp.concatenate([rotate(dq, cos_own, -sin_own), rotate(dk[:rows], cos_own, -sin_own), dv[:rows]], axis=1)
    )
    dproj_seen = low(jnp.concatenate([rotate(dk[rows:], cos_seen, -sin_seen), dv[rows:]], axis=1))
    share = dot(dproj, full_qkv, 1, 1)
    share_seen = dot(dproj_seen, full_qkv[:, local:], 1, 1)
    share_near, share_far = share_seen[:rows], share_seen[rows:]

    def quarter_of(values):
        mine = values[:half] + wide(swap_core(low(values[half:])))
        return mine[:quarter] + wide(swap_y(low(mine[quarter:])))

    far_q = low(quarter_of(share_far))
    near_q = quarter_of(share_near)
    near_in = wide(hop(low(near_q), [(i, i + half_ctx) for i in range(half_ctx)]))
    far_in = wide(hop(far_q, [(1, 2)])) + wide(hop(far_q, [(3, 2)]))
    da_one = quarter_of(share) + far_in + jnp.where(z >= half_ctx, near_q + near_in, 0.0)
    grad_q = low(dmid[:quarter] + norm_grad(da_one, values[:quarter], gain_one))
    grad_half = jnp.concatenate([grad_q, swap_y(grad_q)], axis=0)
    grad_input = wide(unturned(jnp.concatenate([grad_half, swap_core(grad_half)], axis=0)))

    gb_qkv = jnp.sum(wide(dproj), axis=0)
    gb_seen = jnp.sum(wide(dproj_seen), axis=0)
    gb_qkv = gb_qkv + jnp.concatenate([jnp.zeros((local,), jnp.float32), gb_seen])
    g_qkv_seen = dot(normed_seen, dproj_seen, 0, 0)
    g_qkv = dot(normed, dproj, 0, 0) + jnp.concatenate([jnp.zeros((width, local), jnp.float32), g_qkv_seen], axis=1)
    second_group = reduce_weights(jnp.concatenate([g_out, g_qkv], axis=1))

    def gain_grad(weight, grad, bias_grad, gain, shift):
        full = wide(weight)
        by_shift = jnp.sum(full * bias_grad[None, :], axis=1)
        return (jnp.sum(full * grad, axis=1) - shift * by_shift) / gain, by_shift

    g_gain_one, g_shift_one = gain_grad(full_qkv, g_qkv, gb_qkv, gain_one, shift_one)
    g_gain_two, g_shift_two = gain_grad(full_up, g_up, gb_up, gain_two, shift_two)
    over_tp = jnp.stack([gb_out, gb_down, g_gain_one, g_shift_one, g_gain_two, g_shift_two])
    over_tp = over_tp + swap_core(over_tp)
    over_tp = over_tp + swap_y(over_tp)
    if paired:
        keep = lambda v, shape: lax.dynamic_index_in_dim(v.reshape(shape), f, 1, keepdims=False)
        give = lambda v, shape: lax.dynamic_index_in_dim(v.reshape(shape), 1 - f, 1, keepdims=False)
        shape_qkv, shape_up = (gb_qkv.size // HD, 2, HD // 2), (units // HD, 2, HD // 2)
        mine = jnp.concatenate([over_tp[:, :part].reshape(-1), keep(gb_qkv, shape_qkv).reshape(-1), keep(gb_up, shape_up).reshape(-1)])
        other = jnp.concatenate([over_tp[:, part:].reshape(-1), give(gb_qkv, shape_qkv).reshape(-1), give(gb_up, shape_up).reshape(-1)])
        vectors = mine + lax.ppermute(other, "fsdp", PAIR)
    else:
        scattered = (
            lax.psum_scatter(over_tp, "fsdp", scatter_dimension=1, tiled=True),
            lax.psum_scatter(gb_qkv.reshape(-1, HD), "fsdp", scatter_dimension=1, tiled=True),
            lax.psum_scatter(gb_up.reshape(-1, HD), "fsdp", scatter_dimension=1, tiled=True),
        )
        vectors = jnp.concatenate([v.reshape(-1) for v in scattered])
    vectors = vectors + hop(vectors, [(i, i ^ 1) for i in range(4)])
    vectors = vectors + hop(vectors, [(i, i ^ 2) for i in range(4)])
    own = width // members
    named = vectors[: 6 * own].reshape(6, own)
    n_qkv, n_up = b_qkv.size, b_up.size
    out_b_qkv = vectors[6 * own : 6 * own + n_qkv].reshape(b_qkv.shape)
    out_b_up = vectors[6 * own + n_qkv :].reshape(b_up.shape)
    return (
        result[None],
        grad_input[None],
        second_group[:, local:].reshape(w_qkv.shape),
        out_b_qkv,
        second_group[:, :local].T,
        named[0],
        first_group[:, :units],
        out_b_up,
        first_group[:, units:].T,
        named[1],
        named[2],
        named[3],
        named[4],
        named[5],
    )


def solution(mesh):
    rows = P("fsdp", "ctx", None)
    weights = (P("fsdp", None, "tp"), P(None, "tp", "fsdp"), P("tp", "fsdp"), P("fsdp"), P("fsdp", "tp"), P("tp", "fsdp"), P("tp", "fsdp"))
    vectors = (P("fsdp"),) * 5
    return jax.shard_map(
        body,
        mesh=mesh,
        in_specs=(rows, P("fsdp")) + weights + vectors + (rows,),
        out_specs=(rows, rows) + weights + vectors,
        check_vma=False,
    )
```

time: 950 us -> 459 us (0.48)
  waiting for transfers between devices: 560 us -> 115 us
  matrix products: 178 us -> 53.3 us
  starting transfers between devices: 1.25 us -> 71.9 us
  local copies, waits for them, and re-layouts: 27.8 us -> 97.1 us
  blocking collectives: 62.5 us -> 0 us
  Pallas kernels: 0 us -> 42.1 us
  other arithmetic: 94.1 us -> 68.4 us
  between operations: 18.2 us -> 3.73 us
    psum x5 -> x0, waiting for transfers between devices: 332 us -> none  [the longest x1 105 us: body(): lax.psum((g_qkv, g_bqkv, g_out, g_bout, g_up, g_bup, g_down, g_bdown, g_g...]
    reduce_scatter x6 -> x0, waiting for transfers between devices: 178 us -> none  [the longest x1 61.2 us: body(): lax.psum_scatter(grad_values.reshape(total_rows, local_width), 'ctx', sca...]
    dot_general x22 -> x24, matrix products: 173 us -> 53.3 us  [dot(): lax.dot_general(a, b, (((ca,), (cb,)), ((), ())), preferred_element_type=...]
    ppermute x0 -> x47, waiting for transfers between devices: none -> 115 us  [the longest x16 48.6 us: hop(): return lax.ppermute(values, 'ctx', pairs)]
    ppermute x0 -> x47, starting transfers between devices: none -> 71.9 us  [the longest x16 37.7 us: hop(): return lax.ppermute(values, 'ctx', pairs)]
    pallas_call x0 -> x2, Pallas kernels: none -> 42.1 us  [the longest x1 23.5 us: attention_grads(): pl.pallas_call(functools.partial(bwd_kernel, tiles, heads), name='attn_bw...]
    all_gather x10 -> x0, blocking collectives: 40 us -> none  [the longest x1 8.42 us: body(): lax.all_gather(w_qkv, 'fsdp', axis=0, tiled=True)]
    reduce_sum x13 -> x14, other arithmetic: 44 us -> 15.6 us  [the longest x4 4.97 us: row_stats(): mean = jnp.mean(values, axis=-1, keepdims=True)]
  transfers between devices with their start and end apart: 17 -> 47, of which waited for: 15 -> 12; matrix products, arithmetic and copies ran while one was open for 15% -> 40% of each run, Pallas kernels for 0% -> 9%
where the time goes in v1:
time: 459 us; the launch traced here: 452 us
  waiting for transfers between devices  115 us (25%)
  local copies, waits for them, and re-layouts  97.1 us (21%)
  starting transfers between devices  71.9 us (16%)
  other arithmetic  68.4 us (15%)
  matrix products  53.3 us (12%)
  Pallas kernels  42.1 us (9%)
    dot_general x24, matrix products, dot(): lax.dot_general(a, b, (((ca,), (cb,)), ((), ())), preferred_element_type=...  53.3 us
    ppermute x16, waiting for transfers between devices, hop(): return lax.ppermute(values, 'ctx', pairs)  48.6 us
    ppermute x10, waiting for transfers between devices, swap_y(): return lax.ppermute(values, 'tp', [(i, i ^ 2) for i in range(4)])  48 us
    ppermute x16, starting transfers between devices, hop(): return lax.ppermute(values, 'ctx', pairs)  37.7 us
    unnamed x256, local copies, waits for them, and re-layouts  28 us
    pallas_call x1, Pallas kernels, attention_grads(): pl.pallas_call(functools.partial(bwd_kernel, tiles, heads), name='attn_bw...  23.5 us
    pallas_call x1, Pallas kernels, attention(): pl.pallas_call(functools.partial(fwd_kernel, tiles, heads), name='attn_fw...  18.6 us
    ppermute x13, starting transfers between devices, swap_core(): return lax.ppermute(values, 'tp', [(i, i ^ 1) for i in range(4)])  18 us
  transfers between devices with their start and end apart: 47, of which 12 were waited for; matrix products, arithmetic and copies ran while one was open for 40% of the time, Pallas kernels for 9%

profile of v1, /device:TPU:25, one launch (start us, length us, event | category | flops | bytes accessed | tf_op | source)
XLA Modules:
  0.0 451.8 jit_solution(17682912513010290073)
XLA Ops:
  0.7 3.4 reshape_squeeze.6
  4.1 3.4 reshape_squeeze.7
  7.5 7.5 %constant_dynamic-slice_fusion.8 = (bf16[4,256,1,384]{3,2,1,0:T(2,128)(2,1)}, bf16[4,256,1,384]{3,2,1,0:T(2,128)(2,1)}, bf16[4,256,1,384]{3,2,1,0:T(2,128)(2,1)S(1)}, bf16[4,256,1,384]{3,2,1,0:T(2,128)(2,1)S(1)}) fusion(bf16[4,256,2,384]{3,2,1,0:T(2,128)(2,1)S(1)} %reshape_squeeze.7, s32[]{:T(128)S(6)} %select_n.197, s32[]{:T(128)S(6)} %select_n.196, ...), kind=kLoop, calls=%fused_computation.244 | loop fusion | bytes 6291464 | tf_op jit(solution)/shard_map/jit(dynamic_index_in_dim)/dynamic_slice | solution.py:380
  18.3 2.9 collective-permute-start.2
  33.1 2.1 copy.97
  35.2 2.5 copy.122
  41.4 2.0 pad_maximum_fusion.13
  43.4 2.1 collective-permute-start.4
  58.6 3.4 convolution_add_fusion.1
  62.0 6.5 %collective-permute-done.7 = bf16[256,768]{1,0:T(8,128)(2,1)S(1)} collective-permute-done((bf16[256,768]{1,0:T(8,128)(2,1)S(1)}, bf16[256,768]{1,0:T(8,128)(2,1)S(1)}, u32[]{:S(2)}, u32[]{:S(2)}) %collective-permute-start.7) | collective-permute-done | bytes 393248 | tf_op jit(solution)/shard_map/ppermute | solution.py:318
  75.5 2.1 constant_dynamic-update-slice_fusion
  77.5 2.5 convert_reduce_fusion
  81.5 1.7 fusion.5
  83.2 3.3 convolution_add_fusion
  88.1 1.7 copy.92
  92.8 1.7 pad_maximum_fusion.3.v_ref
  94.9 18.6 %attn_fwd.1 = (bf16[1024,192]{1,0:T(8,128)(2,1)S(1)}, f32[4,8,256]{2,1,0:T(8,128)S(1)}) custom-call(s32[4]{0:T(128)S(1)} %pad_add_fusion.2.sc_ref, bf16[1024,192]{1,0:T(8,128)(2,1)S(1)} %copy.95.q_ref, bf16[3072,192]{1,0:T(8,128)(2,1)S(1)} %pad_maximum_fusion.2.k_ref, bf16[3072,192]{1,0:T(8,128)(2,1)S(1)} %pad_maximum_fusion.3.v_ref), custom_call_target="tpu_custom_call" | custom-call | flops 12000000000 | bytes 4000000 | tf_op jit(solution)/shard_map/attn_fwd/pallas_call | solution.py:130
  121.2 1.9 constant_dynamic-update-slice_fusion.8
  123.1 16.0 %collective-permute-done.11 = bf16[512,768]{1,0:T(8,128)(2,1)} collective-permute-done((bf16[512,768]{1,0:T(8,128)(2,1)}, bf16[512,768]{1,0:T(8,128)(2,1)}, u32[]{:S(2)}, u32[]{:S(2)}) %collective-permute-start.11) | collective-permute-done | bytes 786464 | tf_op jit(solution)/shard_map/ppermute | solution.py:318
  140.3 2.1 fusion.91
  144.4 2.0 multiply_convert_fusion.1
  150.0 2.0 multiply_convert_fusion
  152.0 1.7 convolution_convert_fusion.1
  155.2 2.7 convolution_convert_fusion
  158.9 2.7 fusion.6
  167.2 2.8 add_convert_fusion.1
  170.4 3.3 add_convert_fusion.3
  174.4 16.5 %collective-permute-done.42 = bf16[384,1536]{0,1:T(8,128)(2,1)} collective-permute-done((bf16[384,1536]{0,1:T(8,128)(2,1)}, bf16[384,1536]{0,1:T(8,128)(2,1)}, u32[]{:S(2)}, u32[]{:S(2)}) %collective-permute-start.42) | collective-permute-done | bytes 1179680 | tf_op jit(solution)/shard_map/ppermute | solution.py:501
  190.9 3.0 fusion.9
  193.9 3.1 copy.109
  198.4 11.3 %collective-permute-start.43 = (bf16[192,1536]{1,0:T(8,128)(2,1)S(1)}, bf16[192,1536]{1,0:T(8,128)(2,1)S(1)}, u32[]{:S(2)}, u32[]{:S(2)}) collective-permute-start(bf16[192,1536]{1,0:T(8,128)(2,1)S(1)} %fusion.37), channel_id=1, source_target_pairs={{0,4},{4,0},{8,12},{12,8},{1,5},{5,1},{9,13},{13,9},{2,6},{6,2},{1... | collective-permute-start | bytes 1769480 | tf_op jit(solution)/shard_map/ppermute | solution.py:322
  213.1 4.1 convert_reduce_fusion.8
  218.7 3.3 collective-permute-done.43
  222.2 6.7 %collective-permute-start.44 = (bf16[96,1536]{1,0:T(8,128)(2,1)S(1)}, bf16[96,1536]{1,0:T(8,128)(2,1)S(1)}, u32[]{:S(2)}, u32[]{:S(2)}) collective-permute-start(bf16[96,1536]{1,0:T(8,128)(2,1)S(1)} %fusion.57), channel_id=1, source_target_pairs={{0,8},{4,12},{8,0},{12,4},{1,9},{5,13},{9,1},{13,5},{2,10},{6,14},... | collective-permute-start | bytes 884744 | tf_op jit(solution)/shard_map/ppermute | solution.py:322
  230.0 11.5 %collective-permute-done.44 = bf16[96,1536]{1,0:T(8,128)(2,1)S(1)} collective-permute-done((bf16[96,1536]{1,0:T(8,128)(2,1)S(1)}, bf16[96,1536]{1,0:T(8,128)(2,1)S(1)}, u32[]{:S(2)}, u32[]{:S(2)}) %collective-permute-start.44) | collective-permute-done | bytes 294944 | tf_op jit(solution)/shard_map/ppermute | solution.py:322
  241.7 1.8 copy.98
  243.5 1.7 collective-permute-start.17
  246.3 9.5 %collective-permute-done.45 = bf16[96,1536]{1,0:T(8,128)(2,1)} collective-permute-done((bf16[96,1536]{1,0:T(8,128)(2,1)S(1)}, bf16[96,1536]{1,0:T(8,128)(2,1)}, u32[]{:S(2)}, u32[]{:S(2)}) %collective-permute-start.45) | collective-permute-done | bytes 294944 | tf_op jit(solution)/shard_map/ppermute | solution.py:322
  255.9 2.0 maximum_select_fusion.4
  263.0 23.5 %attn_bwd.1 = (f32[1024,192]{1,0:T(8,128)S(1)}, f32[3072,192]{1,0:T(8,128)}, f32[3072,192]{1,0:T(8,128)}) custom-call(s32[4]{0:T(128)S(1)} %pad_add_fusion.2.sc_ref, bf16[1024,192]{1,0:T(8,128)(2,1)S(1)} %copy-done.3, bf16[1024,192]{1,0:T(8,128)(2,1)S(1)} %get-tuple-element.19.o_ref, bf16[1024,192]{1,0:T(8,128)(2,1)S(1)} %pad_maximum_fusion.21.g_ref, ...), custom_call_target="tpu_custom_call" | custom-call | flops 30000001024 | bytes 12000000 | tf_op jit(solution)/shard_map/attn_bwd/pallas_call | solution.py:229
  286.6 3.1 slice.348
  289.7 1.9 copy.105
  293.0 2.3 slice.340
  300.0 2.3 convert_reduce_fusion.1
  302.3 4.7 %fusion.84 = f32[768,384]{0,1:T(8,128)} fusion(bf16[2048,768]{1,0:T(8,128)(2,1)} %copy-done.48, bf16[2048,192]{1,0:T(8,128)(2,1)S(1)} %copy-done.17, bf16[2048,192]{1,0:T(8,128)(2,1)S(1)} %copy.106), kind=kOutput, calls=%fused_computation.307 | convolution fusion | flops 1211105280 | bytes 5898240 | tf_op jit(solution)/shard_map/dot_general | solution.py:277
  318.6 4.0 fusion.11
  322.7 2.6 collective-permute-start.37
  329.4 2.9 collective-permute-start.32
  333.1 6.1 %fusion.101 = (bf16[2048,768]{1,0:T(8,128)(2,1)S(1)}, f32[2048,768]{1,0:T(8,128)}) fusion(bf16[384,576]{0,1:T(8,128)(2,1)} %bitcast.6, bf16[384,576]{0,1:T(8,128)(2,1)} %collective-permute-done.1, bf16[2048,192]{1,0:T(8,128)(2,1)} %slice.427, bf16[2048,192]{1,0:T(8,128)(2,1)} %copy-done.16), kind=kOutput, calls=%fused_computation.320 | convolution fusion | flops 1213857792 | bytes 11894784 | tf_op jit(solution)/shard_map/dot_general | solution.py:277
  344.1 2.0 collective-permute-done.39
  346.9 3.3 maximum_select_fusion
  350.2 5.1 %collective-permute-start.41 = (f32[2976]{0:T(1024)S(1)}, f32[2976]{0:T(1024)S(1)}, u32[]{:S(2)}, u32[]{:S(2)}) collective-permute-start(f32[2976]{0:T(1024)S(1)} %add.459), channel_id=1, source_target_pairs={{0,8},{4,12},{8,0},{12,4},{1,9},{5,13},{9,1},{13,5},{2,10},{6,14},... | collective-permute-start | bytes 35720 | tf_op jit(solution)/shard_map/ppermute | solution.py:322
  355.4 2.7 fusion.83
  358.1 1.7 copy-done.67
  367.8 2.8 slice_add_fusion.1
  375.3 5.8 %collective-permute-done.24 = bf16[256,768]{1,0:T(8,128)(2,1)S(1)} collective-permute-done((bf16[256,768]{1,0:T(8,128)(2,1)S(1)}, bf16[256,768]{1,0:T(8,128)(2,1)S(1)}, u32[]{:S(2)}, u32[]{:S(2)}) %collective-permute-start.24) | collective-permute-done | bytes 393248 | tf_op jit(solution)/shard_map/ppermute | solution.py:318
  381.1 2.0 collective-permute-start.26
  383.2 14.7 %collective-permute-done.28 = bf16[256,768]{1,0:T(8,128)(2,1)S(1)} collective-permute-done((bf16[256,768]{1,0:T(8,128)(2,1)S(1)}, bf16[256,768]{1,0:T(8,128)(2,1)S(1)}, u32[]{:S(2)}, u32[]{:S(2)}) %collective-permute-start.28) | collective-permute-done | bytes 393248 | tf_op jit(solution)/shard_map/ppermute | solution.py:318
  400.3 1.9 maximum_select_fusion.2
  402.2 3.1 collective-permute-start.35
  405.3 23.9 %collective-permute-done.29 = bf16[256,768]{1,0:T(8,128)(2,1)S(1)} collective-permute-done((bf16[256,768]{1,0:T(8,128)(2,1)S(1)}, bf16[256,768]{1,0:T(8,128)(2,1)S(1)}, u32[]{:S(2)}, u32[]{:S(2)}) %collective-permute-start.29) | collective-permute-done | bytes 393248 | tf_op jit(solution)/shard_map/ppermute | solution.py:322
  432.5 5.0 %collective-permute-done.30 = bf16[256,768]{1,0:T(8,128)(2,1)S(1)} collective-permute-done((bf16[256,768]{1,0:T(8,128)(2,1)S(1)}, bf16[256,768]{1,0:T(8,128)(2,1)S(1)}, u32[]{:S(2)}, u32[]{:S(2)}) %collective-permute-start.30) | collective-permute-done | bytes 393248 | tf_op jit(solution)/shard_map/ppermute | solution.py:318
  438.4 4.3 collective-permute-start.31
  449.6 2.0 fusion.26
  (508 shorter events, 135.0 us)
Async XLA Ops:
  15.6 8.9 %copy-start.22 = (bf16[256,768]{1,0:T(8,128)(2,1)}, bf16[256,768]{1,0:T(8,128)(2,1)S(1)}, u32[]{:S(2)}) copy-start(bf16[256,768]{1,0:T(8,128)(2,1)S(1)} %get-tuple-element.134) | copy-start | bytes 1179652
  15.6 98.4 %copy-start.14 = (bf16[256,768]{1,0:T(8,128)(2,1)}, bf16[256,768]{1,0:T(8,128)(2,1)S(1)}, u32[]{:S(2)}) copy-start(bf16[256,768]{1,0:T(8,128)(2,1)S(1)} %get-tuple-element.133) | copy-start | bytes 1179652
  15.6 41.4 %collective-permute-start.6 = (bf16[256,768]{1,0:T(8,128)(2,1)S(1)}, bf16[256,768]{1,0:T(8,128)(2,1)}, u32[]{:S(2)}, u32[]{:S(2)}) collective-permute-start(bf16[256,768]{1,0:T(8,128)(2,1)S(1)} %get-tuple-element.133), channel_id=1, source_target_pairs={{8,12},{9,13},{10,14},{11,15},{24,28},{25,29},{26,30},{27,31}} | collective-permute-start | bytes 1179656 | tf_op jit(solution)/shard_map/ppermute | solution.py:322
  16.9 40.1 %collective-permute-start.5 = (bf16[256,768]{1,0:T(8,128)(2,1)S(1)}, bf16[256,768]{1,0:T(8,128)(2,1)}, u32[]{:S(2)}, u32[]{:S(2)}) collective-permute-start(bf16[256,768]{1,0:T(8,128)(2,1)S(1)} %get-tuple-element.133), channel_id=1, source_target_pairs={{8,4},{9,5},{10,6},{11,7},{24,20},{25,21},{26,22},{27,23}} | collective-permute-start | bytes 1179656 | tf_op jit(solution)/shard_map/ppermute | solution.py:322
  18.3 10.4 %collective-permute-start.2 = (bf16[256,768]{1,0:T(8,128)(2,1)S(1)}, bf16[256,768]{1,0:T(8,128)(2,1)}, u32[]{:S(2)}, u32[]{:S(2)}) collective-permute-start(bf16[256,768]{1,0:T(8,128)(2,1)S(1)} %get-tuple-element.133), channel_id=1, source_target_pairs={{8,0},{12,4},{9,1},{13,5},{10,2},{14,6},{11,3},{15,7},{24,16},{28,... | collective-permute-start | bytes 1179656 | tf_op jit(solution)/shard_map/ppermute | solution.py:322
  22.1 16.7 %collective-permute-start = (bf16[2976]{0:T(1024)(128)(2,1)}, bf16[2976]{0:T(1024)(128)(2,1)S(1)}, u32[]{:S(2)}, u32[]{:S(2)}) collective-permute-start(bf16[2976]{0:T(1024)(128)(2,1)} %concatenate.292), channel_id=1, source_target_pairs={{0,16},{16,0},{1,17},{17,1},{2,18},{18,2},{3,19},{19,3},{4,20},{20... | collective-permute-start | bytes 17864 | tf_op jit(solution)/shard_map/ppermute | solution.py:398
  23.3 28.2 %collective-permute-start.9 = (bf16[192,384]{1,0:T(8,128)(2,1)}, bf16[192,384]{1,0:T(8,128)(2,1)}, u32[]{:S(2)}, u32[]{:S(2)}) collective-permute-start(bf16[192,384]{1,0:T(8,128)(2,1)} %param.19), channel_id=1, source_target_pairs={{0,16},{16,0},{1,17},{17,1},{2,18},{18,2},{3,19},{19,3},{4,20},{20... | collective-permute-start | bytes 442376 | tf_op jit(solution)/shard_map/ppermute | solution.py:391
  29.6 11.8 %collective-permute-start.3 = (bf16[256,768]{1,0:T(8,128)(2,1)}, bf16[256,768]{1,0:T(8,128)(2,1)}, u32[]{:S(2)}, u32[]{:S(2)}) collective-permute-start(bf16[256,768]{1,0:T(8,128)(2,1)} %get-tuple-element.101), channel_id=1, source_target_pairs={{0,2},{1,3},{2,0},{3,1},{4,6},{5,7},{6,4},{7,5},{8,10},{9,11},{10,... | collective-permute-start | bytes 1179656 | tf_op jit(solution)/shard_map/ppermute | solution.py:318
  38.8 19.7 %collective-permute-start.1 = (bf16[384,576]{0,1:T(8,128)(2,1)}, bf16[384,576]{0,1:T(8,128)(2,1)}, u32[]{:S(2)}, u32[]{:S(2)}) collective-permute-start(bf16[384,576]{0,1:T(8,128)(2,1)} %bitcast.6), channel_id=1, source_target_pairs={{0,16},{16,0},{1,17},{17,1},{2,18},{18,2},{3,19},{19,3},{4,20},{20... | collective-permute-start | bytes 1327112 | tf_op jit(solution)/shard_map/ppermute | solution.py:391
  43.4 11.1 %collective-permute-start.4 = (bf16[512,768]{1,0:T(8,128)(2,1)}, bf16[512,768]{1,0:T(8,128)(2,1)}, u32[]{:S(2)}, u32[]{:S(2)}) collective-permute-start(bf16[512,768]{1,0:T(8,128)(2,1)} %pad_maximum_fusion.13), channel_id=1, source_target_pairs={{0,1},{1,0},{2,3},{3,2},{4,5},{5,4},{6,7},{7,6},{8,9},{9,8},{10,11... | collective-permute-start | bytes 2359304 | tf_op jit(solution)/shard_map/ppermute | solution.py:314
  51.5 92.8 %collective-permute-start.12 = (bf16[384,768]{0,1:T(8,128)(2,1)}, bf16[384,768]{0,1:T(8,128)(2,1)}, u32[]{:S(2)}, u32[]{:S(2)}) collective-permute-start(bf16[384,768]{0,1:T(8,128)(2,1)} %copy.97), channel_id=1, source_target_pairs={{0,16},{16,0},{1,17},{17,1},{2,18},{18,2},{3,19},{19,3},{4,20},{20... | collective-permute-start | bytes 1769480 | tf_op jit(solution)/shard_map/ppermute | solution.py:391
  54.5 66.7 %collective-permute-start.13 = (bf16[768,384]{1,0:T(8,128)(2,1)}, bf16[768,384]{1,0:T(8,128)(2,1)}, u32[]{:S(2)}, u32[]{:S(2)}) collective-permute-start(bf16[768,384]{1,0:T(8,128)(2,1)} %param.23), channel_id=1, source_target_pairs={{0,16},{16,0},{1,17},{17,1},{2,18},{18,2},{3,19},{19,3},{4,20},{20... | collective-permute-start | bytes 1769480 | tf_op jit(solution)/shard_map/ppermute | solution.py:391
  58.2 10.3 %collective-permute-start.7 = (bf16[256,768]{1,0:T(8,128)(2,1)S(1)}, bf16[256,768]{1,0:T(8,128)(2,1)S(1)}, u32[]{:S(2)}, u32[]{:S(2)}) collective-permute-start(bf16[256,768]{1,0:T(8,128)(2,1)S(1)} %get-tuple-element.99), channel_id=1, source_target_pairs={{0,2},{1,3},{2,0},{3,1},{4,6},{5,7},{6,4},{7,5},{8,10},{9,11},{10,... | collective-permute-start | bytes 1179656 | tf_op jit(solution)/shard_map/ppermute | solution.py:318
  69.5 6.0 %collective-permute-start.8 = (bf16[512,768]{1,0:T(8,128)(2,1)}, bf16[512,768]{1,0:T(8,128)(2,1)}, u32[]{:S(2)}, u32[]{:S(2)}) collective-permute-start(bf16[512,768]{1,0:T(8,128)(2,1)} %pad_maximum_fusion.14), channel_id=1, source_target_pairs={{0,1},{1,0},{2,3},{3,2},{4,5},{5,4},{6,7},{7,6},{8,9},{9,8},{10,11... | collective-permute-start | bytes 2359304 | tf_op jit(solution)/shard_map/ppermute | solution.py:314
  74.5 20.3 %copy-start.2 = (bf16[1024,192]{1,0:T(8,128)(2,1)}, bf16[1024,192]{1,0:T(8,128)(2,1)S(1)}, u32[]{:S(2)}) copy-start(bf16[1024,192]{1,0:T(8,128)(2,1)S(1)} %copy.95.q_ref) | copy-start | bytes 1179652
  94.9 18.6 %copy-start = (bf16[3072,192]{1,0:T(8,128)(2,1)}, bf16[3072,192]{1,0:T(8,128)(2,1)S(1)}, u32[]{:S(2)}) copy-start(bf16[3072,192]{1,0:T(8,128)(2,1)S(1)} %pad_maximum_fusion.2.k_ref) | copy-start | bytes 3538948
  94.9 18.6 %copy-start.33 = (bf16[192,768]{1,0:T(8,128)(2,1)S(1)}, bf16[192,768]{1,0:T(8,128)(2,1)}, u32[]{:S(2)}) copy-start(bf16[192,768]{1,0:T(8,128)(2,1)} %constant_dynamic-update-slice_fusion.6) | copy-start | bytes 884740
  113.9 4.6 %collective-permute-start.10 = (bf16[512,768]{1,0:T(8,128)(2,1)S(1)}, bf16[512,768]{1,0:T(8,128)(2,1)S(1)}, u32[]{:S(2)}, u32[]{:S(2)}) collective-permute-start(bf16[512,768]{1,0:T(8,128)(2,1)S(1)} %convolution_convert_fusion.2), channel_id=1, source_target_pairs={{0,1},{1,0},{2,3},{3,2},{4,5},{5,4},{6,7},{7,6},{8,9},{9,8},{10,11... | collective-permute-start | bytes 2359304 | tf_op jit(solution)/shard_map/ppermute | solution.py:314
  118.4 29.0 %copy-start.40 = (bf16[256,768]{1,0:T(8,128)(2,1)}, bf16[256,768]{1,0:T(8,128)(2,1)S(1)}, u32[]{:S(2)}) copy-start(bf16[256,768]{1,0:T(8,128)(2,1)S(1)} %get-tuple-element.122) | copy-start | bytes 1179652
  119.7 19.4 %collective-permute-start.11 = (bf16[512,768]{1,0:T(8,128)(2,1)}, bf16[512,768]{1,0:T(8,128)(2,1)}, u32[]{:S(2)}, u32[]{:S(2)}) collective-permute-start(bf16[512,768]{1,0:T(8,128)(2,1)} %add_convert_fusion.5), channel_id=1, source_target_pairs={{0,2},{1,3},{2,0},{3,1},{4,6},{5,7},{6,4},{7,5},{8,10},{9,11},{10,... | collective-permute-start | bytes 2359304 | tf_op jit(solution)/shard_map/ppermute | solution.py:318
  143.5 6.4 %collective-permute-start.14 = (bf16[512,768]{1,0:T(8,128)(2,1)S(1)}, bf16[512,768]{1,0:T(8,128)(2,1)S(1)}, u32[]{:S(2)}, u32[]{:S(2)}) collective-permute-start(bf16[512,768]{1,0:T(8,128)(2,1)S(1)} %add_convert_fusion.4), channel_id=1, source_target_pairs={{0,1},{1,0},{2,3},{3,2},{4,5},{5,4},{6,7},{7,6},{8,9},{9,8},{10,11... | collective-permute-start | bytes 2359304 | tf_op jit(solution)/shard_map/ppermute | solution.py:314
  153.6 16.7 %collective-permute-start.15 = (bf16[512,768]{1,0:T(8,128)(2,1)}, bf16[512,768]{1,0:T(8,128)(2,1)}, u32[]{:S(2)}, u32[]{:S(2)}) collective-permute-start(bf16[512,768]{1,0:T(8,128)(2,1)} %convolution_convert_fusion.1), channel_id=1, source_target_pairs={{0,1},{1,0},{2,3},{3,2},{4,5},{5,4},{6,7},{7,6},{8,9},{9,8},{10,11... | collective-permute-start | bytes 2359304 | tf_op jit(solution)/shard_map/ppermute | solution.py:314
  158.0 9.2 %collective-permute-start.18 = (bf16[512,768]{1,0:T(8,128)(2,1)}, bf16[512,768]{1,0:T(8,128)(2,1)}, u32[]{:S(2)}, u32[]{:S(2)}) collective-permute-start(bf16[512,768]{1,0:T(8,128)(2,1)} %convolution_convert_fusion), channel_id=1, source_target_pairs={{0,1},{1,0},{2,3},{3,2},{4,5},{5,4},{6,7},{7,6},{8,9},{9,8},{10,11... | collective-permute-start | bytes 2359304 | tf_op jit(solution)/shard_map/ppermute | solution.py:314
  163.5 27.4 %collective-permute-start.42 = (bf16[384,1536]{0,1:T(8,128)(2,1)}, bf16[384,1536]{0,1:T(8,128)(2,1)}, u32[]{:S(2)}, u32[]{:S(2)}) collective-permute-start(bf16[384,1536]{0,1:T(8,128)(2,1)} %fusion.10), channel_id=1, source_target_pairs={{0,16},{16,0},{1,17},{17,1},{2,18},{18,2},{3,19},{19,3},{4,20},{20... | collective-permute-start | bytes 3538952 | tf_op jit(solution)/shard_map/ppermute | solution.py:501
  167.2 23.7 %copy-start.11 = (f32[768,768]{0,1:T(8,128)S(1)}, f32[768,768]{0,1:T(8,128)}, u32[]{:S(2)}) copy-start(f32[768,768]{0,1:T(8,128)} %copy-done.10) | copy-start | bytes 7077892
  170.0 40.8 %copy-start.51 = (bf16[512,768]{1,0:T(8,128)(2,1)}, bf16[512,768]{1,0:T(8,128)(2,1)S(1)}, u32[]{:S(2)}) copy-start(bf16[512,768]{1,0:T(8,128)(2,1)S(1)} %add_convert_fusion.1) | copy-start | bytes 2359300
  170.0 20.8 %copy-start.9 = (f32[768,768]{0,1:T(8,128)S(1)}, f32[768,768]{0,1:T(8,128)}, u32[]{:S(2)}) copy-start(f32[768,768]{0,1:T(8,128)} %copy-done.8) | copy-start | bytes 7077892
  170.0 39.6 %collective-permute-start.19 = (bf16[512,768]{1,0:T(8,128)(2,1)S(1)}, bf16[512,768]{1,0:T(8,128)(2,1)}, u32[]{:S(2)}, u32[]{:S(2)}) collective-permute-start(bf16[512,768]{1,0:T(8,128)(2,1)S(1)} %add_convert_fusion.1), channel_id=1, source_target_pairs={{0,2},{1,3},{2,0},{3,1},{4,6},{5,7},{6,4},{7,5},{8,10},{9,11},{10,... | collective-permute-start | bytes 2359304 | tf_op jit(solution)/shard_map/ppermute | solution.py:318
  173.6 38.0 %collective-permute-start.16 = (bf16[512,768]{1,0:T(8,128)(2,1)}, bf16[512,768]{1,0:T(8,128)(2,1)}, u32[]{:S(2)}, u32[]{:S(2)}) collective-permute-start(bf16[512,768]{1,0:T(8,128)(2,1)} %add_convert_fusion.3), channel_id=1, source_target_pairs={{0,2},{1,3},{2,0},{3,1},{4,6},{5,7},{6,4},{7,5},{8,10},{9,11},{10,... | collective-permute-start | bytes 2359304 | tf_op jit(solution)/shard_map/ppermute | solution.py:318
  197.0 13.9 %copy-start.5 = (f32[512,768]{1,0:T(8,128)S(1)}, f32[512,768]{1,0:T(8,128)}, u32[]{:S(2)}) copy-start(f32[512,768]{1,0:T(8,128)} %copy-done.4) | copy-start | bytes 4718596
  198.4 23.6 %collective-permute-start.43 = (bf16[192,1536]{1,0:T(8,128)(2,1)S(1)}, bf16[192,1536]{1,0:T(8,128)(2,1)S(1)}, u32[]{:S(2)}, u32[]{:S(2)}) collective-permute-start(bf16[192,1536]{1,0:T(8,128)(2,1)S(1)} %fusion.37), channel_id=1, source_target_pairs={{0,4},{4,0},{8,12},{12,8},{1,5},{5,1},{9,13},{13,9},{2,6},{6,2},{1... | collective-permute-start | bytes 1769480 | tf_op jit(solution)/shard_map/ppermute | solution.py:322
  213.0 9.0 %copy-start.18 = (f32[384,1536]{1,0:T(8,128)S(1)}, f32[384,1536]{1,0:T(8,128)}, u32[]{:S(2)}) copy-start(f32[384,1536]{1,0:T(8,128)} %copy.109) | copy-start | bytes 7077892
  217.1 11.8 %copy-start.34 = (bf16[192,768]{1,0:T(8,128)(2,1)S(1)}, bf16[192,768]{1,0:T(8,128)(2,1)}, u32[]{:S(2)}) copy-start(bf16[192,768]{1,0:T(8,128)(2,1)} %constant_dynamic-update-slice_fusion.6) | copy-start | bytes 884740
  217.1 40.7 %collective-permute-start.20 = (bf16[512,768]{1,0:T(8,128)(2,1)S(1)}, bf16[512,768]{1,0:T(8,128)(2,1)}, u32[]{:S(2)}, u32[]{:S(2)}) collective-permute-start(bf16[512,768]{1,0:T(8,128)(2,1)S(1)} %get-tuple-element.93), channel_id=1, source_target_pairs={{0,1},{1,0},{2,3},{3,2},{4,5},{5,4},{6,7},{7,6},{8,9},{9,8},{10,11... | collective-permute-start | bytes 2359304 | tf_op jit(solution)/shard_map/ppermute | solution.py:314
  222.2 19.3 %collective-permute-start.44 = (bf16[96,1536]{1,0:T(8,128)(2,1)S(1)}, bf16[96,1536]{1,0:T(8,128)(2,1)S(1)}, u32[]{:S(2)}, u32[]{:S(2)}) collective-permute-start(bf16[96,1536]{1,0:T(8,128)(2,1)S(1)} %fusion.57), channel_id=1, source_target_pairs={{0,8},{4,12},{8,0},{12,4},{1,9},{5,13},{9,1},{13,5},{2,10},{6,14},... | collective-permute-start | bytes 884744 | tf_op jit(solution)/shard_map/ppermute | solution.py:322
  241.6 14.3 %collective-permute-start.45 = (bf16[96,1536]{1,0:T(8,128)(2,1)S(1)}, bf16[96,1536]{1,0:T(8,128)(2,1)}, u32[]{:S(2)}, u32[]{:S(2)}) collective-permute-start(bf16[96,1536]{1,0:T(8,128)(2,1)S(1)} %fusion.38), channel_id=1, source_target_pairs={{0,8},{4,12},{8,0},{12,4},{1,9},{5,13},{9,1},{13,5},{2,10},{6,14},... | collective-permute-start | bytes 884744 | tf_op jit(solution)/shard_map/ppermute | solution.py:322
  243.5 63.5 %collective-permute-start.17 = (bf16[512,768]{1,0:T(8,128)(2,1)}, bf16[512,768]{1,0:T(8,128)(2,1)}, u32[]{:S(2)}, u32[]{:S(2)}) collective-permute-start(bf16[512,768]{1,0:T(8,128)(2,1)} %get-tuple-element.120), channel_id=1, source_target_pairs={{0,1},{1,0},{2,3},{3,2},{4,5},{5,4},{6,7},{7,6},{8,9},{9,8},{10,11... | collective-permute-start | bytes 2359304 | tf_op jit(solution)/shard_map/ppermute | solution.py:314
  257.8 140.9 %collective-permute-start.46 = (bf16[192,1536]{1,0:T(8,128)(2,1)}, bf16[192,1536]{1,0:T(8,128)(2,1)}, u32[]{:S(2)}, u32[]{:S(2)}) collective-permute-start(bf16[192,1536]{1,0:T(8,128)(2,1)} %bitcast.63), channel_id=1, source_target_pairs={{0,4},{4,0},{8,12},{12,8},{1,5},{5,1},{9,13},{13,9},{2,6},{6,2},{1... | collective-permute-start | bytes 1769480 | tf_op jit(solution)/shard_map/ppermute | solution.py:322
  322.7 9.6 %collective-permute-start.37 = (f32[6,768]{1,0:T(8,128)S(1)}, f32[6,768]{1,0:T(8,128)S(1)}, u32[]{:S(2)}, u32[]{:S(2)}) collective-permute-start(f32[6,768]{1,0:T(8,128)S(1)} %stack.76), channel_id=1, source_target_pairs={{0,1},{1,0},{2,3},{3,2},{4,5},{5,4},{6,7},{7,6},{8,9},{9,8},{10,11... | collective-permute-start | bytes 55304 | tf_op jit(solution)/shard_map/ppermute | solution.py:314
  329.4 34.9 %collective-permute-start.32 = (bf16[384,768]{0,1:T(8,128)(2,1)}, bf16[384,768]{0,1:T(8,128)(2,1)}, u32[]{:S(2)}, u32[]{:S(2)}) collective-permute-start(bf16[384,768]{0,1:T(8,128)(2,1)} %fusion.30), channel_id=1, source_target_pairs={{0,16},{16,0},{1,17},{17,1},{2,18},{18,2},{3,19},{19,3},{4,20},{20... | collective-permute-start | bytes 1769480 | tf_op jit(solution)/shard_map/ppermute | solution.py:501
  332.3 7.0 %collective-permute-start.38 = (f32[6,768]{1,0:T(8,128)S(1)}, f32[6,768]{1,0:T(8,128)S(1)}, u32[]{:S(2)}, u32[]{:S(2)}) collective-permute-start(f32[6,768]{1,0:T(8,128)S(1)} %add.455), channel_id=1, source_target_pairs={{0,2},{1,3},{2,0},{3,1},{4,6},{5,7},{6,4},{7,5},{8,10},{9,11},{10,... | collective-permute-start | bytes 55304 | tf_op jit(solution)/shard_map/ppermute | solution.py:318
  340.0 6.1 %collective-permute-start.39 = (f32[2976]{0:T(1024)}, f32[2976]{0:T(1024)}, u32[]{:S(2)}, u32[]{:S(2)}) collective-permute-start(f32[2976]{0:T(1024)} %concatenate.358), channel_id=1, source_target_pairs={{0,16},{16,0},{1,17},{17,1},{2,18},{18,2},{3,19},{19,3},{4,20},{20... | collective-permute-start | bytes 35720 | tf_op jit(solution)/shard_map/ppermute | solution.py:554
  342.0 25.8 %collective-permute-start.23 = (bf16[512,768]{1,0:T(8,128)(2,1)}, bf16[512,768]{1,0:T(8,128)(2,1)}, u32[]{:S(2)}, u32[]{:S(2)}) collective-permute-start(bf16[512,768]{1,0:T(8,128)(2,1)} %get-tuple-element.104), channel_id=1, source_target_pairs={{0,1},{1,0},{2,3},{3,2},{4,5},{5,4},{6,7},{7,6},{8,9},{9,8},{10,11... | collective-permute-start | bytes 2359304 | tf_op jit(solution)/shard_map/ppermute | solution.py:314
  343.3 24.4 %collective-permute-start.27 = (bf16[512,768]{1,0:T(8,128)(2,1)}, bf16[512,768]{1,0:T(8,128)(2,1)}, u32[]{:S(2)}, u32[]{:S(2)}) collective-permute-start(bf16[512,768]{1,0:T(8,128)(2,1)} %get-tuple-element.105), channel_id=1, source_target_pairs={{0,1},{1,0},{2,3},{3,2},{4,5},{5,4},{6,7},{7,6},{8,9},{9,8},{10,11... | collective-permute-start | bytes 2359304 | tf_op jit(solution)/shard_map/ppermute | solution.py:314
  346.8 3.4 collective-permute-start.40
  350.2 10.6 %collective-permute-start.41 = (f32[2976]{0:T(1024)S(1)}, f32[2976]{0:T(1024)S(1)}, u32[]{:S(2)}, u32[]{:S(2)}) collective-permute-start(f32[2976]{0:T(1024)S(1)} %add.459), channel_id=1, source_target_pairs={{0,8},{4,12},{8,0},{12,4},{1,9},{5,13},{9,1},{13,5},{2,10},{6,14},... | collective-permute-start | bytes 35720 | tf_op jit(solution)/shard_map/ppermute | solution.py:322
  355.3 9.0 %copy-start.20 = (f32[768,576]{0,1:T(8,128)S(1)}, f32[768,576]{0,1:T(8,128)}, u32[]{:S(2)}) copy-start(f32[768,576]{0,1:T(8,128)} %copy-done.19) | copy-start | bytes 5308420
  360.8 11.3 %collective-permute-start.21 = (bf16[512,768]{1,0:T(8,128)(2,1)}, bf16[512,768]{1,0:T(8,128)(2,1)}, u32[]{:S(2)}, u32[]{:S(2)}) collective-permute-start(bf16[512,768]{1,0:T(8,128)(2,1)} %slice.567), channel_id=1, source_target_pairs={{0,1},{1,0},{2,3},{3,2},{4,5},{5,4},{6,7},{7,6},{8,9},{9,8},{10,11... | collective-permute-start | bytes 2359304 | tf_op jit(solution)/shard_map/ppermute | solution.py:314
  366.2 8.9 %collective-permute-start.33 = (bf16[192,768]{1,0:T(8,128)(2,1)S(1)}, bf16[192,768]{1,0:T(8,128)(2,1)S(1)}, u32[]{:S(2)}, u32[]{:S(2)}) collective-permute-start(bf16[192,768]{1,0:T(8,128)(2,1)S(1)} %fusion.56), channel_id=1, source_target_pairs={{0,4},{4,0},{8,12},{12,8},{1,5},{5,1},{9,13},{13,9},{2,6},{6,2},{1... | collective-permute-start | bytes 884744 | tf_op jit(solution)/shard_map/ppermute | solution.py:322
  370.6 10.5 %collective-permute-start.24 = (bf16[256,768]{1,0:T(8,128)(2,1)S(1)}, bf16[256,768]{1,0:T(8,128)(2,1)S(1)}, u32[]{:S(2)}, u32[]{:S(2)}) collective-permute-start(bf16[256,768]{1,0:T(8,128)(2,1)S(1)} %slice.570), channel_id=1, source_target_pairs={{0,2},{1,3},{2,0},{3,1},{4,6},{5,7},{6,4},{7,5},{8,10},{9,11},{10,... | collective-permute-start | bytes 1179656 | tf_op jit(solution)/shard_map/ppermute | solution.py:318
  373.5 31.8 %collective-permute-start.22 = (bf16[256,768]{1,0:T(8,128)(2,1)S(1)}, bf16[256,768]{1,0:T(8,128)(2,1)S(1)}, u32[]{:S(2)}, u32[]{:S(2)}) collective-permute-start(bf16[256,768]{1,0:T(8,128)(2,1)S(1)} %slice.571), channel_id=1, source_target_pairs={{0,2},{1,3},{2,0},{3,1},{4,6},{5,7},{6,4},{7,5},{8,10},{9,11},{10,... | collective-permute-start | bytes 1179656 | tf_op jit(solution)/shard_map/ppermute | solution.py:318
  374.0 23.9 %collective-permute-start.28 = (bf16[256,768]{1,0:T(8,128)(2,1)S(1)}, bf16[256,768]{1,0:T(8,128)(2,1)S(1)}, u32[]{:S(2)}, u32[]{:S(2)}) collective-permute-start(bf16[256,768]{1,0:T(8,128)(2,1)S(1)} %slice.569), channel_id=1, source_target_pairs={{0,2},{1,3},{2,0},{3,1},{4,6},{5,7},{6,4},{7,5},{8,10},{9,11},{10,... | collective-permute-start | bytes 1179656 | tf_op jit(solution)/shard_map/ppermute | solution.py:318
  375.2 27.0 %collective-permute-start.34 = (bf16[96,768]{1,0:T(8,128)(2,1)S(1)}, bf16[96,768]{1,0:T(8,128)(2,1)S(1)}, u32[]{:S(2)}, u32[]{:S(2)}) collective-permute-start(bf16[96,768]{1,0:T(8,128)(2,1)S(1)} %fusion.64), channel_id=1, source_target_pairs={{0,8},{4,12},{8,0},{12,4},{1,9},{5,13},{9,1},{13,5},{2,10},{6,14},... | collective-permute-start | bytes 442376 | tf_op jit(solution)/shard_map/ppermute | solution.py:322
  381.1 48.1 %collective-permute-start.26 = (bf16[256,768]{1,0:T(8,128)(2,1)S(1)}, bf16[256,768]{1,0:T(8,128)(2,1)S(1)}, u32[]{:S(2)}, u32[]{:S(2)}) collective-permute-start(bf16[256,768]{1,0:T(8,128)(2,1)S(1)} %fusion.31), channel_id=1, source_target_pairs={{12,8},{13,9},{14,10},{15,11},{28,24},{29,25},{30,26},{31,27}} | collective-permute-start | bytes 1179656 | tf_op jit(solution)/shard_map/ppermute | solution.py:322
  397.9 31.3 %collective-permute-start.25 = (bf16[256,768]{1,0:T(8,128)(2,1)S(1)}, bf16[256,768]{1,0:T(8,128)(2,1)S(1)}, u32[]{:S(2)}, u32[]{:S(2)}) collective-permute-start(bf16[256,768]{1,0:T(8,128)(2,1)S(1)} %fusion.31), channel_id=1, source_target_pairs={{4,8},{5,9},{6,10},{7,11},{20,24},{21,25},{22,26},{23,27}} | collective-permute-start | bytes 1179656 | tf_op jit(solution)/shard_map/ppermute | solution.py:322
  398.6 30.6 %copy-start.13 = (f32[1024,768]{1,0:T(8,128)S(1)}, f32[1024,768]{1,0:T(8,128)}, u32[]{:S(2)}) copy-start(f32[1024,768]{1,0:T(8,128)} %copy-done.12) | copy-start | bytes 9437188
  398.7 30.5 %copy-start.93 = (f32[256]{0:T(256)S(1)}, f32[256]{0:T(256)}, u32[]{:S(2)}) copy-start(f32[256]{0:T(256)} %copy-done.92) | copy-start | bytes 3076
  398.7 30.5 %copy-start.110 = (f32[256]{0:T(256)S(1)}, f32[256]{0:T(256)}, u32[]{:S(2)}) copy-start(f32[256]{0:T(256)} %add_rsqrt_fusion.3) | copy-start | bytes 3076
  398.7 30.5 %collective-permute-start.29 = (bf16[256,768]{1,0:T(8,128)(2,1)S(1)}, bf16[256,768]{1,0:T(8,128)(2,1)S(1)}, u32[]{:S(2)}, u32[]{:S(2)}) collective-permute-start(bf16[256,768]{1,0:T(8,128)(2,1)S(1)} %fusion.39), channel_id=1, source_target_pairs={{0,8},{4,12},{1,9},{5,13},{2,10},{6,14},{3,11},{7,15},{16,24},{20,... | collective-permute-start | bytes 1179656 | tf_op jit(solution)/shard_map/ppermute | solution.py:322
  402.2 27.7 %copy-start.39 = (f32[512,768]{1,0:T(8,128)S(1)}, f32[512,768]{1,0:T(8,128)}, u32[]{:S(2)}) copy-start(f32[512,768]{1,0:T(8,128)} %get-tuple-element.94) | copy-start | bytes 4718596
  402.2 30.1 %collective-permute-start.35 = (bf16[96,768]{1,0:T(8,128)(2,1)S(1)}, bf16[96,768]{1,0:T(8,128)(2,1)S(1)}, u32[]{:S(2)}, u32[]{:S(2)}) collective-permute-start(bf16[96,768]{1,0:T(8,128)(2,1)S(1)} %fusion.58), channel_id=1, source_target_pairs={{0,8},{4,12},{8,0},{12,4},{1,9},{5,13},{9,1},{13,5},{2,10},{6,14},... | collective-permute-start | bytes 442376 | tf_op jit(solution)/shard_map/ppermute | solution.py:322
  430.2 7.3 %collective-permute-start.30 = (bf16[256,768]{1,0:T(8,128)(2,1)S(1)}, bf16[256,768]{1,0:T(8,128)(2,1)S(1)}, u32[]{:S(2)}, u32[]{:S(2)}) collective-permute-start(bf16[256,768]{1,0:T(8,128)(2,1)S(1)} %fusion.35), channel_id=1, source_target_pairs={{0,2},{1,3},{2,0},{3,1},{4,6},{5,7},{6,4},{7,5},{8,10},{9,11},{10,... | collective-permute-start | bytes 1179656 | tf_op jit(solution)/shard_map/ppermute | solution.py:318
  432.4 12.9 %collective-permute-start.36 = (bf16[192,768]{1,0:T(8,128)(2,1)S(1)}, bf16[192,768]{1,0:T(8,128)(2,1)S(1)}, u32[]{:S(2)}, u32[]{:S(2)}) collective-permute-start(bf16[192,768]{1,0:T(8,128)(2,1)S(1)} %bitcast.170), channel_id=1, source_target_pairs={{0,4},{4,0},{8,12},{12,8},{1,5},{5,1},{9,13},{13,9},{2,6},{6,2},{1... | collective-permute-start | bytes 884744 | tf_op jit(solution)/shard_map/ppermute | solution.py:322
  438.4 9.6 %collective-permute-start.31 = (bf16[512,768]{1,0:T(8,128)(2,1)}, bf16[512,768]{1,0:T(8,128)(2,1)}, u32[]{:S(2)}, u32[]{:S(2)}) collective-permute-start(bf16[512,768]{1,0:T(8,128)(2,1)} %pad_maximum_fusion.20), channel_id=1, source_target_pairs={{0,1},{1,0},{2,3},{3,2},{4,5},{5,4},{6,7},{7,6},{8,9},{9,8},{10,11... | collective-permute-start | bytes 2359304 | tf_op jit(solution)/shard_map/ppermute | solution.py:314
  (105 other events, 333.3 us)

commit v2 on v1

v2 whole, which is shorter than its diff:
```python
import functools
import jax
import jax.numpy as jnp
from jax import lax
from jax.experimental import pallas as pl
from jax.experimental.pallas import tpu as pltpu
from jax.sharding import PartitionSpec as P

HD = 64
BLOCK = 16
TILE = 256
WIDE = 512
LOG2E = 1.4426950408889634
NEG = -1e30
epsilon = 1e-05
BF, F32 = jnp.bfloat16, jnp.float32


def low(values):
    return values.astype(BF)


def wide(values):
    return values.astype(F32)


def dot(a, b, ca=1, cb=0):
    return lax.dot_general(a, b, (((ca,), (cb,)), ((), ())), preferred_element_type=F32)


def shape(dims, kind):
    return jax.ShapeDtypeStruct(dims, kind)


def call(kernel, name, scalars, grid, ins, outs, scratch, args, flops, moved, room=24):
    return pl.pallas_call(
        kernel,
        name=name,
        out_shape=[s for s, _ in outs],
        grid_spec=pltpu.PrefetchScalarGridSpec(
            num_scalar_prefetch=1, grid=grid, in_specs=ins, out_specs=[b for _, b in outs], scratch_shapes=scratch
        ),
        compiler_params=pltpu.CompilerParams(dimension_semantics=("arbitrary",) * len(grid), vmem_limit_bytes=room << 20),
        cost_estimate=pl.CostEstimate(flops=flops, bytes_accessed=moved, transcendentals=0),
    )(scalars, *args)


def whole(values):
    dims = values.shape
    return pl.BlockSpec(dims, lambda i, sc: (0,) * len(dims))


def row_block(values, index):
    return pl.BlockSpec((TILE, values.shape[1]), lambda i, sc: (index(i, sc), 0))


def turn_matrix(width):
    k = lax.broadcasted_iota(jnp.int32, (width, width), 0)
    n = lax.broadcasted_iota(jnp.int32, (width, width), 1)
    first = (n & (HD - 1)) < HD // 2
    return jnp.where(first & (k == n + HD // 2), -1.0, jnp.where((~first) & (k == n - HD // 2), 1.0, 0.0)).astype(BF)


def tile_angles(base_ref, tile_ref, index):
    cos, sin = base_ref[0], base_ref[1]
    cos_t, sin_t = tile_ref[0, pl.ds(index, 1), :], tile_ref[1, pl.ds(index, 1), :]
    return cos * cos_t - sin * sin_t, sin * cos_t + cos * sin_t


def unit_rows(x):
    mean = jnp.mean(x, axis=-1, keepdims=True)
    centered = x - mean
    variance = jnp.mean(centered * centered, axis=-1, keepdims=True)
    scale = lax.rsqrt(variance + epsilon)
    return centered * scale, scale


def project_kernel(parts, with_q, far, tiles, sc_ref, *refs):
    refs = list(refs)
    xs = [refs.pop(0) for _ in range(parts)]
    dy_ref = refs.pop(0) if with_q else None
    vec_ref, wa_ref, wb_ref, bias_ref, base_ref, tile_ref = [refs.pop(0) for _ in range(6)]
    outs = [refs.pop(0) for _ in range(3 if with_q else 2)]
    norm_ref = refs.pop(0)
    if with_q:
        keep_ref, dy_out = refs.pop(0), refs.pop(0)
    w_s, r_s, b_s, x_s, a_s = refs
    j = pl.program_id(0)
    f = sc_ref[5]
    local = outs[0].shape[1]
    part = wa_ref.shape[0]
    skip = 0 if with_q else 1
    count = len(outs)

    @pl.when(j == 0)
    def _():
        turn = turn_matrix(local)
        for n in range(count):
            cols = slice((n + skip) * local, (n + skip + 1) * local)
            w_s[n, :part] = wa_ref[:, cols]
            w_s[n, part:] = wb_ref[:, cols]
            if n < count - 1:
                r_s[n] = low(dot(w_s[n], turn))
                b_s[n] = dot(jnp.broadcast_to(bias_ref[:, cols], (8, local)).astype(BF), turn)

    if parts == 1:
        x = wide(xs[0][...])
    else:
        for n in range(parts):

            @pl.when(j == n)
            def _(n=n):
                x_s[...] = xs[n][...]

        x = wide(x_s[...])
    unit, _ = unit_rows(x)
    a_s[...] = unit * vec_ref[0:1] + vec_ref[1:2]
    first = pl.ds(pl.multiple_of(f * part, 128), part)
    second = pl.ds(pl.multiple_of((1 - f) * part, 128), part)
    a = jnp.concatenate([low(a_s[:, first]), low(a_s[:, second])], axis=1)
    norm_ref[...] = a
    if with_q:
        keep_ref[:, :part] = xs[0][:, first]
        keep_ref[:, part:] = xs[0][:, second]
        dy_out[:, :part] = dy_ref[:, first]
        dy_out[:, part:] = dy_ref[:, second]
    at = j ^ sc_ref[1 if with_q else 2]
    cos, sin = tile_angles(base_ref, tile_ref, at if far else at + lax.rem(sc_ref[0], sc_ref[4]) * tiles)
    for n in range(count):
        cols = slice((n + skip) * local, (n + skip + 1) * local)
        u = dot(a, w_s[n]) + bias_ref[:, cols]
        if n < count - 1:
            u = u * cos + (dot(a, r_s[n]) + b_s[n, 0:1]) * sin
        u = low(u)
        if n == 0 and with_q:
            u = u * jnp.asarray(HD**-0.5, BF)
        outs[n][...] = u


def project(scalars, xs, dy, far, rows, vec, wa, wb, bias, base, turns):
    with_q = dy is not None
    width = wa.shape[0] * 2
    local = wa.shape[1] // 3
    tiles = rows // TILE
    if with_q:
        turned = lambda i, sc: i ^ sc[1]
        ins = [row_block(xs[0], turned), row_block(dy, turned)]
        args = [xs[0], dy]
        parts = 1
    else:
        ins = [pl.BlockSpec((TILE, width), lambda i, sc, n=n: (n, 0)) for _, n in xs]
        args = [v for v, _ in xs]
        parts = len(xs)
    ins += [whole(v) for v in (vec, wa, wb, bias, base, turns)]
    args += [vec, wa, wb, bias, base, turns]
    tile = lambda n: pl.BlockSpec((TILE, n), lambda i, sc: (i, 0))
    count = 3 if with_q else 2
    outs = [(shape((rows, local), BF), tile(local))] * count + [(shape((rows, width), BF), tile(width))] * (3 if with_q else 1)
    scratch = [
        pltpu.VMEM((count, width, local), BF),
        pltpu.VMEM((count - 1, width, local), BF),
        pltpu.VMEM((count - 1, 8, local), F32),
        pltpu.VMEM((TILE, width), BF),
        pltpu.VMEM((TILE, width), F32),
    ]
    return call(
        functools.partial(project_kernel, parts, with_q, far, tiles), "project" if with_q else "project_seen", scalars, (tiles,), ins, outs, scratch, args,
        2 * rows * width * local * 5, 8_000_000,
    )


def stack_heads(rows, heads):
    lane = lax.broadcasted_iota(jnp.int32, rows.shape, 1) // HD
    return jnp.concatenate([jnp.where(lane == h, rows, jnp.zeros_like(rows)) for h in range(heads)], axis=0)


def tile_plan(sc_ref, tile, tiles):
    z, prefix, half = sc_ref[0], sc_ref[3], sc_ref[4]
    noisy = z < half
    late = lax.rem(z, half)
    at = tile ^ sc_ref[1]
    prefix = jnp.where(late == 0, prefix, 0)
    top = jnp.maximum(at + 1, (prefix + TILE - 1) // TILE)
    return noisy, late == 1, at, top, prefix


def near_rows(sc_ref, t):
    return pl.ds(pl.multiple_of((t ^ sc_ref[2]) * TILE, TILE), TILE)


def edge_mask(block_gap, k_pos, t, at, noisy, prefix):
    limit = (at - t) * (TILE // BLOCK) + jnp.where(noisy, 0, 1)
    return (block_gap < limit) | (k_pos < prefix - t * TILE)


def fwd_kernel(first, stride, tiles, sc_ref, q_ref, ko_ref, vo_ref, km_ref, vm_ref, kf_ref, vf_ref, wa_ref, wb_ref, o_ref, lse_ref, share_ref, sbuf, mbuf, lbuf, acc):
    tile = first + stride * pl.program_id(0)
    noisy, late, at, top, prefix = tile_plan(sc_ref, tile, tiles)
    width = q_ref.shape[1]
    heads = width // HD
    qs = stack_heads(q_ref[...], heads)
    mbuf[...] = jnp.full_like(mbuf, NEG)
    lbuf[...] = jnp.zeros_like(lbuf)
    acc[...] = jnp.zeros_like(acc)
    high = heads * TILE
    own = pl.ds(pl.multiple_of(tile * TILE, TILE), TILE)

    def keep(slot, s):
        best = mbuf[...]
        for n in range(s.shape[1] // TILE):
            sbuf[slot + n] = s[:, n * TILE : (n + 1) * TILE]
        for n in range(s.shape[1] // 128):
            best = jnp.maximum(best, s[:, n * 128 : (n + 1) * 128])
        mbuf[...] = best

    def plain_step(t, carry):
        keep(t, dot(qs, km_ref[near_rows(sc_ref, t), :], 1, 1))
        return carry

    lax.fori_loop(0, at, plain_step, 0)
    wides = tiles * TILE // WIDE

    def far_rows(n):
        return pl.ds(pl.multiple_of(n * WIDE, WIDE), WIDE)

    def far_step(n, carry):
        keep(tiles + n * (WIDE // TILE), dot(qs, kf_ref[far_rows(n), :], 1, 1))
        return carry

    lax.fori_loop(0, jnp.where(late, wides, 0), far_step, 0)
    q_block = (lax.broadcasted_iota(jnp.int32, (high, TILE), 0) & (TILE - 1)) >> 4
    k_pos = lax.broadcasted_iota(jnp.int32, (high, TILE), 1)
    gap = (k_pos >> 4) - q_block

    def edge_step(t, carry):
        s = dot(qs, km_ref[near_rows(sc_ref, t), :], 1, 1)
        keep(t, jnp.where(edge_mask(gap, k_pos, t, at, noisy, prefix), s, NEG))
        return carry

    lax.fori_loop(at, top, edge_step, 0)

    @pl.when(noisy)
    def _():
        keep(2 * tiles, jnp.where(gap == 0, dot(qs, ko_ref[own, :], 1, 1), NEG))

    best = jnp.max(mbuf[...], axis=1, keepdims=True) * LOG2E
    mbuf[...] = jnp.broadcast_to(best, mbuf.shape)

    def add(slot, v):
        m = mbuf[...]
        total = lbuf[...]
        cols = []
        for n in range(v.shape[0] // TILE):
            s = sbuf[slot + n]
            for k in range(TILE // 128):
                p = jnp.exp2(s[:, k * 128 : (k + 1) * 128] * LOG2E - m)
                total = total + p
                cols.append(low(p))
        lbuf[...] = total
        acc[...] += dot(jnp.concatenate(cols, axis=1), v)

    def near_sum(t, carry):
        add(t, vm_ref[near_rows(sc_ref, t), :])
        return carry

    lax.fori_loop(0, top, near_sum, 0)

    def far_sum(n, carry):
        add(tiles + n * (WIDE // TILE), vf_ref[far_rows(n), :])
        return carry

    lax.fori_loop(0, jnp.where(late, wides, 0), far_sum, 0)

    @pl.when(noisy)
    def _():
        add(2 * tiles, vo_ref[own, :])

    norm = jnp.sum(lbuf[...], axis=1, keepdims=True)
    out = acc[...] * (1.0 / norm)
    lane = lax.broadcasted_iota(jnp.int32, (TILE, width), 1) // HD
    picked = out[:TILE]
    for h in range(1, heads):
        picked = jnp.where(lane == h, out[h * TILE : (h + 1) * TILE], picked)
    picked = low(picked)
    o_ref[...] = picked
    lse = jnp.broadcast_to(best + jnp.log2(norm), (high, 128))
    lse_ref[0] = jnp.concatenate(
        [lse[h * TILE : (h + 1) * TILE].T[:1] for h in range(heads)] + [jnp.zeros((8 - heads, TILE), F32)], axis=0
    )
    part = wa_ref.shape[1]
    share_ref[:, :part] = low(dot(picked, wa_ref[...]))
    share_ref[:, part:] = low(dot(picked, wb_ref[...]))


def attention(scalars, first, stride, q, keys, values, wa, wb):
    rows, width = q.shape
    tiles, heads = rows // TILE, width // HD
    count = tiles // stride
    flat = [v for pair in zip(keys, values) for v in pair]
    tile = lambda n: pl.BlockSpec((TILE, n), lambda i, sc: (i, 0))
    full = 2 * wa.shape[1]
    return call(
        functools.partial(fwd_kernel, first, stride, tiles), "attn_fwd", scalars, (count,),
        [row_block(q, lambda i, sc: first + stride * i)] + [whole(v) for v in flat + [wa, wb]],
        [
            (shape((count * TILE, width), BF), tile(width)),
            (shape((count, 8, TILE), F32), pl.BlockSpec((1, 8, TILE), lambda i, sc: (i, 0, 0))),
            (shape((count * TILE, full), BF), tile(full)),
        ],
        [
            pltpu.VMEM((2 * tiles + 1, heads * TILE, TILE), F32),
            pltpu.VMEM((heads * TILE, 128), F32),
            pltpu.VMEM((heads * TILE, 128), F32),
            pltpu.VMEM((heads * TILE, width), F32),
        ],
        [q] + flat + [wa, wb], 3_000_000_000 * count, 4_000_000,
    )


def turn_back(grad, cos, sin, turn):
    moved = grad * sin
    high = low(moved)
    rest = low(moved - wide(high))
    return low(grad * cos - (dot(high, turn) + dot(rest, turn)))


def bwd_kernel(first, stride, tiles, sc_ref, q_ref, o_ref, za_ref, zb_ref, lse_ref, ko_ref, vo_ref, km_ref, vm_ref, kf_ref, vf_ref, wa_ref, wb_ref, base_ref, tile_ref,
               dq_ref, dk_ref, dv_ref, dqt, st, gt, lse_s, del_s, qs_s, gs_s, z_s, dk_s, dv_s):
    g_id = pl.program_id(0)
    tile = first + stride * g_id
    noisy, late, at, top, prefix = tile_plan(sc_ref, tile, tiles)
    width = q_ref.shape[1]
    heads = width // HD
    high = heads * TILE
    part = wa_ref.shape[1]
    rows = tiles * TILE
    per = za_ref.shape[0] // TILE

    @pl.when(g_id == 0)
    def _():
        dk_s[...] = jnp.zeros_like(dk_s)
        dv_s[...] = jnp.zeros_like(dv_s)

    for n in range(2 * per):

        @pl.when(g_id == n)
        def _(n=n):
            z_s[...] = (za_ref if n < per else zb_ref)[(n % per) * TILE : (n % per + 1) * TILE, :]

    z = z_s[...]
    g32 = dot(z[:, :part], wa_ref[...], 1, 1) + dot(z[:, part:], wb_ref[...], 1, 1)
    g = low(g32)
    g32 = wide(g)
    q = q_ref[...]
    qs_s[...] = stack_heads(q, heads)
    gs_s[...] = stack_heads(g, heads)
    q_t = wide(q).T
    g_t = g32.T
    prod = (wide(o_ref[...]) * g32).T
    head_of = lax.broadcasted_iota(jnp.int32, (width, TILE), 0) // HD
    for h in range(heads):
        cols = slice(h * TILE, (h + 1) * TILE)
        st[:, cols] = low(jnp.where(head_of == h, q_t, 0.0))
        gt[:, cols] = low(jnp.where(head_of == h, g_t, 0.0))
        del_s[:, cols] = jnp.sum(prod[h * HD : (h + 1) * HD], axis=0, keepdims=True)
        lse_s[:, cols] = lse_ref[0, h : h + 1, :]
    dqt[...] = jnp.zeros_like(dqt)

    def step(k, v, base, mask):
        n = k.shape[0]
        to = pl.ds(base, n)
        s = dot(k, st[...])
        p = jnp.exp2(s * LOG2E - lse_s[...])
        if mask is not None:
            p = jnp.where(mask, p, 0.0)
        dp = dot(v, gt[...])
        ds = low(p * (dp - del_s[...]))
        p = low(p)
        dv_s[to, :] += dot(p, gs_s[...])
        dk_s[to, :] += dot(ds, qs_s[...])
        dqt[...] += dot(k, ds, 0, 0)

    def near_at(t):
        return pl.multiple_of(rows + (t ^ sc_ref[2]) * TILE, TILE)

    def plain_step(t, carry):
        at_t = near_rows(sc_ref, t)
        step(km_ref[at_t, :], vm_ref[at_t, :], near_at(t), None)
        return carry

    lax.fori_loop(0, at, plain_step, 0)
    wides = rows // WIDE

    def far_step(n, carry):
        at_n = pl.ds(pl.multiple_of(n * WIDE, WIDE), WIDE)
        step(kf_ref[at_n, :], vf_ref[at_n, :], pl.multiple_of(2 * rows + n * WIDE, WIDE), None)
        return carry

    lax.fori_loop(0, jnp.where(late, wides, 0), far_step, 0)
    k_pos = lax.broadcasted_iota(jnp.int32, (TILE, high), 0)
    gap = (k_pos >> 4) - ((lax.broadcasted_iota(jnp.int32, (TILE, high), 1) & (TILE - 1)) >> 4)

    def edge_step(t, carry):
        at_t = near_rows(sc_ref, t)
        step(km_ref[at_t, :], vm_ref[at_t, :], near_at(t), edge_mask(gap, k_pos, t, at, noisy, prefix))
        return carry

    lax.fori_loop(at, top, edge_step, 0)

    @pl.when(noisy)
    def _():
        own = pl.ds(pl.multiple_of(tile * TILE, TILE), TILE)
        step(ko_ref[own, :], vo_ref[own, :], pl.multiple_of(tile * TILE, TILE), gap == 0)

    turn = turn_matrix(width)
    dq_t = jnp.where(head_of == 0, dqt[:, :TILE], 0.0)
    for h in range(1, heads):
        dq_t = jnp.where(head_of == h, dqt[:, h * TILE : (h + 1) * TILE], dq_t)
    late_at = late.astype(jnp.int32) * tiles
    dq_ref[...] = turn_back(dq_t.T * (HD**-0.5), *tile_angles(base_ref, tile_ref, at + late_at), turn)

    @pl.when(g_id == pl.num_programs(0) - 1)
    def _():
        dv_ref[...] = low(dv_s[...])

        def finish(base, true_tile):
            to = pl.ds(pl.multiple_of(base, TILE), TILE)
            dk_ref[to, :] = turn_back(dk_s[to, :], *tile_angles(base_ref, tile_ref, true_tile), turn)

        def all_three(j, carry):
            finish(j * TILE, (j ^ sc_ref[1]) + late_at)
            finish(rows + j * TILE, (j ^ sc_ref[2]) + late_at)
            finish(2 * rows + j * TILE, j ^ sc_ref[2])
            return carry

        lax.fori_loop(0, tiles, all_three, 0)


def attention_grads(scalars, first, stride, q, o, za, zb, lse, keys, values, wa, wb, base, turns):
    rows, width = q.shape
    tiles, heads = rows // TILE, width // HD
    count = tiles // stride
    flat = [v for pair in zip(keys, values) for v in pair]
    tile = pl.BlockSpec((TILE, width), lambda i, sc: (i, 0))
    total = pl.BlockSpec((3 * rows, width), lambda i, sc: (0, 0))
    high = heads * TILE
    return call(
        functools.partial(bwd_kernel, first, stride, tiles), "attn_bwd", scalars, (count,),
        [row_block(q, lambda i, sc: first + stride * i), tile, whole(za), whole(zb), pl.BlockSpec((1, 8, TILE), lambda i, sc: (i, 0, 0))]
        + [whole(v) for v in flat + [wa, wb, base, turns]],
        [(shape((count * TILE, width), BF), tile), (shape((3 * rows, width), BF), total), (shape((3 * rows, width), BF), total)],
        [
            pltpu.VMEM((width, high), F32),
            pltpu.VMEM((width, high), BF),
            pltpu.VMEM((width, high), BF),
            pltpu.VMEM((1, high), F32),
            pltpu.VMEM((1, high), F32),
            pltpu.VMEM((high, width), BF),
            pltpu.VMEM((high, width), BF),
            pltpu.VMEM((TILE, za.shape[1]), BF),
            pltpu.VMEM((3 * rows, width), F32),
            pltpu.VMEM((3 * rows, width), F32),
        ],
        [q, o, za, zb, lse] + flat + [wa, wb, base, turns], 8_000_000_000 * count, 10_000_000,
    )


def norm_kernel(sc_ref, x_ref, mine_ref, theirs_ref, vec_ref, mid_ref, a_ref):
    mid = wide(x_ref[...]) + (wide(mine_ref[...]) + wide(theirs_ref[...])) + vec_ref[4:5]
    mid_ref[...] = mid
    unit, _ = unit_rows(mid)
    a_ref[...] = low(unit * vec_ref[5:6] + vec_ref[6:7])


def norm_two(scalars, index, x, mine, theirs, vec):
    rows, width = mine.shape
    block = pl.BlockSpec((rows, width), lambda i, sc: (0, 0))
    return call(
        norm_kernel, "norm_two", scalars, (1,),
        [row_block(x, lambda i, sc: index), block, block, whole(vec)],
        [(shape((rows, width), F32), block), (shape((rows, width), BF), block)], [], [x, mine, theirs, vec], 10 * rows * width, 3_000_000,
    )


def norm_back(grad, x, gain):
    unit, scale = unit_rows(x)
    weighted = grad * gain
    return scale * (weighted - jnp.mean(weighted, axis=-1, keepdims=True) - unit * jnp.mean(weighted * unit, axis=-1, keepdims=True))


def norm_grad_kernel(sc_ref, dy_ref, mid_ref, mine_ref, theirs_ref, vec_ref, dmid_ref, dz_ref):
    dmid = wide(dy_ref[...]) + norm_back(wide(mine_ref[...]) + wide(theirs_ref[...]), mid_ref[...], vec_ref[5:6])
    dmid_ref[...] = dmid
    dz_ref[...] = low(dmid)


def norm_two_grad(scalars, index, dy, mid, mine, theirs, vec):
    rows, width = mid.shape
    block = pl.BlockSpec((rows, width), lambda i, sc: (0, 0))
    return call(
        norm_grad_kernel, "norm_two_grad", scalars, (1,),
        [row_block(dy, lambda i, sc: index), block, block, block, whole(vec)],
        [(shape((rows, width), F32), block), (shape((rows, width), BF), block)], [], [dy, mid, mine, theirs, vec], 20 * rows * width, 3_000_000,
    )


def mlp_kernel(sc_ref, a_ref, b_ref, dy_ref, ua_ref, ub_ref, da_ref, db_ref, bias_ref, share_ref, act_ref, pre_ref, x_s):
    g = pl.program_id(0)
    part = ua_ref.shape[0]

    @pl.when(g == 0)
    def _():
        x_s[...] = a_ref[...]

    @pl.when(g == 1)
    def _():
        x_s[...] = b_ref[...]

    x, dy = x_s[...], dy_ref[...]
    pre = dot(x[:, :part], ua_ref[...]) + dot(x[:, part:], ub_ref[...]) + bias_ref[...]
    cdf = 0.5 + 0.5 * lax.erf(pre * (2.0**-0.5))
    act_ref[...] = low(pre * cdf)
    slope = cdf + pre * (jnp.exp2(pre * pre * (-0.5 * LOG2E)) * 0.3989422804014327)
    grad = dot(dy[:, :part], da_ref[...], 1, 1) + dot(dy[:, part:], db_ref[...], 1, 1)
    dpre = low(grad * slope)
    pre_ref[...] = dpre
    share_ref[:, :part] = low(dot(dpre, ua_ref[...], 1, 1))
    share_ref[:, part:] = low(dot(dpre, ub_ref[...], 1, 1))


def mlp(scalars, first, stride, own, other, dy, ua, ub, da, db, bias):
    width, units = own.shape[1], ua.shape[1]
    tile = lambda n: pl.BlockSpec((TILE, n), lambda i, sc: (i, 0))
    return call(
        mlp_kernel, "mlp", scalars, (2,),
        [whole(own), whole(other), row_block(dy, lambda i, sc: first + stride * i)] + [whole(v) for v in (ua, ub, da, db, bias)],
        [(shape((2 * TILE, width), BF), tile(width)), (shape((2 * TILE, units), BF), tile(units)), (shape((2 * TILE, units), BF), tile(units))],
        [pltpu.VMEM((TILE, width), BF)], [own, other, dy, ua, ub, da, db, bias], 6 * 2 * TILE * width * units, 8_000_000,
    )


def share_kernel(blocks, n_q, tiles, chunks, sc_ref, *refs):
    refs = list(refs)
    dqs = [refs.pop(0) for _ in range(n_q)]
    dks = [refs.pop(0) for _ in range(chunks)]
    dvs = [refs.pop(0) for _ in range(chunks)]
    norms = [refs.pop(0) for _ in range(blocks)]
    wa_ref, wb_ref, share_ref = refs.pop(0), refs.pop(0), refs.pop(0)
    kinds = 3 if n_q else 2
    grads = [refs.pop(0) for _ in range(kinds)]
    sums = refs.pop(0)
    w_s, a_s, t_s, q_s = refs
    j = pl.program_id(0)
    local = dks[0].shape[1]
    part = wa_ref.shape[0]
    skip = 3 - kinds

    @pl.when(j == 0)
    def _():
        t_s[...] = jnp.zeros_like(t_s)
        sums[...] = jnp.zeros_like(sums)
        for n in range(kinds):
            cols = slice((n + skip) * local, (n + skip + 1) * local)
            w_s[n, :part] = wa_ref[:, cols]
            w_s[n, part:] = wb_ref[:, cols]

    for b in range(blocks):

        @pl.when((j >= b * tiles) & (j < (b + 1) * tiles))
        def _(b=b):
            a_s[...] = norms[b][...]

    a = a_s[...]
    parts = []
    if n_q == 1:
        parts.append(dqs[0][...])
    elif n_q:
        for n in range(n_q):

            @pl.when(lax.rem(j, n_q) == n)
            def _(n=n):
                q_s[...] = dqs[n][...]

        parts.append(q_s[...])
    total = lambda group: group[0][...] if chunks == 1 else low(sum(wide(r[...]) for r in group))
    parts += [total(dks), total(dvs)]
    share = sum(dot(p, w_s[n], 1, 1) for n, p in enumerate(parts))
    share_ref[...] = low(share)
    for n, p in enumerate(parts):
        t_s[n] += dot(p, a, 0, 0)
        sums[n : n + 1, :] += jnp.sum(wide(p), axis=0, keepdims=True)

    @pl.when(j == pl.num_programs(0) - 1)
    def _():
        for n in range(kinds):
            grads[n][...] = t_s[n].T


def shares(scalars, start, dqs, dks, dvs, norms, wa, wb):
    rows, width = norms[0].shape
    local = dks[0].shape[1]
    tiles, blocks, chunks = rows // TILE, len(norms), len(dks)
    kinds = 3 if dqs else 2
    ins = [row_block(v, lambda i, sc: i // len(dqs)) for v in dqs]
    ins += [row_block(v, lambda i, sc: i + start) for v in dks + dvs]
    ins += [row_block(v, lambda i, sc, b=b: jnp.clip(i - b * tiles, 0, tiles - 1)) for b, v in enumerate(norms)]
    ins += [whole(wa), whole(wb)]
    fixed = lambda dims: pl.BlockSpec(dims, lambda i, sc: (0,) * len(dims))
    outs = [(shape((blocks * rows, width), BF), pl.BlockSpec((TILE, width), lambda i, sc: (i, 0)))]
    outs += [(shape((width, local), F32), fixed((width, local)))] * kinds + [(shape((8, local), F32), fixed((8, local)))]
    scratch = [
        pltpu.VMEM((kinds, width, local), BF),
        pltpu.VMEM((TILE, width), BF),
        pltpu.VMEM((kinds, local, width), F32),
        pltpu.VMEM((TILE, local), BF),
    ]
    return call(
        functools.partial(share_kernel, blocks, len(dqs), tiles, chunks), "share" if dqs else "share_seen", scalars, (blocks * tiles,), ins, outs, scratch,
        dqs + dks + dvs + norms + [wa, wb], 4 * blocks * rows * width * local * kinds, 8_000_000,
    )


def place_kernel(pieces, which, sc_ref, *refs):
    out_ref, x_s = refs[pieces], refs[pieces + 1]
    j = pl.program_id(0)
    f = sc_ref[5]
    part = out_ref.shape[1] // 2
    for n in range(pieces):

        @pl.when(j == n)
        def _(n=n):
            x_s[...] = refs[n][...].astype(x_s.dtype)

    out_ref[:, pl.ds(pl.multiple_of(f * part, 128), part)] = x_s[:, :part]
    out_ref[:, pl.ds(pl.multiple_of((1 - f) * part, 128), part)] = x_s[:, part:]


def placed(scalars, which, pieces, kind):
    width = pieces[0][0].shape[1]
    ins = [pl.BlockSpec((TILE, width), lambda i, sc, n=n: (n, 0)) for _, n in pieces]
    rows = TILE * len(pieces)
    return call(
        functools.partial(place_kernel, len(pieces), which), "placed", scalars, (len(pieces),), ins,
        [(shape((rows, width), kind), pl.BlockSpec((TILE, width), lambda i, sc: (i ^ sc[which], 0)))],
        [pltpu.VMEM((TILE, width), kind)], [v for v, _ in pieces], 0, 6_000_000,
    )[0]


def pack_kernel(n, *refs):
    out_ref, row_s = refs[-2], refs[-1]
    row_s[...] = jnp.zeros_like(row_s)
    for k in range(n):
        row_s[k : k + 1, :] = wide(refs[k][...])
    top = n
    for ref in refs[n:-2]:
        row_s[top : top + ref.shape[0], : ref.shape[1]] = wide(ref[...])
        top += ref.shape[0]
    out_ref[...] = low(row_s[...])


def packed(vectors, folds):
    part = vectors[0].shape[0]
    args = [v.reshape(1, part) for v in vectors] + [v.reshape(-1, v.shape[-1]) for v in folds]
    rows = len(vectors) + sum(v.shape[0] for v in args[len(vectors) :])
    rows += -rows % 16
    return pl.pallas_call(
        functools.partial(pack_kernel, len(vectors)), name="packed", out_shape=shape((rows, part), BF),
        scratch_shapes=[pltpu.VMEM((rows, part), F32)],
        compiler_params=pltpu.CompilerParams(vmem_limit_bytes=8 << 20),
        cost_estimate=pl.CostEstimate(flops=0, bytes_accessed=100_000, transcendentals=0),
    )(*args)


def unpack_kernel(sizes, sc_ref, a_ref, b_ref, vec_ref, qkv_ref, up_ref):
    f = sc_ref[5]
    a, b = wide(a_ref[...]), wide(b_ref[...])
    lo, hi = jnp.where(f == 0, a, b), jnp.where(f == 0, b, a)
    part = a.shape[1]
    n = 6
    vec_ref[0:2, :part], vec_ref[0:2, part:] = lo[0:2], hi[0:2]
    vec_ref[2:8, :part], vec_ref[2:8, part:] = a[0:6], b[0:6]
    lanes = HD // 2
    for ref, start, count in ((qkv_ref, n, sizes[0]), (up_ref, n + sizes[0], sizes[1])):
        ref[...] = jnp.concatenate([p[start + k : start + k + 1, :lanes] for k in range(count) for p in (lo, hi)], axis=1)


def unpacked(scalars, a, b, sizes):
    outs = [shape((8, 2 * a.shape[1]), F32), shape((1, sizes[0] * HD), F32), shape((1, sizes[1] * HD), F32)]
    fixed = [(o, pl.BlockSpec(o.shape, lambda i, sc: (0, 0))) for o in outs]
    return call(functools.partial(unpack_kernel, sizes), "unpacked", scalars, (1,), [whole(a), whole(b)], fixed, [], [a, b], 0, 100_000, 8)


def weights_kernel(pieces, order, sc_ref, *refs):
    refs = list(refs)
    a_refs = [refs.pop(0) for _ in range(pieces)]
    dy_ref = refs.pop(0)
    pre_refs, act_refs = [refs.pop(0) for _ in range(2)], [refs.pop(0) for _ in range(2)]
    own_ref, other_ref, sum_ref, a_s, d_s, p_s, c_s, g_s = refs
    j = pl.program_id(0)

    @pl.when(j == 0)
    def _():
        for n in range(pieces):
            to = slice(n * TILE, (n + 1) * TILE)
            a_s[to, :] = a_refs[n][...]
            d_s[to, :] = dy_ref[order[n] * TILE : (order[n] + 1) * TILE, :]
        for n in range(2):
            to = slice(n * 2 * TILE, (n + 1) * 2 * TILE)
            p_s[to, :] = pre_refs[n][...]
            c_s[to, :] = act_refs[n][...]
        sum_ref[...] = jnp.zeros_like(sum_ref)
        sum_ref[0:1, :] = jnp.sum(wide(p_s[...]), axis=0, keepdims=True)
        sum_ref[1:2, :] = jnp.sum(wide(d_s[...]), axis=0, keepdims=True)

    part, units = own_ref.shape[0], p_s.shape[1]
    cols = pl.ds(pl.multiple_of((1 - j) * part, 128), part)
    g_s[:, :units] = dot(a_s[:, cols], p_s[...], 0, 0)
    g_s[:, units:] = dot(d_s[:, cols], c_s[...], 0, 0)

    @pl.when(j == 0)
    def _():
        other_ref[...] = low(g_s[...])

    @pl.when(j == 1)
    def _():
        own_ref[...] = g_s[...]


def mlp_weights(scalars, twos, dy, order, pres, acts):
    rows, width = dy.shape
    units = pres[0].shape[1]
    part = width // 2
    outs = [shape((part, 2 * units), F32), shape((part, 2 * units), BF), shape((8, max(width, units)), F32)]
    fixed = [(o, pl.BlockSpec(o.shape, lambda i, sc: (0, 0))) for o in outs]
    args = twos + [dy] + pres + acts
    scratch = [pltpu.VMEM((rows, n), BF) for n in (width, width, units, units)] + [pltpu.VMEM((part, 2 * units), F32)]
    return call(
        functools.partial(weights_kernel, len(twos), order), "mlp_weights", scalars, (2,), [whole(v) for v in args], fixed, scratch, args,
        4 * rows * width * units, 12_000_000, 40,
    )


PAIR = [(0, 1), (1, 0)]


def swap_core(values):
    return lax.ppermute(values, "tp", [(i, i ^ 1) for i in range(4)])


def swap_y(values):
    return lax.ppermute(values, "tp", [(i, i ^ 2) for i in range(4)])


def hop(values, pairs):
    return lax.ppermute(values, "ctx", pairs)


def after(values, *deps):
    return lax.optimization_barrier((values, *deps))[0]


def pick(parts, index):
    return lax.dynamic_index_in_dim(parts, index, 0, keepdims=False)


def ordered(first, second, flip):
    return jnp.where(flip == 0, jnp.stack([first, second]), jnp.stack([second, first]))


def sum_ctx(values, z):
    near, far = z & 1, z >> 1
    near_pairs, far_pairs = [(i, i ^ 1) for i in range(4)], [(i, i ^ 2) for i in range(4)]
    rows, cols = values.shape
    halves = values.reshape(2, rows // 2, cols)
    half = pick(halves, near) + wide(hop(low(pick(halves, 1 - near)), near_pairs))
    quarters = half.reshape(2, rows // 4, cols)
    quarter = low(pick(quarters, far) + wide(hop(low(pick(quarters, 1 - far)), far_pairs)))
    half = ordered(quarter, hop(quarter, far_pairs), far).reshape(rows // 2, cols)
    return wide(ordered(half, hop(half, near_pairs), near).reshape(rows, cols))


def body(
    hidden,
    prefix,
    w_qkv,
    b_qkv,
    w_out,
    b_out,
    w_up,
    b_up,
    w_down,
    b_down,
    ln1_gain,
    ln1_shift,
    ln2_gain,
    ln2_shift,
    cotangent,
):
    members = lax.axis_size("fsdp")
    paired = members == 2
    z = lax.axis_index("ctx")
    t = lax.axis_index("tp")
    half_ctx = lax.axis_size("ctx") // 2
    core, side = t & 1, t >> 1
    turn_q, turn_k = 2 * core, 2 * core + side
    f = lax.axis_index("fsdp") if paired else jnp.int32(0)
    rows, width = hidden.shape[1], hidden.shape[2]
    local, units = w_qkv.shape[2], w_up.shape[1]
    half, quarter, part = rows // 2, rows // 4, width // 2
    tiles = rows // TILE
    scalars = jnp.stack([z, turn_q, turn_k, prefix[0], jnp.int32(half_ctx), f]).astype(jnp.int32)

    def both(values, axis):
        if paired:
            return values, lax.ppermute(values, "fsdp", PAIR)
        return tuple(jnp.split(lax.all_gather(values, "fsdp", axis=axis, tiled=True), 2, axis=axis))

    qkv_a, qkv_b = both(w_qkv.reshape(w_qkv.shape[0], 3 * local), 0)
    own_quarter = lax.dynamic_slice(hidden[0], (turn_k * quarter, 0), (quarter, width))
    near_quarter = hop(own_quarter, [(i + half_ctx, i) for i in range(half_ctx)])
    far_from = after(own_quarter, near_quarter)
    near_quarter = jnp.where(z >= half_ctx, own_quarter, near_quarter)
    far_quarter = hop(far_from, [(2, 1)]) + hop(far_from, [(2, 3)])

    def spread(values):
        other = swap_y(values)
        pair = swap_core(jnp.concatenate([values, other], axis=0))
        return [(values, 0), (other, 0), (pair, 0), (pair, 1)]

    vectors_in = (ln1_gain, ln1_shift, b_out, ln2_gain, ln2_shift, b_down)
    fold_rows = (b_qkv.size // b_qkv.shape[-1], b_up.shape[0])
    if paired:
        small = packed(vectors_in, (b_qkv, b_up))
        vec, bias_qkv, bias_up = unpacked(scalars, small, lax.ppermute(small, "fsdp", PAIR), fold_rows)
    else:
        gather = lambda v: wide(lax.all_gather(v, "fsdp", axis=v.ndim - 1, tiled=True))
        found = [gather(v) for v in vectors_in]
        vec = jnp.stack(found[:2] + found)
        bias_qkv, bias_up = gather(b_qkv).reshape(1, -1), gather(b_up).reshape(1, -1)
    gain_one, shift_one, gain_two, shift_two, bias_down = vec[2], vec[3], vec[5], vec[6], vec[7]
    later = after((w_out, w_up, w_down), qkv_b)
    out_a, out_b = both(later[0], 1)
    up_a, up_b = both(later[1], 0)
    down_a, down_b = both(later[2], 1)

    lane = jnp.arange(local, dtype=jnp.int32) % (HD // 2)
    frequency = jnp.power(jnp.float32(10000.0), -2.0 * wide(lane) / HD)[None, :]
    base = wide(jnp.arange(TILE, dtype=jnp.int32))[:, None] * frequency
    turns = wide(jnp.arange(half_ctx * tiles, dtype=jnp.int32) * TILE)[:, None] * frequency
    base, turns = jnp.stack([jnp.cos(base), jnp.sin(base)]), jnp.stack([jnp.cos(turns), jnp.sin(turns)])

    q, k_own, v_own, norm_own, x_turned, dy = project(
        scalars, [hidden[0]], cotangent[0], False, rows, vec, qkv_a, qkv_b, bias_qkv, base, turns
    )
    k_near, v_near, norm_near = project(scalars, spread(near_quarter), None, False, rows, vec, qkv_a, qkv_b, bias_qkv, base, turns)
    k_far, v_far, norm_far = project(scalars, spread(far_quarter), None, True, rows, vec, qkv_a, qkv_b, bias_qkv, base, turns)
    keys, values = [k_own, k_near, k_far], [v_own, v_near, v_far]

    def core_sum(share):
        return low(wide(share[:TILE]) + wide(swap_core(share[TILE:])))

    o0, lse0, share = attention(scalars, 0, 2, q, keys, values, out_a, out_b)
    mine0 = core_sum(share)
    o1, lse1, share = attention(scalars, 1, 2, after(q, mine0), keys, values, out_a, out_b)
    mine1 = core_sum(share)
    mid0, two0 = norm_two(scalars, 0, x_turned, mine0, swap_y(mine0), vec)
    twos0 = (two0, swap_core(two0))
    share, act0, pre0 = mlp(scalars, 0, 2, after(twos0[0], mine1), twos0[1], dy, up_a, up_b, down_a, down_b, bias_up)
    back0 = core_sum(share)
    mid1, two1 = norm_two(scalars, 1, x_turned, mine1, after(swap_y(mine1), back0), vec)
    twos1 = (two1, swap_core(two1))
    share, act1, pre1 = mlp(scalars, 1, 2, *twos1, dy, up_a, up_b, down_a, down_b, bias_up)
    back1 = core_sum(share)
    back_y0, back_y1 = swap_y(back0), swap_y(back1)

    act0, act1, pre0, pre1 = after((act0, act1, pre0, pre1), back1)
    g_own, g_other, sums_mlp = mlp_weights(scalars, list(twos0) + list(twos1), dy, (0, 2, 1, 3), [pre0, pre1], [act0, act1])
    full_down = jnp.concatenate([down_a, down_b], axis=1)
    down0 = core_sum(low(dot(act0, full_down)))
    down1 = core_sum(low(dot(act1, full_down)))
    down_y0, down_y1 = swap_y(after(down0, back_y0, back_y1)), swap_y(after(down1, back_y0, back_y1))

    def partner_sum(own_part, other_part):
        if paired:
            return own_part + wide(lax.ppermute(other_part, "fsdp", PAIR))
        return lax.psum_scatter(jnp.concatenate([own_part, wide(other_part)], axis=0), "fsdp", scatter_dimension=0, tiled=True)

    if not paired:
        g_own, g_other = g_own, g_other
    group = partner_sum(g_own, g_other)
    near_bit, far_bit = z & 1, z >> 1
    near_pairs, far_pairs = [(i, i ^ 1) for i in range(4)], [(i, i ^ 2) for i in range(4)]

    def split(values, bit):
        grid = values.reshape(2, values.shape[0] // 2, values.shape[1])
        return pick(grid, bit), low(pick(grid, 1 - bit))

    dmid0, dz0 = norm_two_grad(scalars, 0, dy, mid0, back0, back_y0, vec)
    dzs0 = (dz0, swap_core(dz0))
    dmid1, dz1 = norm_two_grad(scalars, 1, dy, mid1, back1, back_y1, vec)
    dzs1 = (dz1, swap_core(dz1))
    dq0, dk0, dv0 = attention_grads(scalars, 0, 2, q, o0, *dzs0, lse0, keys, values, out_a, out_b, base, turns)
    g_keep, g_send = split(group, near_bit)
    dq1, dk1, dv1 = attention_grads(scalars, 1, 2, after(q, dk0, g_send), o1, *dzs1, lse1, keys, values, out_a, out_b, base, turns)
    g_half = g_keep + wide(hop(g_send, near_pairs))
    g_keep, g_send = split(g_half, far_bit)
    g_quarter = low(g_keep + wide(hop(g_send, far_pairs)))
    g_half = ordered(g_quarter, hop(g_quarter, far_pairs), far_bit).reshape(g_half.shape)
    first_group = wide(ordered(g_half, hop(g_half, near_pairs), near_bit).reshape(group.shape))

    result0 = low(mid0 + (wide(down0) + wide(down_y0)) + bias_down)
    result1 = low(mid1 + (wide(down1) + wide(down_y1)) + bias_down)
    other = swap_core(jnp.concatenate([result0, result1], axis=0))
    result = placed(scalars, 1, [(result0, 0), (result1, 0), (other, 0), (other, 1)], BF)

    dks, dvs = [dk0, dk1], [dv0, dv1]
    share_seen, gk_seen, gv_seen, sums_seen = shares(scalars, tiles, [], dks, dvs, [norm_near, norm_far], qkv_a, qkv_b)
    share_own, gq, gk, gv, sums = shares(scalars, 0, after([dq0, dq1], share_seen), dks, dvs, [norm_own], qkv_a, qkv_b)

    def core_half(share):
        return low(wide(share[:half]) + wide(swap_core(share[half:])))

    near_mine = core_half(share_seen[:rows])
    far_mine = core_half(share_seen[rows:])
    near_q = low(wide(near_mine[:quarter]) + wide(swap_y(near_mine[quarter:])))
    near_in = hop(near_q, [(0, 1), (1, 3)])
    far_q = wide(far_mine[:quarter]) + wide(swap_y(far_mine[quarter:]))
    far_q = low(far_q + jnp.where(z == 1, wide(near_in), 0.0))
    far_in = wide(hop(far_q, [(1, 2)])) + wide(hop(far_q, [(3, 2)]))
    own_mine = core_half(share_own).reshape(2, quarter, width)
    da_one = wide(pick(own_mine, side)) + wide(swap_y(pick(own_mine, 1 - side)))
    da_one = da_one + far_in + jnp.where(z >= half_ctx, wide(near_q) + jnp.where(z == 3, wide(near_in), 0.0), 0.0)
    x_q = wide(lax.dynamic_slice(x_turned, (side * quarter, 0), (quarter, width)))
    grad_q = low(jnp.where(side == 0, dmid0, dmid1) + norm_back(da_one, x_q, gain_one))
    grad_y = swap_y(grad_q)
    grad_c = swap_core(jnp.concatenate([grad_q, grad_y], axis=0))
    grad_input = placed(scalars, 2, [(grad_q, 0), (grad_y, 0), (grad_c, 0), (grad_c, 1)], F32)

    dz_all = jnp.concatenate([*dzs0, *dzs1], axis=0)
    g_out = dot(dz_all, jnp.concatenate([o0, o1], axis=0), 0, 0)
    g_qkv = jnp.concatenate([gq, gk + gk_seen, gv + gv_seen], axis=1)
    gb_qkv = jnp.concatenate([sums[0], sums[1] + sums_seen[0], sums[2] + sums_seen[1]])
    g_all = jnp.concatenate([g_out, g_qkv], axis=1)
    second_group = sum_ctx(partner_sum(g_all[:part], low(g_all[part:])), z)

    def gain_grad(weights, grad, bias_grad, gain, shift):
        full = wide(jnp.concatenate(weights, axis=0))
        by_shift = jnp.sum(full * bias_grad[None, :], axis=1)
        return (jnp.sum(full * grad, axis=1) - shift * by_shift) / gain, by_shift

    gb_up, gb_down = sums_mlp[0], sums_mlp[1] * 0.25
    gb_out = (jnp.sum(wide(dz0), axis=0) + jnp.sum(wide(dz1), axis=0)) * 0.5
    g_gain_one, g_shift_one = gain_grad((qkv_a, qkv_b), g_qkv, gb_qkv, gain_one, shift_one)
    g_up = jnp.concatenate([g_own[:, :units], wide(g_other[:, :units])], axis=0)
    g_gain_two, g_shift_two = gain_grad((up_a, up_b), g_up, gb_up, gain_two, shift_two)
    over_tp = after(jnp.stack([gb_out, gb_down, g_gain_one, g_shift_one, g_gain_two, g_shift_two]), near_q)
    over_tp = over_tp + swap_core(over_tp)
    over_tp = over_tp + swap_y(over_tp)
    if paired:
        take = lambda v, n: lax.dynamic_index_in_dim(v.reshape(-1, 2, HD // 2), n, 1, keepdims=False).reshape(-1)
        mine = jnp.concatenate([over_tp[:, :part].reshape(-1), take(gb_qkv, f), take(gb_up, f)])
        other = jnp.concatenate([over_tp[:, part:].reshape(-1), take(gb_qkv, 1 - f), take(gb_up, 1 - f)])
        vectors = mine + lax.ppermute(other, "fsdp", PAIR)
    else:
        scattered = [
            lax.psum_scatter(v, "fsdp", scatter_dimension=1, tiled=True).reshape(-1)
            for v in (over_tp, gb_qkv.reshape(-1, HD), gb_up.reshape(-1, HD))
        ]
        vectors = jnp.concatenate(scattered)
    vectors = vectors + hop(vectors, [(i, i ^ 1) for i in range(4)])
    vectors = vectors + hop(vectors, [(i, i ^ 2) for i in range(4)])
    own = width // members
    named = vectors[: 6 * own].reshape(6, own)
    cut = 6 * own + b_qkv.size
    return (
        result[None],
        grad_input[None],
        second_group[:, local:].reshape(w_qkv.shape),
        vectors[6 * own : cut].reshape(b_qkv.shape),
        second_group[:, :local].T,
        named[0],
        first_group[:, :units],
        vectors[cut:].reshape(b_up.shape),
        first_group[:, units:].T,
        named[1],
        named[2],
        named[3],
        named[4],
        named[5],
    )


def solution(mesh):
    rows = P("fsdp", "ctx", None)
    weights = (P("fsdp", None, "tp"), P(None, "tp", "fsdp"), P("tp", "fsdp"), P("fsdp"), P("fsdp", "tp"), P("tp", "fsdp"), P("tp", "fsdp"))
    vectors = (P("fsdp"),) * 5
    return jax.shard_map(
        body,
        mesh=mesh,
        in_specs=(rows, P("fsdp")) + weights + vectors + (rows,),
        out_specs=(rows, rows) + weights + vectors,
        check_vma=False,
    )
```

time: 459 us -> 381 us (0.83)
  Pallas kernels: 42.1 us -> 100 us
  matrix products: 53.3 us -> 6.75 us
  local copies, waits for them, and re-layouts: 97.1 us -> 55.6 us
  waiting for transfers between devices: 115 us -> 81.5 us
  other arithmetic: 68.4 us -> 45.9 us
  starting transfers between devices: 71.9 us -> 81.5 us
    pallas_call x2 -> x20, Pallas kernels: 42.1 us -> 100 us  [the longest x19 100 us: call(): pl.pallas_call(kernel, name=name, out_shape=[s for s, _ in outs], grid_sp...]
    dot_general x24 -> x3, matrix products: 53.3 us -> 6.75 us  [dot(): lax.dot_general(a, b, (((ca,), (cb,)), ((), ())), preferred_element_type=...]
    ppermute x16, waiting for transfers between devices: 48.6 us -> 23.5 us  [hop(): return lax.ppermute(values, 'ctx', pairs)]
    ppermute x10 -> x13, waiting for transfers between devices: 48 us -> 26.7 us  [swap_y(): return lax.ppermute(values, 'tp', [(i, i ^ 2) for i in range(4)])]
    slice x26 -> x15, local copies, waits for them, and re-layouts: 22.5 us -> 6.64 us  [the longest x2 2.21 us: core_half(): return low(wide(share[:half]) + wide(swap_core(share[half:])))]
    ppermute x7, waiting for transfers between devices: 16.5 us -> 27 us  [the longest x4 24.2 us: both(): return (values, lax.ppermute(values, 'fsdp', PAIR))]
    ppermute x13 -> x18, starting transfers between devices: 18 us -> 26.2 us  [swap_core(): return lax.ppermute(values, 'tp', [(i, i ^ 1) for i in range(4)])]
    reduce_sum x14 -> x7, other arithmetic: 15.6 us -> 7.95 us  [the longest x2 3.47 us: gain_grad(): return ((jnp.sum(full * grad, axis=1) - shift * by_shift) / gain, by_shift)]
  transfers between devices with their start and end apart: 47 -> 55, of which waited for: 12 -> 18; matrix products, arithmetic and copies ran while one was open for 40% -> 22% of each run, Pallas kernels for 9% -> 22%
where the time goes in v2:
time: 381 us; the launch traced here: 374 us
  Pallas kernels  100 us (26%)
  starting transfers between devices  81.5 us (21%)
  waiting for transfers between devices  81.5 us (21%)
  local copies, waits for them, and re-layouts  55.6 us (15%)
  other arithmetic  45.9 us (12%)
  matrix products  6.75 us (2%)
    pallas_call x19, Pallas kernels, call(): pl.pallas_call(kernel, name=name, out_shape=[s for s, _ in outs], grid_sp...  100 us
    ppermute x16, starting transfers between devices, hop(): return lax.ppermute(values, 'ctx', pairs)  37.1 us
    ppermute x13, waiting for transfers between devices, swap_y(): return lax.ppermute(values, 'tp', [(i, i ^ 2) for i in range(4)])  26.7 us
    ppermute x18, starting transfers between devices, swap_core(): return lax.ppermute(values, 'tp', [(i, i ^ 1) for i in range(4)])  26.2 us
    unnamed x213, local copies, waits for them, and re-layouts  24.6 us
    ppermute x4, waiting for transfers between devices, both(): return (values, lax.ppermute(values, 'fsdp', PAIR))  24.2 us
    ppermute x16, waiting for transfers between devices, hop(): return lax.ppermute(values, 'ctx', pairs)  23.5 us
    convert_element_type x14, other arithmetic, low(): return values.astype(BF)  12.7 us
  transfers between devices with their start and end apart: 55, of which 18 were waited for; matrix products, arithmetic and copies ran while one was open for 22% of the time, Pallas kernels for 22%

profile of v2, /device:TPU:25, one launch (start us, length us, event | category | flops | bytes accessed | tf_op | source)
XLA Modules:
  0.0 374.3 jit_solution(11326979745041853982)
XLA Ops:
  1.7 2.0 collective-permute-start.2
  3.7 7.8 %collective-permute-done.2 = bf16[256,768]{1,0:T(8,128)(2,1)S(1)} collective-permute-done((bf16[256,768]{1,0:T(8,128)(2,1)S(1)}, bf16[256,768]{1,0:T(8,128)(2,1)S(1)}, u32[]{:S(2)}, u32[]{:S(2)}) %collective-permute-start.2) | collective-permute-done | bytes 393248 | tf_op jit(solution)/shard_map/ppermute | solution.py:755
  25.0 4.2 %collective-permute-done.6 = bf16[256,768]{1,0:T(8,128)(2,1)S(1)} collective-permute-done((bf16[256,768]{1,0:T(8,128)(2,1)S(1)}, bf16[256,768]{1,0:T(8,128)(2,1)S(1)}, u32[]{:S(2)}, u32[]{:S(2)}) %collective-permute-start.6) | collective-permute-done | bytes 393248 | tf_op jit(solution)/shard_map/ppermute | solution.py:755
  30.2 1.5 collective-permute-start.7
  33.7 4.4 %collective-permute-start.4 = (bf16[512,768]{1,0:T(8,128)(2,1)}, bf16[512,768]{1,0:T(8,128)(2,1)}, u32[]{:S(2)}, u32[]{:S(2)}) collective-permute-start(bf16[512,768]{1,0:T(8,128)(2,1)} %pad_maximum_fusion.3), channel_id=1, source_target_pairs={{0,1},{1,0},{2,3},{3,2},{4,5},{5,4},{6,7},{7,6},{8,9},{9,8},{10,11... | collective-permute-start | bytes 2359304 | tf_op jit(solution)/shard_map/ppermute | solution.py:747
  38.1 3.3 collective-permute-done.7.refs_1_
  42.4 2.3 collective-permute-start.8
  52.2 5.6 %project.1 = (bf16[1024,192]{1,0:T(8,128)(2,1)S(1)}, bf16[1024,192]{1,0:T(8,128)(2,1)S(1)}, bf16[1024,192]{1,0:T(8,128)(2,1)S(1)}, bf16[1024,768]{1,0:T(8,128)(2...) custom-call(s32[6]{0:T(128)S(1)} %stack.86.sc_ref, bf16[1024,768]{1,0:T(8,128)(2,1)S(1)} %bitcast.72, ...), custom_call_target="tpu_custom_call" | custom-call | flops 1509949440 | bytes 8000000 | tf_op jit(solution)/shard_map/project/pallas_call | solution.py:36
  59.0 5.9 %project_seen.2 = (bf16[1024,192]{1,0:T(8,128)(2,1)S(1)}, bf16[1024,192]{1,0:T(8,128)(2,1)S(1)}, bf16[1024,768]{1,0:T(8,128)(2,1)S(1)}) custom-call(s32[6]{0:T(128)S(1)} %stack.86.sc_ref, bf16[256,768]{1,0:T(8,128)(2,1)S(1)} %broadcast_select_fusion.refs_0_, bf16[256,768]{1,0:T(8,128)(2,1)S(1)} %copy-done.41, ...), custom_call_target="tpu_custom_call" | custom-call | flops 1509949440 | bytes 8000000 | tf_op jit(solution)/shard_map/project_seen/pallas_call | solution.py:36
  66.1 5.3 %project_seen.3 = (bf16[1024,192]{1,0:T(8,128)(2,1)S(1)}, bf16[1024,192]{1,0:T(8,128)(2,1)S(1)}, bf16[1024,768]{1,0:T(8,128)(2,1)S(1)}) custom-call(s32[6]{0:T(128)S(1)} %stack.86.sc_ref, bf16[256,768]{1,0:T(8,128)(2,1)S(1)} %add.235.refs_0_, bf16[256,768]{1,0:T(8,128)(2,1)S(1)} %copy-done.43, bf16[512,768]{1,0:T(8,128)(2,1)} %collective-permute-done.8.refs_2_.refs_3_, ...), custom_call_target="tpu_custom_call" | custom-call | flops 1509949440 | bytes 8000000 | tf_op jit(solution)/shard_map/project_seen/pallas_call | solution.py:36
  72.5 7.9 %attn_fwd.2 = (bf16[512,192]{1,0:T(8,128)(2,1)S(1)}, f32[2,8,256]{2,1,0:T(8,128)S(1)}, bf16[512,768]{1,0:T(8,128)(2,1)S(1)}) custom-call(s32[6]{0:T(128)S(1)} %stack.86.sc_ref, bf16[1024,192]{1,0:T(8,128)(2,1)S(1)} %get-tuple-element.130.q_ref, bf16[1024,192]{1,0:T(8,128)(2,1)S(1)} %get-tuple-element.88.ko_ref, ...), custom_call_target="tpu_custom_call" | custom-call | flops 6000000000 | bytes 4000000 | tf_op jit(solution)/shard_map/attn_fwd/pallas_call | solution.py:36
  80.9 1.4 collective-permute-done.10
  83.8 9.1 %attn_fwd.3 = (bf16[512,192]{1,0:T(8,128)(2,1)S(1)}, f32[2,8,256]{2,1,0:T(8,128)S(1)}, bf16[512,768]{1,0:T(8,128)(2,1)S(1)}) custom-call(s32[6]{0:T(128)S(1)} %stack.86.sc_ref, bf16[1024,192]{1,0:T(8,128)(2,1)S(1)} %get-tuple-element.130.q_ref, bf16[1024,192]{1,0:T(8,128)(2,1)S(1)} %get-tuple-element.88.ko_ref, ...), custom_call_target="tpu_custom_call" | custom-call | flops 6000000000 | bytes 4000000 | tf_op jit(solution)/shard_map/attn_fwd/pallas_call | solution.py:36
  96.9 11.6 %collective-permute-done.14.ub_ref = bf16[384,768]{1,0:T(8,128)(2,1)S(1)} collective-permute-done((bf16[384,768]{1,0:T(8,128)(2,1)S(1)}, bf16[384,768]{1,0:T(8,128)(2,1)S(1)}, u32[]{:S(2)}, u32[]{:S(2)}) %collective-permute-start.14) | collective-permute-done | bytes 589856 | tf_op jit(solution)/shard_map/ppermute | solution.py:815
  108.4 12.6 %collective-permute-done.15.db_ref = bf16[768,384]{1,0:T(8,128)(2,1)S(1)} collective-permute-done((bf16[768,384]{1,0:T(8,128)(2,1)S(1)}, bf16[768,384]{1,0:T(8,128)(2,1)S(1)}, u32[]{:S(2)}, u32[]{:S(2)}) %collective-permute-start.15) | collective-permute-done | bytes 589856 | tf_op jit(solution)/shard_map/ppermute | solution.py:815
  121.1 3.7 mlp.2
  128.1 8.4 %collective-permute-done.16.theirs_ref = bf16[256,768]{1,0:T(8,128)(2,1)S(1)} collective-permute-done((bf16[256,768]{1,0:T(8,128)(2,1)S(1)}, bf16[256,768]{1,0:T(8,128)(2,1)S(1)}, u32[]{:S(2)}, u32[]{:S(2)}) %collective-permute-start.16) | collective-permute-done | bytes 393248 | tf_op jit(solution)/shard_map/ppermute | solution.py:751
  136.5 1.7 norm_two.3
  147.3 4.5 %mlp.3 = (bf16[512,768]{1,0:T(8,128)(2,1)S(1)}, bf16[512,768]{1,0:T(8,128)(2,1)S(1)}, bf16[512,768]{1,0:T(8,128)(2,1)S(1)}) custom-call(s32[6]{0:T(128)S(1)} %stack.86.sc_ref, bf16[256,768]{1,0:T(8,128)(2,1)} %get-tuple-element.109.a_ref.refs_2_, bf16[256,768]{1,0:T(8,128)(2,1)} %collective-permute-done.18.b_ref.refs_3_, bf16[1024,768]{1,0:T(8,128)(2,1)S(1)} %copy-done.1, ...), custom_call_target="tpu_custom_call" | custom-call | flops 1811939328 | bytes 8000000 | tf_op jit(solution)/shard_map/mlp/pallas_call | solution.py:36
  153.6 1.8 norm_two_grad.2
  155.9 1.8 convert_reduce_fusion.2
  158.8 1.7 convolution_convert_fusion.1
  160.5 5.8 %mlp_weights.1 = (f32[384,1536]{1,0:T(8,128)S(1)}, bf16[384,1536]{1,0:T(8,128)(2,1)S(1)}, f32[8,768]{1,0:T(8,128)S(1)}) custom-call(s32[6]{0:T(128)S(1)} %stack.86.sc_ref, bf16[256,768]{1,0:T(8,128)(2,1)S(1)} %copy-done.49, bf16[256,768]{1,0:T(8,128)(2,1)S(1)} %copy-done.51, bf16[256,768]{1,0:T(8,128)(2,1)} %get-tuple-element.109.a_ref.refs_2_, ...), custom_call_target="tpu_custom_call" | custom-call | flops 2415919104 | bytes 12000000 | tf_op jit(solution)/shard_map/mlp_weights/pallas_call | solution.py:36
  170.0 1.4 dynamic-slice_reduce_fusion
  175.3 2.4 convolution_convert_fusion
  180.6 14.3 %attn_bwd.2 = (bf16[512,192]{1,0:T(8,128)(2,1)S(1)}, bf16[3072,192]{1,0:T(8,128)(2,1)S(1)}, bf16[3072,192]{1,0:T(8,128)(2,1)S(1)}) custom-call(s32[6]{0:T(128)S(1)} %stack.86.sc_ref, bf16[1024,192]{1,0:T(8,128)(2,1)S(1)} %copy-done.59, bf16[512,192]{1,0:T(8,128)(2,1)S(1)} %copy-done.78, bf16[256,768]{1,0:T(8,128)(2,1)} %get-tuple-element.122.za_ref, ...), custom_call_target="tpu_custom_call" | custom-call | flops 16000000000 | bytes 10000000 | tf_op jit(solution)/shard_map/attn_bwd/pallas_call | solution.py:36
  197.8 2.2 norm_two_grad.3
  204.8 2.6 fusion.4
  208.8 3.6 collective-permute-start.51
  212.4 14.3 %attn_bwd.3 = (bf16[512,192]{1,0:T(8,128)(2,1)S(1)}, bf16[3072,192]{1,0:T(8,128)(2,1)S(1)}, bf16[3072,192]{1,0:T(8,128)(2,1)S(1)}) custom-call(s32[6]{0:T(128)S(1)} %stack.86.sc_ref, bf16[1024,192]{1,0:T(8,128)(2,1)S(1)} %copy-done.59, bf16[512,192]{1,0:T(8,128)(2,1)S(1)} %copy-done.76, bf16[256,768]{1,0:T(8,128)(2,1)S(1)} %get-tuple-element.132.za_ref, ...), custom_call_target="tpu_custom_call" | custom-call | flops 16000000000 | bytes 10000000 | tf_op jit(solution)/shard_map/attn_bwd/pallas_call | solution.py:36
  226.8 6.2 %share_seen.1 = (bf16[2048,768]{1,0:T(8,128)(2,1)S(1)}, f32[768,192]{1,0:T(8,128)S(1)}, f32[768,192]{1,0:T(8,128)S(1)}, f32[8,192]{1,0:T(8,128)S(1)}) custom-call(s32[6]{0:T(128)S(1)} %stack.86.sc_ref, bf16[3072,192]{1,0:T(8,128)(2,1)S(1)} %get-tuple-element.125.refs_0_.refs_2_, bf16[3072,192]{1,0:T(8,128)(2,1)S(1)} %get-tuple-element.135.refs_1_.refs_3_, ...), custom_call_target="tpu_custom_call" | custom-call | flops 2415919104 | bytes 8000000 | tf_op jit(solution)/shard_map/share_seen/pallas_call | solution.py:36
  233.0 1.7 copy-done.6
  234.6 5.1 %share.1 = (bf16[1024,768]{1,0:T(8,128)(2,1)S(1)}, f32[768,192]{1,0:T(8,128)S(1)}, f32[768,192]{1,0:T(8,128)S(1)}, f32[768,192]{1,0:T(8,128)S(1)}, f32[8,192]{1,0:T(8,128)S(1)}) custom-call(s32[6]{0:T(128)S(1)} %stack.86.sc_ref, bf16[512,192]{1,0:T(8,128)(2,1)S(1)} %get-tuple-element.141.refs_0_, bf16[512,192]{1,0:T(8,128)(2,1)S(1)} %get-tuple-element.142.refs_1_, ...), custom_call_target="tpu_custom_call" | custom-call | flops 1811939328 | bytes 8000000 | tf_op jit(solution)/shard_map/share/pallas_call | solution.py:36
  243.0 2.4 fusion.2
  247.1 2.5 pad_maximum_fusion
  250.5 1.5 collective-permute-start.41
  253.0 1.9 collective-permute-start.30
  254.9 1.9 add_convert_fusion.4
  259.6 1.7 bitcast_add_fusion
  261.4 2.8 collective-permute-done.41
  264.2 8.0 %collective-permute-start.52 = (bf16[96,1536]{1,0:T(8,128)(2,1)S(1)}, bf16[96,1536]{1,0:T(8,128)(2,1)S(1)}, u32[]{:S(2)}, u32[]{:S(2)}) collective-permute-start(bf16[96,1536]{1,0:T(8,128)(2,1)S(1)} %fusion.35), channel_id=1, source_target_pairs={{0,8},{4,12},{8,0},{12,4},{1,9},{5,13},{9,1},{13,5},{2,10},{6,14},... | collective-permute-start | bytes 884744 | tf_op jit(solution)/shard_map/ppermute | solution.py:755
  273.4 1.5 add_convert_fusion.2
  277.1 1.6 add_convert_fusion.1
  281.1 2.3 placed.2
  284.2 9.3 %collective-permute-done.35 = bf16[256,768]{1,0:T(8,128)(2,1)S(1)} collective-permute-done((bf16[256,768]{1,0:T(8,128)(2,1)S(1)}, bf16[256,768]{1,0:T(8,128)(2,1)S(1)}, u32[]{:S(2)}, u32[]{:S(2)}) %collective-permute-start.35) | collective-permute-done | bytes 393248 | tf_op jit(solution)/shard_map/ppermute | solution.py:751
  293.6 4.7 %collective-permute-start.46 = (f32[6,768]{1,0:T(8,128)S(1)}, f32[6,768]{1,0:T(8,128)S(1)}, u32[]{:S(2)}, u32[]{:S(2)}) collective-permute-start(f32[6,768]{1,0:T(8,128)S(1)} %stack.96), channel_id=1, source_target_pairs={{0,1},{1,0},{2,3},{3,2},{4,5},{5,4},{6,7},{7,6},{8,9},{9,8},{10,11... | collective-permute-start | bytes 55304 | tf_op jit(solution)/shard_map/ppermute | solution.py:747
  300.5 1.9 collective-permute-done.47
  303.3 1.5 collective-permute-start.48
  304.7 4.7 %collective-permute-done.43 = bf16[96,768]{1,0:T(8,128)(2,1)} collective-permute-done((bf16[96,768]{1,0:T(8,128)(2,1)S(1)}, bf16[96,768]{1,0:T(8,128)(2,1)}, u32[]{:S(2)}, u32[]{:S(2)}) %collective-permute-start.43) | collective-permute-done | bytes 147488 | tf_op jit(solution)/shard_map/ppermute | solution.py:755
  313.3 1.6 collective-permute-start.49
  314.8 2.2 maximum_select_fusion.2
  317.4 2.5 collective-permute-done.44
  319.9 4.8 %collective-permute-start.50 = (f32[2976]{0:T(1024)S(1)}, f32[2976]{0:T(1024)S(1)}, u32[]{:S(2)}, u32[]{:S(2)}) collective-permute-start(f32[2976]{0:T(1024)S(1)} %add.289), channel_id=1, source_target_pairs={{0,8},{4,12},{8,0},{12,4},{1,9},{5,13},{9,1},{13,5},{2,10},{6,14},... | collective-permute-start | bytes 35720 | tf_op jit(solution)/shard_map/ppermute | solution.py:755
  325.5 3.0 collective-permute-done.50
  328.5 8.6 %collective-permute-start.45 = (bf16[192,768]{1,0:T(8,128)(2,1)}, bf16[192,768]{1,0:T(8,128)(2,1)}, u32[]{:S(2)}, u32[]{:S(2)}) collective-permute-start(bf16[192,768]{1,0:T(8,128)(2,1)} %bitcast.24), channel_id=1, source_target_pairs={{0,4},{4,0},{8,12},{12,8},{1,5},{5,1},{9,13},{13,9},{2,6},{6,2},{1... | collective-permute-start | bytes 884744 | tf_op jit(solution)/shard_map/ppermute | solution.py:755
  339.1 2.1 fusion.23
  341.2 2.6 collective-permute-start.38
  345.2 1.4 maximum_select_fusion.1
  348.1 2.4 copy.54
  351.7 2.2 fusion.42
  355.4 1.9 maximum_select_fusion
  357.3 3.7 collective-permute-done.39.refs_1_
  361.9 6.4 %collective-permute-start.40 = (bf16[512,768]{1,0:T(8,128)(2,1)}, bf16[512,768]{1,0:T(8,128)(2,1)S(1)}, u32[]{:S(2)}, u32[]{:S(2)}) collective-permute-start(bf16[512,768]{1,0:T(8,128)(2,1)} %pad_maximum_fusion.6), channel_id=1, source_target_pairs={{0,1},{1,0},{2,3},{3,2},{4,5},{5,4},{6,7},{7,6},{8,9},{9,8},{10,11... | collective-permute-start | bytes 2359304 | tf_op jit(solution)/shard_map/ppermute | solution.py:747
  371.2 2.8 placed.3
  (400 shorter events, 104.9 us)
Async XLA Ops:
  1.7 9.8 %collective-permute-start.2 = (bf16[256,768]{1,0:T(8,128)(2,1)S(1)}, bf16[256,768]{1,0:T(8,128)(2,1)S(1)}, u32[]{:S(2)}, u32[]{:S(2)}) collective-permute-start(bf16[256,768]{1,0:T(8,128)(2,1)S(1)} %dynamic-slice_bitcast_fusion.1), channel_id=1, source_target_pairs={{8,0},{12,4},{9,1},{13,5},{10,2},{14,6},{11,3},{15,7},{24,16},{28,... | collective-permute-start | bytes 1179656 | tf_op jit(solution)/shard_map/ppermute | solution.py:755
  11.5 17.6 %collective-permute-start.6 = (bf16[256,768]{1,0:T(8,128)(2,1)S(1)}, bf16[256,768]{1,0:T(8,128)(2,1)S(1)}, u32[]{:S(2)}, u32[]{:S(2)}) collective-permute-start(bf16[256,768]{1,0:T(8,128)(2,1)S(1)} %dynamic-slice_bitcast_fusion.1), channel_id=1, source_target_pairs={{8,12},{9,13},{10,14},{11,15},{24,28},{25,29},{26,30},{27,31}} | collective-permute-start | bytes 1179656 | tf_op jit(solution)/shard_map/ppermute | solution.py:755
  12.8 16.3 %collective-permute-start.5 = (bf16[256,768]{1,0:T(8,128)(2,1)S(1)}, bf16[256,768]{1,0:T(8,128)(2,1)}, u32[]{:S(2)}, u32[]{:S(2)}) collective-permute-start(bf16[256,768]{1,0:T(8,128)(2,1)S(1)} %dynamic-slice_bitcast_fusion.1), channel_id=1, source_target_pairs={{8,4},{9,5},{10,6},{11,7},{24,20},{25,21},{26,22},{27,23}} | collective-permute-start | bytes 1179656 | tf_op jit(solution)/shard_map/ppermute | solution.py:755
  19.7 26.7 %collective-permute-start = (bf16[32,384]{1,0:T(8,128)(2,1)S(1)}, bf16[32,384]{1,0:T(8,128)(2,1)S(1)}, u32[]{:S(2)}, u32[]{:S(2)}) collective-permute-start(bf16[32,384]{1,0:T(8,128)(2,1)S(1)} %packed.1.a_ref), channel_id=1, source_target_pairs={{0,16},{16,0},{1,17},{17,1},{2,18},{18,2},{3,19},{19,3},{4,20},{20... | collective-permute-start | bytes 73736 | tf_op jit(solution)/shard_map/ppermute | solution.py:834
  22.3 24.8 %collective-permute-start.1 = (bf16[384,576]{1,0:T(8,128)(2,1)S(1)}, bf16[384,576]{1,0:T(8,128)(2,1)S(1)}, u32[]{:S(2)}, u32[]{:S(2)}) collective-permute-start(bf16[384,576]{1,0:T(8,128)(2,1)S(1)} %copy.48.refs_3_.refs_5_.refs_6_.refs_7_), channel_id=1, source_target_pairs={{0,16},{16,0},{1,17},{17,1},{2,18},{18,2},{3,19},{19,3},{4,20},{20... | collective-permute-start | bytes 1327112 | tf_op jit(solution)/shard_map/ppermute | solution.py:815
  23.7 9.0 %collective-permute-start.3 = (bf16[256,768]{1,0:T(8,128)(2,1)S(1)}, bf16[256,768]{1,0:T(8,128)(2,1)S(1)}, u32[]{:S(2)}, u32[]{:S(2)}) collective-permute-start(bf16[256,768]{1,0:T(8,128)(2,1)S(1)} %broadcast_select_fusion.refs_0_), channel_id=1, source_target_pairs={{0,2},{1,3},{2,0},{3,1},{4,6},{5,7},{6,4},{7,5},{8,10},{9,11},{10,... | collective-permute-start | bytes 1179656 | tf_op jit(solution)/shard_map/ppermute | solution.py:751
  30.2 11.2 %collective-permute-start.7 = (bf16[256,768]{1,0:T(8,128)(2,1)S(1)}, bf16[256,768]{1,0:T(8,128)(2,1)S(1)}, u32[]{:S(2)}, u32[]{:S(2)}) collective-permute-start(bf16[256,768]{1,0:T(8,128)(2,1)S(1)} %add.235.refs_0_), channel_id=1, source_target_pairs={{0,2},{1,3},{2,0},{3,1},{4,6},{5,7},{6,4},{7,5},{8,10},{9,11},{10,... | collective-permute-start | bytes 1179656 | tf_op jit(solution)/shard_map/ppermute | solution.py:751
  33.7 25.3 %collective-permute-start.4 = (bf16[512,768]{1,0:T(8,128)(2,1)}, bf16[512,768]{1,0:T(8,128)(2,1)}, u32[]{:S(2)}, u32[]{:S(2)}) collective-permute-start(bf16[512,768]{1,0:T(8,128)(2,1)} %pad_maximum_fusion.3), channel_id=1, source_target_pairs={{0,1},{1,0},{2,3},{3,2},{4,5},{5,4},{6,7},{7,6},{8,9},{9,8},{10,11... | collective-permute-start | bytes 2359304 | tf_op jit(solution)/shard_map/ppermute | solution.py:747
  42.4 23.6 %collective-permute-start.8 = (bf16[512,768]{1,0:T(8,128)(2,1)}, bf16[512,768]{1,0:T(8,128)(2,1)}, u32[]{:S(2)}, u32[]{:S(2)}) collective-permute-start(bf16[512,768]{1,0:T(8,128)(2,1)} %pad_maximum_fusion.4), channel_id=1, source_target_pairs={{0,1},{1,0},{2,3},{3,2},{4,5},{5,4},{6,7},{7,6},{8,9},{9,8},{10,11... | collective-permute-start | bytes 2359304 | tf_op jit(solution)/shard_map/ppermute | solution.py:747
  47.1 25.5 %collective-permute-start.9 = (bf16[192,384]{1,0:T(8,128)(2,1)S(1)}, bf16[192,384]{1,0:T(8,128)(2,1)S(1)}, u32[]{:S(2)}, u32[]{:S(2)}) collective-permute-start(bf16[192,384]{1,0:T(8,128)(2,1)S(1)} %copy-done.52), channel_id=1, source_target_pairs={{0,16},{16,0},{1,17},{17,1},{2,18},{18,2},{3,19},{19,3},{4,20},{20... | collective-permute-start | bytes 442376 | tf_op jit(solution)/shard_map/ppermute | solution.py:815
  58.9 24.8 %copy-start.58 = (bf16[1024,192]{1,0:T(8,128)(2,1)}, bf16[1024,192]{1,0:T(8,128)(2,1)S(1)}, u32[]{:S(2)}) copy-start(bf16[1024,192]{1,0:T(8,128)(2,1)S(1)} %get-tuple-element.130.q_ref) | copy-start | bytes 1179652
  59.0 24.8 %copy-start.60 = (bf16[1024,192]{1,0:T(8,128)(2,1)}, bf16[1024,192]{1,0:T(8,128)(2,1)S(1)}, u32[]{:S(2)}) copy-start(bf16[1024,192]{1,0:T(8,128)(2,1)S(1)} %get-tuple-element.88.ko_ref) | copy-start | bytes 1179652
  59.0 24.8 %copy-start.62 = (bf16[1024,192]{1,0:T(8,128)(2,1)}, bf16[1024,192]{1,0:T(8,128)(2,1)S(1)}, u32[]{:S(2)}) copy-start(bf16[1024,192]{1,0:T(8,128)(2,1)S(1)} %get-tuple-element.89.vo_ref) | copy-start | bytes 1179652
  59.0 62.1 %copy-start = (bf16[1024,768]{1,0:T(8,128)(2,1)}, bf16[1024,768]{1,0:T(8,128)(2,1)S(1)}, u32[]{:S(2)}) copy-start(bf16[1024,768]{1,0:T(8,128)(2,1)S(1)} %get-tuple-element.102.dy_ref.refs_4_) | copy-start | bytes 4718596
  66.1 17.7 %copy-start.68 = (bf16[1024,192]{1,0:T(8,128)(2,1)}, bf16[1024,192]{1,0:T(8,128)(2,1)S(1)}, u32[]{:S(2)}) copy-start(bf16[1024,192]{1,0:T(8,128)(2,1)S(1)} %get-tuple-element.91.vm_ref) | copy-start | bytes 1179652
  80.5 1.8 collective-permute-start.10
  82.5 12.6 %collective-permute-start.11 = (bf16[256,768]{1,0:T(8,128)(2,1)S(1)}, bf16[256,768]{1,0:T(8,128)(2,1)S(1)}, u32[]{:S(2)}, u32[]{:S(2)}) collective-permute-start(bf16[256,768]{1,0:T(8,128)(2,1)S(1)} %add_convert_fusion.11.mine_ref), channel_id=1, source_target_pairs={{0,2},{1,3},{2,0},{3,1},{4,6},{5,7},{6,4},{7,5},{8,10},{9,11},{10,... | collective-permute-start | bytes 1179656 | tf_op jit(solution)/shard_map/ppermute | solution.py:751
  93.0 3.7 collective-permute-start.12
  93.6 14.8 %collective-permute-start.14 = (bf16[384,768]{1,0:T(8,128)(2,1)S(1)}, bf16[384,768]{1,0:T(8,128)(2,1)S(1)}, u32[]{:S(2)}, u32[]{:S(2)}) collective-permute-start(bf16[384,768]{1,0:T(8,128)(2,1)S(1)} %copy-done.31), channel_id=1, source_target_pairs={{0,16},{16,0},{1,17},{17,1},{2,18},{18,2},{3,19},{19,3},{4,20},{20... | collective-permute-start | bytes 1769480 | tf_op jit(solution)/shard_map/ppermute | solution.py:815
  93.9 27.2 %collective-permute-start.15 = (bf16[768,384]{1,0:T(8,128)(2,1)S(1)}, bf16[768,384]{1,0:T(8,128)(2,1)S(1)}, u32[]{:S(2)}, u32[]{:S(2)}) collective-permute-start(bf16[768,384]{1,0:T(8,128)(2,1)S(1)} %copy-done.27), channel_id=1, source_target_pairs={{0,16},{16,0},{1,17},{17,1},{2,18},{18,2},{3,19},{19,3},{4,20},{20... | collective-permute-start | bytes 1769480 | tf_op jit(solution)/shard_map/ppermute | solution.py:815
  96.0 28.7 %copy-start.48 = (bf16[256,768]{1,0:T(8,128)(2,1)}, bf16[256,768]{1,0:T(8,128)(2,1)S(1)}, u32[]{:S(2)}) copy-start(bf16[256,768]{1,0:T(8,128)(2,1)S(1)} %get-tuple-element.101.a_ref.refs_0_) | copy-start | bytes 1179652
  96.0 25.0 %collective-permute-start.13 = (bf16[256,768]{1,0:T(8,128)(2,1)S(1)}, bf16[256,768]{1,0:T(8,128)(2,1)S(1)}, u32[]{:S(2)}, u32[]{:S(2)}) collective-permute-start(bf16[256,768]{1,0:T(8,128)(2,1)S(1)} %get-tuple-element.101.a_ref.refs_0_), channel_id=1, source_target_pairs={{0,1},{1,0},{2,3},{3,2},{4,5},{5,4},{6,7},{7,6},{8,9},{9,8},{10,11... | collective-permute-start | bytes 1179656 | tf_op jit(solution)/shard_map/ppermute | solution.py:747
  124.9 2.4 collective-permute-start.17
  125.9 10.6 %collective-permute-start.16 = (bf16[256,768]{1,0:T(8,128)(2,1)S(1)}, bf16[256,768]{1,0:T(8,128)(2,1)S(1)}, u32[]{:S(2)}, u32[]{:S(2)}) collective-permute-start(bf16[256,768]{1,0:T(8,128)(2,1)S(1)} %add_convert_fusion.10.mine_ref), channel_id=1, source_target_pairs={{0,2},{1,3},{2,0},{3,1},{4,6},{5,7},{6,4},{7,5},{8,10},{9,11},{10,... | collective-permute-start | bytes 1179656 | tf_op jit(solution)/shard_map/ppermute | solution.py:751
  139.0 2.6 collective-permute-start.18
  140.4 12.7 %collective-permute-start.21 = (bf16[256,768]{1,0:T(8,128)(2,1)}, bf16[256,768]{1,0:T(8,128)(2,1)S(1)}, u32[]{:S(2)}, u32[]{:S(2)}) collective-permute-start(bf16[256,768]{1,0:T(8,128)(2,1)} %add_convert_fusion.9.mine_ref), channel_id=1, source_target_pairs={{0,2},{1,3},{2,0},{3,1},{4,6},{5,7},{6,4},{7,5},{8,10},{9,11},{10,... | collective-permute-start | bytes 1179656 | tf_op jit(solution)/shard_map/ppermute | solution.py:751
  151.9 5.7 %collective-permute-start.19 = (bf16[256,768]{1,0:T(8,128)(2,1)S(1)}, bf16[256,768]{1,0:T(8,128)(2,1)S(1)}, u32[]{:S(2)}, u32[]{:S(2)}) collective-permute-start(bf16[256,768]{1,0:T(8,128)(2,1)S(1)} %slice.203), channel_id=1, source_target_pairs={{0,1},{1,0},{2,3},{3,2},{4,5},{5,4},{6,7},{7,6},{8,9},{9,8},{10,11... | collective-permute-start | bytes 1179656 | tf_op jit(solution)/shard_map/ppermute | solution.py:747
  155.5 23.7 %collective-permute-start.27 = (bf16[256,768]{1,0:T(8,128)(2,1)}, bf16[256,768]{1,0:T(8,128)(2,1)}, u32[]{:S(2)}, u32[]{:S(2)}) collective-permute-start(bf16[256,768]{1,0:T(8,128)(2,1)} %get-tuple-element.122.za_ref), channel_id=1, source_target_pairs={{0,1},{1,0},{2,3},{3,2},{4,5},{5,4},{6,7},{7,6},{8,9},{9,8},{10,11... | collective-permute-start | bytes 1179656 | tf_op jit(solution)/shard_map/ppermute | solution.py:747
  158.6 39.3 %collective-permute-start.22 = (bf16[256,768]{1,0:T(8,128)(2,1)}, bf16[256,768]{1,0:T(8,128)(2,1)}, u32[]{:S(2)}, u32[]{:S(2)}) collective-permute-start(bf16[256,768]{1,0:T(8,128)(2,1)} %add_convert_fusion.8.mine_ref), channel_id=1, source_target_pairs={{0,2},{1,3},{2,0},{3,1},{4,6},{5,7},{6,4},{7,5},{8,10},{9,11},{10,... | collective-permute-start | bytes 1179656 | tf_op jit(solution)/shard_map/ppermute | solution.py:751
  177.8 23.7 %collective-permute-start.24 = (bf16[256,768]{1,0:T(8,128)(2,1)S(1)}, bf16[256,768]{1,0:T(8,128)(2,1)S(1)}, u32[]{:S(2)}, u32[]{:S(2)}) collective-permute-start(bf16[256,768]{1,0:T(8,128)(2,1)S(1)} %slice.253), channel_id=1, source_target_pairs={{0,1},{1,0},{2,3},{3,2},{4,5},{5,4},{6,7},{7,6},{8,9},{9,8},{10,11... | collective-permute-start | bytes 1179656 | tf_op jit(solution)/shard_map/ppermute | solution.py:747
  178.5 25.2 %collective-permute-start.20 = (bf16[256,768]{1,0:T(8,128)(2,1)S(1)}, bf16[256,768]{1,0:T(8,128)(2,1)S(1)}, u32[]{:S(2)}, u32[]{:S(2)}) collective-permute-start(bf16[256,768]{1,0:T(8,128)(2,1)S(1)} %slice.251), channel_id=1, source_target_pairs={{0,1},{1,0},{2,3},{3,2},{4,5},{5,4},{6,7},{7,6},{8,9},{9,8},{10,11... | collective-permute-start | bytes 1179656 | tf_op jit(solution)/shard_map/ppermute | solution.py:747
  179.0 28.4 %collective-permute-start.28 = (bf16[384,1536]{1,0:T(8,128)(2,1)S(1)}, bf16[384,1536]{1,0:T(8,128)(2,1)S(1)}, u32[]{:S(2)}, u32[]{:S(2)}) collective-permute-start(bf16[384,1536]{1,0:T(8,128)(2,1)S(1)} %copy-done.45), channel_id=1, source_target_pairs={{0,16},{16,0},{1,17},{17,1},{2,18},{18,2},{3,19},{19,3},{4,20},{20... | collective-permute-start | bytes 3538952 | tf_op jit(solution)/shard_map/ppermute | solution.py:885
  200.1 4.7 %collective-permute-start.29 = (bf16[256,768]{1,0:T(8,128)(2,1)S(1)}, bf16[256,768]{1,0:T(8,128)(2,1)S(1)}, u32[]{:S(2)}, u32[]{:S(2)}) collective-permute-start(bf16[256,768]{1,0:T(8,128)(2,1)S(1)} %get-tuple-element.132.za_ref), channel_id=1, source_target_pairs={{0,1},{1,0},{2,3},{3,2},{4,5},{5,4},{6,7},{7,6},{8,9},{9,8},{10,11... | collective-permute-start | bytes 1179656 | tf_op jit(solution)/shard_map/ppermute | solution.py:747
  202.4 52.4 %collective-permute-start.25 = (bf16[256,768]{1,0:T(8,128)(2,1)}, bf16[256,768]{1,0:T(8,128)(2,1)}, u32[]{:S(2)}, u32[]{:S(2)}) collective-permute-start(bf16[256,768]{1,0:T(8,128)(2,1)} %add_convert_fusion.5), channel_id=1, source_target_pairs={{0,2},{1,3},{2,0},{3,1},{4,6},{5,7},{6,4},{7,5},{8,10},{9,11},{10,... | collective-permute-start | bytes 1179656 | tf_op jit(solution)/shard_map/ppermute | solution.py:751
  204.6 50.3 %collective-permute-start.23 = (bf16[256,768]{1,0:T(8,128)(2,1)}, bf16[256,768]{1,0:T(8,128)(2,1)}, u32[]{:S(2)}, u32[]{:S(2)}) collective-permute-start(bf16[256,768]{1,0:T(8,128)(2,1)} %add_convert_fusion.7), channel_id=1, source_target_pairs={{0,2},{1,3},{2,0},{3,1},{4,6},{5,7},{6,4},{7,5},{8,10},{9,11},{10,... | collective-permute-start | bytes 1179656 | tf_op jit(solution)/shard_map/ppermute | solution.py:751
  208.8 50.8 %collective-permute-start.51 = (bf16[192,1536]{1,0:T(8,128)(2,1)}, bf16[192,1536]{1,0:T(8,128)(2,1)}, u32[]{:S(2)}, u32[]{:S(2)}) collective-permute-start(bf16[192,1536]{1,0:T(8,128)(2,1)} %fusion.29), channel_id=1, source_target_pairs={{0,4},{4,0},{8,12},{12,8},{1,5},{5,1},{9,13},{13,9},{2,6},{6,2},{1... | collective-permute-start | bytes 1769480 | tf_op jit(solution)/shard_map/ppermute | solution.py:755
  250.5 13.6 %collective-permute-start.41 = (bf16[384,768]{1,0:T(8,128)(2,1)}, bf16[384,768]{1,0:T(8,128)(2,1)}, u32[]{:S(2)}, u32[]{:S(2)}) collective-permute-start(bf16[384,768]{1,0:T(8,128)(2,1)} %slice.303), channel_id=1, source_target_pairs={{0,16},{16,0},{1,17},{17,1},{2,18},{18,2},{3,19},{19,3},{4,20},{20... | collective-permute-start | bytes 1769480 | tf_op jit(solution)/shard_map/ppermute | solution.py:885
  253.0 20.4 %collective-permute-start.30 = (bf16[512,768]{1,0:T(8,128)(2,1)}, bf16[512,768]{1,0:T(8,128)(2,1)}, u32[]{:S(2)}, u32[]{:S(2)}) collective-permute-start(bf16[512,768]{1,0:T(8,128)(2,1)} %slice.210), channel_id=1, source_target_pairs={{0,1},{1,0},{2,3},{3,2},{4,5},{5,4},{6,7},{7,6},{8,9},{9,8},{10,11... | collective-permute-start | bytes 2359304 | tf_op jit(solution)/shard_map/ppermute | solution.py:747
  257.7 22.1 %collective-permute-start.26 = (bf16[512,768]{1,0:T(8,128)(2,1)}, bf16[512,768]{1,0:T(8,128)(2,1)S(1)}, u32[]{:S(2)}, u32[]{:S(2)}) collective-permute-start(bf16[512,768]{1,0:T(8,128)(2,1)} %pad_maximum_fusion.5), channel_id=1, source_target_pairs={{0,1},{1,0},{2,3},{3,2},{4,5},{5,4},{6,7},{7,6},{8,9},{9,8},{10,11... | collective-permute-start | bytes 2359304 | tf_op jit(solution)/shard_map/ppermute | solution.py:747
  259.0 16.8 %collective-permute-start.32 = (bf16[512,768]{1,0:T(8,128)(2,1)}, bf16[512,768]{1,0:T(8,128)(2,1)}, u32[]{:S(2)}, u32[]{:S(2)}) collective-permute-start(bf16[512,768]{1,0:T(8,128)(2,1)} %get-tuple-element.215), channel_id=1, source_target_pairs={{0,1},{1,0},{2,3},{3,2},{4,5},{5,4},{6,7},{7,6},{8,9},{9,8},{10,11... | collective-permute-start | bytes 2359304 | tf_op jit(solution)/shard_map/ppermute | solution.py:747
  259.5 17.5 %collective-permute-start.34 = (bf16[512,768]{1,0:T(8,128)(2,1)}, bf16[512,768]{1,0:T(8,128)(2,1)S(1)}, u32[]{:S(2)}, u32[]{:S(2)}) collective-permute-start(bf16[512,768]{1,0:T(8,128)(2,1)} %get-tuple-element.216), channel_id=1, source_target_pairs={{0,1},{1,0},{2,3},{3,2},{4,5},{5,4},{6,7},{7,6},{8,9},{9,8},{10,11... | collective-permute-start | bytes 2359304 | tf_op jit(solution)/shard_map/ppermute | solution.py:747
  264.2 19.2 %collective-permute-start.52 = (bf16[96,1536]{1,0:T(8,128)(2,1)S(1)}, bf16[96,1536]{1,0:T(8,128)(2,1)S(1)}, u32[]{:S(2)}, u32[]{:S(2)}) collective-permute-start(bf16[96,1536]{1,0:T(8,128)(2,1)S(1)} %fusion.35), channel_id=1, source_target_pairs={{0,8},{4,12},{8,0},{12,4},{1,9},{5,13},{9,1},{13,5},{2,10},{6,14},... | collective-permute-start | bytes 884744 | tf_op jit(solution)/shard_map/ppermute | solution.py:755
  273.3 24.9 %collective-permute-start.42 = (bf16[192,768]{1,0:T(8,128)(2,1)S(1)}, bf16[192,768]{1,0:T(8,128)(2,1)S(1)}, u32[]{:S(2)}, u32[]{:S(2)}) collective-permute-start(bf16[192,768]{1,0:T(8,128)(2,1)S(1)} %fusion.34), channel_id=1, source_target_pairs={{0,4},{4,0},{8,12},{12,8},{1,5},{5,1},{9,13},{13,9},{2,6},{6,2},{1... | collective-permute-start | bytes 884744 | tf_op jit(solution)/shard_map/ppermute | solution.py:755
  275.8 74.7 %collective-permute-start.31 = (bf16[256,768]{1,0:T(8,128)(2,1)}, bf16[256,768]{1,0:T(8,128)(2,1)}, u32[]{:S(2)}, u32[]{:S(2)}) collective-permute-start(bf16[256,768]{1,0:T(8,128)(2,1)} %dynamic-slice_bitcast_fusion), channel_id=1, source_target_pairs={{0,2},{1,3},{2,0},{3,1},{4,6},{5,7},{6,4},{7,5},{8,10},{9,11},{10,... | collective-permute-start | bytes 1179656 | tf_op jit(solution)/shard_map/ppermute | solution.py:751
  279.5 13.9 %collective-permute-start.35 = (bf16[256,768]{1,0:T(8,128)(2,1)S(1)}, bf16[256,768]{1,0:T(8,128)(2,1)S(1)}, u32[]{:S(2)}, u32[]{:S(2)}) collective-permute-start(bf16[256,768]{1,0:T(8,128)(2,1)S(1)} %slice.257), channel_id=1, source_target_pairs={{0,2},{1,3},{2,0},{3,1},{4,6},{5,7},{6,4},{7,5},{8,10},{9,11},{10,... | collective-permute-start | bytes 1179656 | tf_op jit(solution)/shard_map/ppermute | solution.py:751
  279.8 59.3 %collective-permute-start.33 = (bf16[256,768]{1,0:T(8,128)(2,1)}, bf16[256,768]{1,0:T(8,128)(2,1)}, u32[]{:S(2)}, u32[]{:S(2)}) collective-permute-start(bf16[256,768]{1,0:T(8,128)(2,1)} %slice.255), channel_id=1, source_target_pairs={{0,2},{1,3},{2,0},{3,1},{4,6},{5,7},{6,4},{7,5},{8,10},{9,11},{10,... | collective-permute-start | bytes 1179656 | tf_op jit(solution)/shard_map/ppermute | solution.py:751
  284.2 18.3 %copy-start.103 = (f32[384]{0:T(512)S(1)}, f32[384]{0:T(512)}, u32[]{:S(2)}) copy-start(f32[384]{0:T(512)} %reshape.465) | copy-start | bytes 4612
  284.2 29.1 %collective-permute-start.53 = (bf16[96,1536]{1,0:T(8,128)(2,1)}, bf16[96,1536]{1,0:T(8,128)(2,1)}, u32[]{:S(2)}, u32[]{:S(2)}) collective-permute-start(bf16[96,1536]{1,0:T(8,128)(2,1)} %fusion.30), channel_id=1, source_target_pairs={{0,8},{4,12},{8,0},{12,4},{1,9},{5,13},{9,1},{13,5},{2,10},{6,14},... | collective-permute-start | bytes 884744 | tf_op jit(solution)/shard_map/ppermute | solution.py:755
  293.6 23.5 %copy-start.87 = (bf16[256,768]{1,0:T(8,128)(2,1)}, bf16[256,768]{1,0:T(8,128)(2,1)S(1)}, u32[]{:S(2)}) copy-start(bf16[256,768]{1,0:T(8,128)(2,1)S(1)} %add_convert_fusion.3) | copy-start | bytes 1179652
  293.6 5.6 %collective-permute-start.46 = (f32[6,768]{1,0:T(8,128)S(1)}, f32[6,768]{1,0:T(8,128)S(1)}, u32[]{:S(2)}, u32[]{:S(2)}) collective-permute-start(f32[6,768]{1,0:T(8,128)S(1)} %stack.96), channel_id=1, source_target_pairs={{0,1},{1,0},{2,3},{3,2},{4,5},{5,4},{6,7},{7,6},{8,9},{9,8},{10,11... | collective-permute-start | bytes 55304 | tf_op jit(solution)/shard_map/ppermute | solution.py:747
  298.3 40.7 %copy-start.85 = (bf16[512,768]{1,0:T(8,128)(2,1)S(1)}, bf16[512,768]{1,0:T(8,128)(2,1)}, u32[]{:S(2)}) copy-start(bf16[512,768]{1,0:T(8,128)(2,1)} %copy-done.84) | copy-start | bytes 2359300
  299.1 3.3 collective-permute-start.47
  300.5 9.0 %collective-permute-start.43 = (bf16[96,768]{1,0:T(8,128)(2,1)S(1)}, bf16[96,768]{1,0:T(8,128)(2,1)}, u32[]{:S(2)}, u32[]{:S(2)}) collective-permute-start(bf16[96,768]{1,0:T(8,128)(2,1)S(1)} %fusion.37), channel_id=1, source_target_pairs={{0,8},{4,12},{8,0},{12,4},{1,9},{5,13},{9,1},{13,5},{2,10},{6,14},... | collective-permute-start | bytes 442376 | tf_op jit(solution)/shard_map/ppermute | solution.py:755
  303.3 8.0 %collective-permute-start.48 = (f32[2976]{0:T(1024)S(1)}, f32[2976]{0:T(1024)}, u32[]{:S(2)}, u32[]{:S(2)}) collective-permute-start(f32[2976]{0:T(1024)S(1)} %concatenate.67), channel_id=1, source_target_pairs={{0,16},{16,0},{1,17},{17,1},{2,18},{18,2},{3,19},{19,3},{4,20},{20... | collective-permute-start | bytes 35720 | tf_op jit(solution)/shard_map/ppermute | solution.py:963
  310.4 9.5 %collective-permute-start.44 = (bf16[96,768]{1,0:T(8,128)(2,1)S(1)}, bf16[96,768]{1,0:T(8,128)(2,1)S(1)}, u32[]{:S(2)}, u32[]{:S(2)}) collective-permute-start(bf16[96,768]{1,0:T(8,128)(2,1)S(1)} %fusion.36), channel_id=1, source_target_pairs={{0,8},{4,12},{8,0},{12,4},{1,9},{5,13},{9,1},{13,5},{2,10},{6,14},... | collective-permute-start | bytes 442376 | tf_op jit(solution)/shard_map/ppermute | solution.py:755
  311.3 27.8 %collective-permute-start.36 = (bf16[256,768]{1,0:T(8,128)(2,1)S(1)}, bf16[256,768]{1,0:T(8,128)(2,1)S(1)}, u32[]{:S(2)}, u32[]{:S(2)}) collective-permute-start(bf16[256,768]{1,0:T(8,128)(2,1)S(1)} %add_convert_fusion.3), channel_id=1, source_target_pairs={{0,4},{4,12},{1,5},{5,13},{2,6},{6,14},{3,7},{7,15},{16,20},{20,28... | collective-permute-start | bytes 1179656 | tf_op jit(solution)/shard_map/ppermute | solution.py:755
  313.3 3.8 %collective-permute-start.49 = (f32[2976]{0:T(1024)S(1)}, f32[2976]{0:T(1024)S(1)}, u32[]{:S(2)}, u32[]{:S(2)}) collective-permute-start(f32[2976]{0:T(1024)S(1)} %add.288), channel_id=1, source_target_pairs={{0,4},{4,0},{8,12},{12,8},{1,5},{5,1},{9,13},{13,9},{2,6},{6,2},{1... | collective-permute-start | bytes 35720 | tf_op jit(solution)/shard_map/ppermute | solution.py:755
  317.1 38.4 %collective-permute-start.54 = (bf16[192,1536]{1,0:T(8,128)(2,1)}, bf16[192,1536]{1,0:T(8,128)(2,1)}, u32[]{:S(2)}, u32[]{:S(2)}) collective-permute-start(bf16[192,1536]{1,0:T(8,128)(2,1)} %bitcast.40), channel_id=1, source_target_pairs={{0,4},{4,0},{8,12},{12,8},{1,5},{5,1},{9,13},{13,9},{2,6},{6,2},{1... | collective-permute-start | bytes 1769480 | tf_op jit(solution)/shard_map/ppermute | solution.py:755
  319.9 8.6 %collective-permute-start.50 = (f32[2976]{0:T(1024)S(1)}, f32[2976]{0:T(1024)S(1)}, u32[]{:S(2)}, u32[]{:S(2)}) collective-permute-start(f32[2976]{0:T(1024)S(1)} %add.289), channel_id=1, source_target_pairs={{0,8},{4,12},{8,0},{12,4},{1,9},{5,13},{9,1},{13,5},{2,10},{6,14},... | collective-permute-start | bytes 35720 | tf_op jit(solution)/shard_map/ppermute | solution.py:755
  328.5 16.7 %collective-permute-start.45 = (bf16[192,768]{1,0:T(8,128)(2,1)}, bf16[192,768]{1,0:T(8,128)(2,1)}, u32[]{:S(2)}, u32[]{:S(2)}) collective-permute-start(bf16[192,768]{1,0:T(8,128)(2,1)} %bitcast.24), channel_id=1, source_target_pairs={{0,4},{4,0},{8,12},{12,8},{1,5},{5,1},{9,13},{13,9},{2,6},{6,2},{1... | collective-permute-start | bytes 884744 | tf_op jit(solution)/shard_map/ppermute | solution.py:755
  341.2 10.5 %collective-permute-start.38 = (bf16[256,768]{1,0:T(8,128)(2,1)}, bf16[256,768]{1,0:T(8,128)(2,1)}, u32[]{:S(2)}, u32[]{:S(2)}) collective-permute-start(bf16[256,768]{1,0:T(8,128)(2,1)} %fusion.23), channel_id=1, source_target_pairs={{12,8},{13,9},{14,10},{15,11},{28,24},{29,25},{30,26},{31,27}} | collective-permute-start | bytes 1179656 | tf_op jit(solution)/shard_map/ppermute | solution.py:755
  343.8 7.8 %collective-permute-start.37 = (bf16[256,768]{1,0:T(8,128)(2,1)}, bf16[256,768]{1,0:T(8,128)(2,1)}, u32[]{:S(2)}, u32[]{:S(2)}) collective-permute-start(bf16[256,768]{1,0:T(8,128)(2,1)} %fusion.23), channel_id=1, source_target_pairs={{4,8},{5,9},{6,10},{7,11},{20,24},{21,25},{22,26},{23,27}} | collective-permute-start | bytes 1179656 | tf_op jit(solution)/shard_map/ppermute | solution.py:755
  354.3 6.7 %collective-permute-start.39 = (bf16[256,768]{1,0:T(8,128)(2,1)S(1)}, bf16[256,768]{1,0:T(8,128)(2,1)S(1)}, u32[]{:S(2)}, u32[]{:S(2)}) collective-permute-start(bf16[256,768]{1,0:T(8,128)(2,1)S(1)} %fusion.20.refs_0_), channel_id=1, source_target_pairs={{0,2},{1,3},{2,0},{3,1},{4,6},{5,7},{6,4},{7,5},{8,10},{9,11},{10,... | collective-permute-start | bytes 1179656 | tf_op jit(solution)/shard_map/ppermute | solution.py:751
  361.9 9.3 %collective-permute-start.40 = (bf16[512,768]{1,0:T(8,128)(2,1)}, bf16[512,768]{1,0:T(8,128)(2,1)S(1)}, u32[]{:S(2)}, u32[]{:S(2)}) collective-permute-start(bf16[512,768]{1,0:T(8,128)(2,1)} %pad_maximum_fusion.6), channel_id=1, source_target_pairs={{0,1},{1,0},{2,3},{3,2},{4,5},{5,4},{6,7},{7,6},{8,9},{9,8},{10,11... | collective-permute-start | bytes 2359304 | tf_op jit(solution)/shard_map/ppermute | solution.py:747
  (95 other events, 459.1 us)
